TPU v7x, 32 devices: a whole 2x2x4 slice. The times are simulated.
32 devices in a mesh: orb: 8 (over y, x, core), grid: 4 (over z).
Axes of the slice: x: 2, y: 2, z: 4, core: 2. Of those that a mesh axis runs over, the one named last changes fastest.
Arguments:
- ground_orbitals: float32 [32, 81000], P('orb'), may hold values from -6 to 6
- occupation_signs: int32 [32], P('orb'), may hold values from -1 to 1, as said below
- response_orbitals: float32 [32, 81000], P(('orb', 'grid')), may hold values from -1.5 to 1.5
- window_offsets: int32 [32, 2], P(('orb', 'grid')), may hold values from 0 to 3
- ground_density: float32 [81000], replicated, may hold values from 0.5 to 4
Outputs:
- response_action: float32 [32, 81000], P(('orb', 'grid'))
Inputs may be any that keep to these rules, and one draw needn't show every extreme that they name: `occupation_signs`: every entry is -1 or +1.
All inputs are finite; a program needn't handle non-finite values.
Results may differ from a plain program's by a relative error of at most 0.0003.
Values sent between devices are 32-bit elements; how exact they have to be, the bound alone decides.
No kernel may reach another device: no remote copies, remote signals or barrier semaphores. Data moves between devices by JAX's collectives and lax.ppermute only.
A program may use at most 128 MiB of HBM per device.

v0:
```python
import functools
import math

import numpy as np

import jax
import jax.numpy as jnp
from jax import lax
from jax.experimental import pallas as pl
from jax.experimental.pallas import tpu as pltpu
from jax.sharding import PartitionSpec as P

NX = 30
NY = 45
NZ = 60
SPACING = 0.5
SCREEN = 0.5
XC_COEF = 0.3282
HYBRID = 0.25

F32 = jnp.float32
BF16 = jnp.bfloat16
LANES = 128
POINTS = NX * NY * NZ
XP = 32
YP = 48
ZP = LANES // 2
LINES = math.lcm(NZ, LANES) // NZ
CHUNKS = math.lcm(NZ, LANES) // LANES
PERIODS = -(-NX * NY // LINES)
LINE_ROWS = PERIODS * LINES
FLAT_ROWS = PERIODS * CHUNKS
WHOLE = POINTS // LANES
TAIL = POINTS - WHOLE * LANES
SENT_ROWS = 640


def real_basis(count):
    waves = np.arange(count)
    folded = np.where(waves <= count // 2, waves, count - waves)
    angle = 2.0 * np.pi * np.outer(folded, waves) / count
    basis = np.where((waves <= count // 2)[:, None], np.cos(angle), np.sin(angle))
    return basis / np.sqrt(np.sum(basis**2, 1, keepdims=True))


def split_table(table):
    table = table.astype(np.float32)
    high = table.astype(jnp.bfloat16)
    return high, (table - high.astype(np.float32)).astype(jnp.bfloat16)


def padded(table, size):
    return np.pad(table, ((0, size - table.shape[0]), (0, size - table.shape[1])))


def lane_table(matrix):
    high, low = (np.kron(np.eye(2, dtype=jnp.bfloat16), padded(part, ZP)) for part in split_table(matrix))
    return np.block([[high, low], [high, np.zeros_like(low)]])


def row_table(matrix, size):
    high, low = (padded(part, size) for part in split_table(matrix))
    return np.concatenate([high, high, low], 1)


def kernel_table():
    def squares(count):
        places = np.arange(count)
        folded = np.where(places <= count // 2, places, places - count)
        waves = folded.astype(np.float32) * np.float32(2.0 * math.pi / (count * SPACING))
        return waves * waves

    squared = squares(NX)[None, :, None] + squares(NY)[:, None, None] + squares(NZ)[None, None, :]
    table = np.zeros((YP, XP, 2, ZP), np.float32)
    table[:NY, :NX, :, :NZ] = (4.0 * math.pi / (squared + SCREEN * SCREEN))[:, :, None, :]
    return table.reshape(YP * XP, LANES)


def split(values):
    high = values.astype(BF16)
    return high, (values - high.astype(F32)).astype(BF16)


def lane_product(values, table):
    high, low = split(values)
    halves = []
    for start in range(0, values.shape[1], LANES):
        lanes = slice(start, start + LANES)
        both = jnp.dot(jnp.concatenate([high[:, lanes], low[:, lanes]], 1), table, preferred_element_type=F32)
        halves.append(both[:, :LANES] + both[:, LANES:])
    return jnp.concatenate(halves, 1)


def row_product(table, values):
    high, low = split(values)
    return jnp.dot(table, jnp.concatenate([high, low, high], 0), preferred_element_type=F32)


def lane_ids(rows):
    return lax.broadcasted_iota(jnp.int32, (rows, LANES), 1)


def turned(values, shift):
    shift %= LANES
    return pltpu.roll(values, shift, 1) if shift else values


def line_of(flat, line, place):
    chunk, start = divmod(NZ * line, LANES)
    first = turned(flat[pl.ds(chunk, PERIODS, stride=CHUNKS), :], place - start)
    if start + NZ <= LANES:
        return first
    second = turned(flat[pl.ds(chunk + 1, PERIODS, stride=CHUNKS), :], place - start)
    return jnp.where(lane_ids(PERIODS) < place + LANES - start, first, second)


def to_lines(left, right, lines):
    ids = lane_ids(PERIODS)
    for line in range(LINES):
        low, high = line_of(left, line, 0), line_of(right, line, ZP)
        both = jnp.where(ids < NZ, low, jnp.where((ids >= ZP) & (ids < ZP + NZ), high, 0.0))
        lines[pl.ds(line, PERIODS, stride=LINES), :] = both


def to_flat(lines, flat):
    ids = lane_ids(PERIODS)
    for chunk in range(CHUNKS):
        low = chunk * LANES
        merged = None
        for line in range(low // NZ, -(-(low + LANES) // NZ)):
            value = turned(lines[pl.ds(line, PERIODS, stride=LINES), :], NZ * line - low)
            merged = value if merged is None else jnp.where(ids >= NZ * line - low, value, merged)
        flat[pl.ds(chunk, PERIODS, stride=CHUNKS), :] = merged


def fill_flat(row, flat):
    flat[pl.ds(0, WHOLE), :] = row.at[:, pl.ds(0, WHOLE * LANES)].reshape(WHOLE, LANES)[...]
    flat[pl.ds(WHOLE, flat.shape[0] - WHOLE), :] = jnp.zeros((flat.shape[0] - WHOLE, LANES), F32)
    flat[pl.ds(WHOLE, 1), pl.ds(0, TAIL)] = row[:, pl.ds(WHOLE * LANES, TAIL)]


def grouped(count, group, body):
    lax.fori_loop(0, count // group, lambda step, carry: (body(step * group), carry)[1], 0)


def prelude_kernel(position, signs, offsets, ground, response, term, own, kept, sent, row_g, row_r, sems):
    place = position[0]
    copies = [
        pltpu.make_async_copy(ground.at[pl.ds(place, 1), :], row_g, sems.at[0]),
        pltpu.make_async_copy(response, row_r, sems.at[1]),
    ]
    for copy in copies:
        copy.start()
    for copy in copies:
        copy.wait()
    fill_flat(row_g, own)
    fill_flat(row_r, kept)
    term[...] = signs[place].astype(F32) * own[...] * kept[...]
    sent[...] = kept[...]
    last = pl.ds(SENT_ROWS - 1, 1)
    kept[last, :] = jnp.full((1, LANES), offsets[0, 0].astype(F32))
    sent[last, :] = jnp.full((1, LANES), offsets[0, 1].astype(F32))


def lines_kernel(ground, lines, rows, flats, sems):
    copies = [
        pltpu.make_async_copy(ground.at[pl.ds(j, 1), :], rows.at[j], sems.at[j]) for j in range(4)
    ]
    for copy in copies:
        copy.start()
    for j in range(4):
        copies[j].wait()
        fill_flat(rows.at[j], flats.at[j])
    for half in range(2):
        to_lines(flats.at[2 * half], flats.at[2 * half + 1], lines.at[half])


def coefficient_kernel(density, own, coefficient, flat):
    fill_flat(density, flat)
    spots = lax.broadcasted_iota(jnp.int32, (SENT_ROWS, LANES), 0) * LANES + lane_ids(SENT_ROWS)
    values = jnp.where(spots < POINTS, flat[...], 1.0)
    coefficient[...] = -XC_COEF * jnp.exp(jnp.log(values) * (-2.0 / 3.0)) * own[...]


def forward_kernel(lines, response, z_table, y_table, waves, flat, response_lines):
    flat[pl.ds(0, WHOLE + 1), :] = response[pl.ds(0, WHOLE + 1), :]
    flat[pl.ds(WHOLE + 1, FLAT_ROWS - WHOLE - 1), :] = jnp.zeros((FLAT_ROWS - WHOLE - 1, LANES), F32)
    to_lines(flat, flat, response_lines)
    for half in range(2):
        for x in range(NX, XP):
            waves[half, pl.ds(x, YP, stride=XP), :] = jnp.zeros((YP, LANES), F32)
    z_weights, y_weights = z_table[...], y_table[...]
    group = 15

    def body(x):
        products = []
        for u in range(group):
            spot = pl.ds((x + u) * NY, YP)
            value = response_lines[spot, :]
            products.append(jnp.concatenate([lines[0, spot, :] * value, lines[1, spot, :] * value], 1))
        values = lane_product(jnp.concatenate(products, 0), z_weights)
        values = jnp.concatenate([values[u * YP : (u + 1) * YP] for u in range(group)], 1)
        values = row_product(y_weights, values)
        for u in range(group):
            for half in range(2):
                start = (2 * u + half) * LANES
                waves[half, pl.ds(x + u, YP, stride=XP), :] = values[:, start : start + LANES]

    grouped(NX, group, body)


def middle_kernel(waves, kernel, forward_table, inverse_table, out):
    for half in range(2):
        for y in range(NY, YP):
            out[half, pl.ds(y, XP, stride=YP), :] = jnp.zeros((XP, LANES), F32)
    forward, inverse = forward_table[...], inverse_table[...]
    group = 15

    def body(y):
        values, factors = [], []
        for u in range(group):
            spot = pl.ds(pl.multiple_of((y + u) * XP, XP), XP)
            factor = kernel[spot, :]
            values += [waves[0, spot, :], waves[1, spot, :]]
            factors += [factor, factor]
        value = row_product(forward, jnp.concatenate(values, 1))
        value = row_product(inverse, value * jnp.concatenate(factors, 1))
        for u in range(group):
            for half in range(2):
                start = (2 * u + half) * LANES
                out[half, pl.ds(y + u, XP, stride=YP), :] = value[:, start : start + LANES]

    grouped(NY, group, body)


def inverse_kernel(signs, waves, lines, response, y_table, z_table, exchange, total, flat, offset, sem):
    copy = pltpu.make_async_copy(response.at[pl.ds(SENT_ROWS - 8, 8), :], offset, sem)
    copy.start()
    copy.wait()
    z_weights, y_weights = z_table[...], y_table[...]
    ids = lane_ids(1)
    factors = []
    for half in range(2):
        orbital = 2 * half + (ids >= ZP).astype(jnp.int32)
        sign = jnp.where(ids < ZP, signs[2 * half].astype(F32), signs[2 * half + 1].astype(F32))
        factors.append(jnp.where(orbital.astype(F32) >= offset[7:8, :], sign, 0.0))
    group = 15

    def body(x):
        values = []
        for u in range(group):
            spot = pl.ds(pl.multiple_of((x + u) * YP, YP), YP)
            values += [waves[0, spot, :], waves[1, spot, :]]
        value = row_product(y_weights, jnp.concatenate(values, 1))
        value = jnp.concatenate([value[:, 2 * u * LANES : 2 * (u + 1) * LANES] for u in range(group)], 0)
        value = lane_product(value, z_weights)
        for u in range(group):
            spot = pl.ds((x + u) * NY, YP)
            rows = value[u * YP : (u + 1) * YP]
            summed = rows[:, :LANES] * (lines[0, spot, :] * factors[0])
            summed += rows[:, LANES:] * (lines[1, spot, :] * factors[1])
            total[spot, :] = summed + pltpu.roll(summed, ZP, 1)

    grouped(NX, group, body)
    to_flat(total, flat)
    exchange[...] = flat[pl.ds(0, SENT_ROWS), :]


def finish_kernel(coefficient, density, first, second, out):
    value = coefficient[...] * density[...] - HYBRID * (first[...] + second[...])
    out.at[:, pl.ds(0, WHOLE * LANES)].reshape(WHOLE, LANES)[...] = value[:WHOLE]
    out[:, pl.ds(WHOLE * LANES, TAIL)] = value[WHOLE : WHOLE + 1, :TAIL]


SCALARS = pl.BlockSpec(memory_space=pltpu.SMEM)
VECTORS = pl.BlockSpec(memory_space=pltpu.VMEM)
ANYWHERE = pl.BlockSpec(memory_space=pl.ANY)


def call(body, name, specs, shapes, scratch, microseconds, outs=None):
    cost = pl.CostEstimate(flops=int(microseconds * 1e9), bytes_accessed=int(microseconds * 1e6), transcendentals=0)
    return pl.pallas_call(
        body,
        name=name,
        in_specs=specs,
        out_shape=[jax.ShapeDtypeStruct(shape, F32) for shape in shapes],
        out_specs=[VECTORS] * len(shapes),
        scratch_shapes=scratch,
        cost_estimate=cost,
    )


def swap(values, axis, distance):
    count = lax.axis_size(axis)
    return lax.ppermute(values, axis, [(i, i ^ distance) for i in range(count)])


def summed_over_devices(term):
    orb_bits = [("orb", 1 << bit) for bit in range(lax.axis_size("orb").bit_length() - 1)]
    grid_bits = [("grid", 1 << bit) for bit in range(lax.axis_size("grid").bit_length() - 1)]
    split_bits, rest = orb_bits[:2], orb_bits[2:] + grid_bits
    for axis, distance in split_bits:
        bit = (lax.axis_index(axis) // distance) % 2
        pair = term.reshape(2, term.shape[0] // 2, LANES)
        kept = lax.dynamic_index_in_dim(pair, bit, 0, keepdims=False)
        sent = lax.dynamic_index_in_dim(pair, 1 - bit, 0, keepdims=False)
        term = kept + swap(sent, axis, distance)
    for axis, distance in rest:
        term = term + swap(term, axis, distance)
    for axis, distance in split_bits[::-1]:
        bit = (lax.axis_index(axis) // distance) % 2
        other = swap(term, axis, distance)
        term = jnp.concatenate([jnp.where(bit == 0, term, other), jnp.where(bit == 0, other, term)], 0)
    return term


def exchange_of(signs, lines, response, tables):
    waves = call(
        forward_kernel, "forward", [VECTORS] * 4, [(2, YP * XP, LANES)],
        [pltpu.VMEM((FLAT_ROWS, LANES), F32), pltpu.VMEM((LINE_ROWS, LANES), F32)], 3,
    )(lines, response, tables["z"], tables["y"])[0]
    waves = call(middle_kernel, "middle", [VECTORS] * 4, [(2, XP * YP, LANES)], [], 2)(
        waves, tables["kernel"], tables["x"], tables["x_back"]
    )[0]
    return call(
        inverse_kernel, "inverse", [SCALARS, VECTORS, VECTORS, ANYWHERE, VECTORS, VECTORS], [(SENT_ROWS, LANES)],
        [pltpu.VMEM((LINE_ROWS, LANES), F32), pltpu.VMEM((FLAT_ROWS, LANES), F32), pltpu.VMEM((8, LANES), F32),
         pltpu.SemaphoreType.DMA], 3,
    )(signs, waves, lines, response, tables["y_back"], tables["z_back"])[0]


def per_device(ground_orbitals, occupation_signs, response_orbitals, window_offsets, ground_density):
    assert ground_orbitals.shape == (4, POINTS) and response_orbitals.shape[0] == 1
    basis_x, basis_y, basis_z = real_basis(NX), real_basis(NY), real_basis(NZ)
    tables = {
        "z": lane_table(basis_z.T), "z_back": lane_table(basis_z),
        "y": row_table(basis_y, YP), "y_back": row_table(basis_y.T, YP),
        "x": row_table(basis_x, XP), "x_back": row_table(basis_x.T, XP),
        "kernel": kernel_table(),
    }
    tables = {name: jnp.asarray(table) for name, table in tables.items()}
    flat = (SENT_ROWS, LANES)
    row = pltpu.VMEM((1, POINTS), F32)
    position = lax.axis_index("grid").reshape(1)
    term, own, kept, sent = call(
        prelude_kernel, "prelude", [SCALARS] * 3 + [ANYWHERE] * 2, [flat] * 4, [row, row, pltpu.SemaphoreType.DMA((2,))], 1
    )(position, occupation_signs, window_offsets, ground_orbitals, response_orbitals)
    count = lax.axis_size("orb")
    visiting = lax.ppermute(sent, "orb", [((i + 1) % count, i) for i in range(count)])
    density = summed_over_devices(term)
    lines = call(
        lines_kernel, "lines", [ANYWHERE], [(2, LINE_ROWS, LANES)],
        [pltpu.VMEM((4, 1, POINTS), F32), pltpu.VMEM((4, FLAT_ROWS, LANES), F32), pltpu.SemaphoreType.DMA((4,))], 2,
    )(ground_orbitals)[0]
    coefficient = call(coefficient_kernel, "coefficient", [VECTORS] * 2, [flat], [pltpu.VMEM(flat, F32)], 1)(
        ground_density.reshape(1, POINTS), own
    )[0]
    away = exchange_of(occupation_signs, lines, visiting, tables)
    second = lax.ppermute(away, "orb", [(i, (i + 1) % count) for i in range(count)])
    first = exchange_of(occupation_signs, lines, kept, tables)
    return call(finish_kernel, "finish", [VECTORS] * 4, [(1, POINTS)], [], 1)(coefficient, density, first, second)[0]


def solution(mesh):
    placed = (P("orb", None), P("orb"), P(("orb", "grid"), None), P(("orb", "grid"), None), P())
    return jax.shard_map(
        per_device, mesh=mesh, in_specs=placed, out_specs=P(("orb", "grid"), None), check_vma=False
    )
```

profile of v0, /device:TPU:0, one launch (start us, length us, event | category | flops | bytes accessed | tf_op | source)
XLA Modules:
  0.0 64.1 jit_solution(8687839411596652283)
XLA Ops:
  0.0 2.9 %prelude.1 = (f32[640,128]{1,0:T(8,128)}, f32[640,128]{1,0:T(8,128)}, f32[640,128]{1,0:T(8,128)}, f32[640,128]{1,0:T(8,128)}) custom-call(s32[1]{0:T(128)} %bitcast.position, s32[4]{0:T(128)} %signs.5, s32[1,2]{1,0:T(1,128)} %offsets.1, f32[4,81000]{1,0:T(4,128)} %ground.3, f32[1,81000]{1,0:T(1,128)} %response.1), custom_call_target="tpu_custom_call" | custom-call | flops 1000000000 | bytes 1000000 | tf_op jit(solution)/shard_map/prelude/pallas_call | solution.py:345
  2.9 0.9 %dynamic-slice_bitcast_fusion = f32[320,128]{1,0:T(8,128)S(1)} fusion(f32[2,320,128]{2,1,0:T(8,128)} %bitcast.13, s32[]{:T(128)S(6)} %select_n.66), kind=kLoop, calls=%fused_computation.3 | loop fusion | bytes 327684 | tf_op jit(solution)/shard_map/jit(dynamic_index_in_dim)/squeeze | solution.py:306
  3.8 0.6 collective-permute-start
  4.4 3.5 %collective-permute-start.7 = (f32[640,128]{1,0:T(8,128)}, f32[640,128]{1,0:T(8,128)S(1)}, u32[]{:S(2)}, u32[]{:S(2)}) collective-permute-start(f32[640,128]{1,0:T(8,128)} %get-tuple-element.12), channel_id=1, source_target_pairs={{4,0},{8,4},{12,8},{16,12},{20,16},{24,20},{28,24},{0,28},{5,1},{9... | collective-permute-start | bytes 983048 | tf_op jit(solution)/shard_map/ppermute | solution.py:349
  7.9 4.2 %lines.1 = f32[2,1376,128]{2,1,0:T(8,128)} custom-call(f32[4,81000]{1,0:T(4,128)} %ground.3), custom_call_target="tpu_custom_call" | custom-call | flops 2000000000 | bytes 2000000 | tf_op jit(solution)/shard_map/lines/pallas_call | solution.py:351
  12.2 0.0 copy-start
  12.2 5.5 %forward.2.waves = f32[2,1536,128]{2,1,0:T(8,128)} custom-call(f32[2,1376,128]{2,1,0:T(8,128)} %lines.1, f32[640,128]{1,0:T(8,128)} %get-tuple-element.11.response, bf16[256,256]{1,0:T(8,128)(2,1)} %constant.84.clone.z_table, bf16[48,144]{1,0:T(8,128)(2,1)} %constant.86.clone.y_table), custom_call_target="tpu_custom_call" | custom-call | flops 3000000000 | bytes 3000000 | tf_op jit(solution)/shard_map/forward/pallas_call | solution.py:318
  17.8 0.0 collective-permute-done
  17.8 0.0 copy-done
  17.8 0.1 collective-permute-start.1
  17.9 4.2 %middle.2.waves = f32[2,1536,128]{2,1,0:T(8,128)} custom-call(f32[2,1536,128]{2,1,0:T(8,128)} %forward.2.waves, f32[1536,128]{1,0:T(8,128)} %constant.90.clone.kernel, bf16[32,96]{1,0:T(8,128)(2,1)} %constant.88.clone.forward_table, bf16[32,96]{1,0:T(8,128)(2,1)} %constant.89.clone.inverse_table), custom_call_target="tpu_custom_call" | custom-call | flops 2000000000 | bytes 2000000 | tf_op jit(solution)/shard_map/middle/pallas_call | solution.py:322
  22.1 0.2 collective-permute-done.1
  22.3 0.0 copy-start.1
  22.3 1.0 %collective-permute-start.2 = (f32[160,128]{1,0:T(8,128)S(1)}, f32[160,128]{1,0:T(8,128)S(1)}, u32[]{:S(2)}, u32[]{:S(2)}) collective-permute-start(f32[160,128]{1,0:T(8,128)S(1)} %bitcast_add_fusion.1), channel_id=1, source_target_pairs={{0,16},{4,20},{8,24},{12,28},{16,0},{20,4},{24,8},{28,12},{1,17},{... | collective-permute-start | bytes 245768 | tf_op jit(solution)/shard_map/ppermute | solution.py:295
  23.3 5.0 %inverse.2.first = f32[640,128]{1,0:T(8,128)} custom-call(s32[4]{0:T(128)} %signs.5, f32[2,1536,128]{2,1,0:T(8,128)} %middle.2.waves, f32[2,1376,128]{2,1,0:T(8,128)} %lines.1, f32[640,128]{1,0:T(8,128)} %get-tuple-element.11.response, bf16[48,144]{1,0:T(8,128)(2,1)} %constant.87.clone.y_table, bf16[256,256]{1,0:T(8,128)(2,1)} %constant.85.clone.z_table), custom_call_target="tpu_custom_call" | custom-call | flops 3000000000 | bytes 3000000 | tf_op jit(solution)/shard_map/inverse/pallas_call | solution.py:325
  28.3 0.0 copy-done.1
  28.3 0.9 %reshape.12.density = f32[1,81000]{1,0:T(1,128)} reshape(f32[81000]{0:T(1024)S(1)} %copy-done.1) | data formatting | bytes 648000 | tf_op jit(solution)/shard_map/reshape | solution.py:356
  29.2 0.0 collective-permute-done.2
  29.3 1.6 %collective-permute-start.3 = (f32[160,128]{1,0:T(8,128)S(1)}, f32[160,128]{1,0:T(8,128)S(1)}, u32[]{:S(2)}, u32[]{:S(2)}) collective-permute-start(f32[160,128]{1,0:T(8,128)S(1)} %add.50), channel_id=1, source_target_pairs={{0,1},{1,0},{2,3},{3,2},{4,5},{5,4},{6,7},{7,6},{8,9},{9,8},{10,11... | collective-permute-start | bytes 245768 | tf_op jit(solution)/shard_map/ppermute | solution.py:295
  30.9 2.0 %coefficient.1 = f32[640,128]{1,0:T(8,128)} custom-call(f32[1,81000]{1,0:T(1,128)} %reshape.12.density, f32[640,128]{1,0:T(8,128)} %get-tuple-element.9.own), custom_call_target="tpu_custom_call" | custom-call | flops 1000000000 | bytes 1000000 | tf_op jit(solution)/shard_map/coefficient/pallas_call | solution.py:355
  32.9 0.9 %collective-permute-done.3 = f32[160,128]{1,0:T(8,128)S(1)} collective-permute-done((f32[160,128]{1,0:T(8,128)S(1)}, f32[160,128]{1,0:T(8,128)S(1)}, u32[]{:S(2)}, u32[]{:S(2)}) %collective-permute-start.3) | collective-permute-done | bytes 81952 | tf_op jit(solution)/shard_map/ppermute | solution.py:295
  33.8 2.6 %collective-permute-start.4 = (f32[160,128]{1,0:T(8,128)S(1)}, f32[160,128]{1,0:T(8,128)S(1)}, u32[]{:S(2)}, u32[]{:S(2)}) collective-permute-start(f32[160,128]{1,0:T(8,128)S(1)} %add.51), channel_id=1, source_target_pairs={{0,2},{1,3},{2,0},{3,1},{4,6},{5,7},{6,4},{7,5},{8,10},{9,11},{10,... | collective-permute-start | bytes 245768 | tf_op jit(solution)/shard_map/ppermute | solution.py:295
  36.4 0.0 collective-permute-done.7.response
  36.4 0.0 copy-start.2
  36.4 0.7 %copy-done.2 = f32[640,128]{1,0:T(8,128)} copy-done((f32[640,128]{1,0:T(8,128)}, f32[640,128]{1,0:T(8,128)S(1)}, u32[]{:S(2)}) %copy-start.2) | copy-done | bytes 327704
  37.2 5.5 %forward.3.waves = f32[2,1536,128]{2,1,0:T(8,128)} custom-call(f32[2,1376,128]{2,1,0:T(8,128)} %lines.1, f32[640,128]{1,0:T(8,128)} %copy-done.2, bf16[256,256]{1,0:T(8,128)(2,1)} %constant.84.clone.z_table, bf16[48,144]{1,0:T(8,128)(2,1)} %constant.86.clone.y_table), custom_call_target="tpu_custom_call" | custom-call | flops 3000000000 | bytes 3000000 | tf_op jit(solution)/shard_map/forward/pallas_call | solution.py:318
  42.7 0.0 collective-permute-done.4
  42.7 1.6 %collective-permute-start.5 = (f32[160,128]{1,0:T(8,128)S(1)}, f32[160,128]{1,0:T(8,128)S(1)}, u32[]{:S(2)}, u32[]{:S(2)}) collective-permute-start(f32[160,128]{1,0:T(8,128)S(1)} %add.52), channel_id=1, source_target_pairs={{0,8},{4,12},{8,0},{12,4},{16,24},{20,28},{24,16},{28,20},{1,9},{5... | collective-permute-start | bytes 245768 | tf_op jit(solution)/shard_map/ppermute | solution.py:295
  44.3 4.2 %middle.3.waves = f32[2,1536,128]{2,1,0:T(8,128)} custom-call(f32[2,1536,128]{2,1,0:T(8,128)} %forward.3.waves, f32[1536,128]{1,0:T(8,128)} %constant.90.clone.kernel, bf16[32,96]{1,0:T(8,128)(2,1)} %constant.88.clone.forward_table, bf16[32,96]{1,0:T(8,128)(2,1)} %constant.89.clone.inverse_table), custom_call_target="tpu_custom_call" | custom-call | flops 2000000000 | bytes 2000000 | tf_op jit(solution)/shard_map/middle/pallas_call | solution.py:322
  48.6 0.0 collective-permute-done.5
  48.6 0.1 collective-permute-start.6
  48.7 5.0 %inverse.3 = f32[640,128]{1,0:T(8,128)} custom-call(s32[4]{0:T(128)} %signs.5, f32[2,1536,128]{2,1,0:T(8,128)} %middle.3.waves, f32[2,1376,128]{2,1,0:T(8,128)} %lines.1, f32[640,128]{1,0:T(8,128)} %copy-done.2, bf16[48,144]{1,0:T(8,128)(2,1)} %constant.87.clone.y_table, bf16[256,256]{1,0:T(8,128)(2,1)} %constant.85.clone.z_table), custom_call_target="tpu_custom_call" | custom-call | flops 3000000000 | bytes 3000000 | tf_op jit(solution)/shard_map/inverse/pallas_call | solution.py:325
  53.6 0.5 collective-permute-start.8
  54.2 0.0 collective-permute-done.6
  54.2 0.7 %pad_maximum_fusion.density = f32[640,128]{1,0:T(8,128)} fusion(f32[320,128]{1,0:T(8,128)S(1)} %get-tuple-element.14, f32[320,128]{1,0:T(8,128)S(1)} %get-tuple-element.13), kind=kLoop, calls=%fused_computation | loop fusion | flops 81920 | bytes 655360 | tf_op jit(solution)/shard_map/concatenate | solution.py:313
  55.0 6.3 %collective-permute-done.8.second = f32[640,128]{1,0:T(8,128)S(1)} collective-permute-done((f32[640,128]{1,0:T(8,128)}, f32[640,128]{1,0:T(8,128)S(1)}, u32[]{:S(2)}, u32[]{:S(2)}) %collective-permute-start.8) | collective-permute-done | bytes 327712 | tf_op jit(solution)/shard_map/ppermute | solution.py:359
  61.3 0.0 copy-start.3
  61.3 0.7 %copy-done.3 = f32[640,128]{1,0:T(8,128)} copy-done((f32[640,128]{1,0:T(8,128)}, f32[640,128]{1,0:T(8,128)S(1)}, u32[]{:S(2)}) %copy-start.3) | copy-done | bytes 327704
  62.0 2.1 %finish.1 = f32[1,81000]{1,0:T(1,128)} custom-call(f32[640,128]{1,0:T(8,128)} %coefficient.1, f32[640,128]{1,0:T(8,128)} %pad_maximum_fusion.density, f32[640,128]{1,0:T(8,128)} %inverse.2.first, f32[640,128]{1,0:T(8,128)} %copy-done.3), custom_call_target="tpu_custom_call" | custom-call | flops 1000000000 | bytes 1000000 | tf_op jit(solution)/shard_map/finish/pallas_call | solution.py:361
  (9 shorter events, 0.1 us)
Async XLA Ops:
  3.8 13.9 %collective-permute-start = (f32[320,128]{1,0:T(8,128)S(1)}, f32[320,128]{1,0:T(8,128)S(1)}, u32[]{:S(2)}, u32[]{:S(2)}) collective-permute-start(f32[320,128]{1,0:T(8,128)S(1)} %dynamic-slice_bitcast_fusion), channel_id=1, source_target_pairs={{0,4},{4,0},{8,12},{12,8},{16,20},{20,16},{24,28},{28,24},{1,5},{5... | collective-permute-start | bytes 491528 | tf_op jit(solution)/shard_map/ppermute | solution.py:295
  4.4 32.0 %collective-permute-start.7 = (f32[640,128]{1,0:T(8,128)}, f32[640,128]{1,0:T(8,128)S(1)}, u32[]{:S(2)}, u32[]{:S(2)}) collective-permute-start(f32[640,128]{1,0:T(8,128)} %get-tuple-element.12), channel_id=1, source_target_pairs={{4,0},{8,4},{12,8},{16,12},{20,16},{24,20},{28,24},{0,28},{5,1},{9... | collective-permute-start | bytes 983048 | tf_op jit(solution)/shard_map/ppermute | solution.py:349
  12.2 5.6 %copy-start = (f32[640,128]{1,0:T(8,128)S(1)}, f32[640,128]{1,0:T(8,128)}, u32[]{:S(2)}) copy-start(f32[640,128]{1,0:T(8,128)} %get-tuple-element.10) | copy-start | bytes 983044
  17.8 4.5 %collective-permute-start.1 = (f32[160,128]{1,0:T(8,128)S(1)}, f32[160,128]{1,0:T(8,128)S(1)}, u32[]{:S(2)}, u32[]{:S(2)}) collective-permute-start(f32[160,128]{1,0:T(8,128)S(1)} %dynamic-slice_bitcast_fusion.1), channel_id=1, source_target_pairs={{0,8},{4,12},{8,0},{12,4},{16,24},{20,28},{24,16},{28,20},{1,9},{5... | collective-permute-start | bytes 245768 | tf_op jit(solution)/shard_map/ppermute | solution.py:295
  22.3 6.0 %copy-start.1 = (f32[81000]{0:T(1024)S(1)}, f32[81000]{0:T(1024)}, u32[]{:S(2)}) copy-start(f32[81000]{0:T(1024)} %param.16) | copy-start | bytes 972004
  22.3 6.9 %collective-permute-start.2 = (f32[160,128]{1,0:T(8,128)S(1)}, f32[160,128]{1,0:T(8,128)S(1)}, u32[]{:S(2)}, u32[]{:S(2)}) collective-permute-start(f32[160,128]{1,0:T(8,128)S(1)} %bitcast_add_fusion.1), channel_id=1, source_target_pairs={{0,16},{4,20},{8,24},{12,28},{16,0},{20,4},{24,8},{28,12},{1,17},{... | collective-permute-start | bytes 245768 | tf_op jit(solution)/shard_map/ppermute | solution.py:295
  29.3 4.5 %collective-permute-start.3 = (f32[160,128]{1,0:T(8,128)S(1)}, f32[160,128]{1,0:T(8,128)S(1)}, u32[]{:S(2)}, u32[]{:S(2)}) collective-permute-start(f32[160,128]{1,0:T(8,128)S(1)} %add.50), channel_id=1, source_target_pairs={{0,1},{1,0},{2,3},{3,2},{4,5},{5,4},{6,7},{7,6},{8,9},{9,8},{10,11... | collective-permute-start | bytes 245768 | tf_op jit(solution)/shard_map/ppermute | solution.py:295
  33.8 8.9 %collective-permute-start.4 = (f32[160,128]{1,0:T(8,128)S(1)}, f32[160,128]{1,0:T(8,128)S(1)}, u32[]{:S(2)}, u32[]{:S(2)}) collective-permute-start(f32[160,128]{1,0:T(8,128)S(1)} %add.51), channel_id=1, source_target_pairs={{0,2},{1,3},{2,0},{3,1},{4,6},{5,7},{6,4},{7,5},{8,10},{9,11},{10,... | collective-permute-start | bytes 245768 | tf_op jit(solution)/shard_map/ppermute | solution.py:295
  36.4 0.8 %copy-start.2 = (f32[640,128]{1,0:T(8,128)}, f32[640,128]{1,0:T(8,128)S(1)}, u32[]{:S(2)}) copy-start(f32[640,128]{1,0:T(8,128)S(1)} %collective-permute-done.7.response) | copy-start | bytes 983044
  42.7 5.8 %collective-permute-start.5 = (f32[160,128]{1,0:T(8,128)S(1)}, f32[160,128]{1,0:T(8,128)S(1)}, u32[]{:S(2)}, u32[]{:S(2)}) collective-permute-start(f32[160,128]{1,0:T(8,128)S(1)} %add.52), channel_id=1, source_target_pairs={{0,8},{4,12},{8,0},{12,4},{16,24},{20,28},{24,16},{28,20},{1,9},{5... | collective-permute-start | bytes 245768 | tf_op jit(solution)/shard_map/ppermute | solution.py:295
  48.6 5.6 %collective-permute-start.6 = (f32[320,128]{1,0:T(8,128)S(1)}, f32[320,128]{1,0:T(8,128)S(1)}, u32[]{:S(2)}, u32[]{:S(2)}) collective-permute-start(f32[320,128]{1,0:T(8,128)S(1)} %pad_maximum_fusion.1), channel_id=1, source_target_pairs={{0,4},{4,0},{8,12},{12,8},{16,20},{20,16},{24,28},{28,24},{1,5},{5... | collective-permute-start | bytes 491528 | tf_op jit(solution)/shard_map/ppermute | solution.py:295
  53.6 7.7 %collective-permute-start.8 = (f32[640,128]{1,0:T(8,128)}, f32[640,128]{1,0:T(8,128)S(1)}, u32[]{:S(2)}, u32[]{:S(2)}) collective-permute-start(f32[640,128]{1,0:T(8,128)} %inverse.3), channel_id=1, source_target_pairs={{0,4},{4,8},{8,12},{12,16},{16,20},{20,24},{24,28},{28,0},{1,5},{5... | collective-permute-start | bytes 983048 | tf_op jit(solution)/shard_map/ppermute | solution.py:359
  61.3 0.7 %copy-start.3 = (f32[640,128]{1,0:T(8,128)}, f32[640,128]{1,0:T(8,128)S(1)}, u32[]{:S(2)}) copy-start(f32[640,128]{1,0:T(8,128)S(1)} %collective-permute-done.8.second) | copy-start | bytes 983044
where the time goes:
time: 64.6 us; the launch traced here: 64.1 us
  Pallas kernels  40.6 us (63%)
  starting transfers between devices  11.7 us (18%)
  waiting for transfers between devices  7.47 us (12%)
  local copies, waits for them, and re-layouts  3.38 us (5%)
  other arithmetic  0.85 us (1%)
    pallas_call x2, Pallas kernels, exchange_of(): call(forward_kernel, 'forward', [VECTORS] * 4, [(2, YP * XP, LANES)], [pl...  11.1 us
    pallas_call x2, Pallas kernels, exchange_of(): call(inverse_kernel, 'inverse', [SCALARS, VECTORS, VECTORS, ANYWHERE, VEC...  9.94 us
    pallas_call x2, Pallas kernels, exchange_of(): call(middle_kernel, 'middle', [VECTORS] * 4, [(2, XP * YP, LANES)], [], 2)  8.44 us
    ppermute x7, starting transfers between devices, swap(): return lax.ppermute(values, axis, [(i, i ^ distance) for i in range(count)])  7.57 us
    ppermute x1, waiting for transfers between devices, per_device(): lax.ppermute(away, 'orb', [(i, (i + 1) % count) for i in range(count)])  6.34 us
    pallas_call x1, Pallas kernels, per_device(): call(lines_kernel, 'lines', [ANYWHERE], [(2, LINE_ROWS, LANES)], [pltpu.V...  4.23 us
    ppermute x1, starting transfers between devices, per_device(): lax.ppermute(sent, 'orb', [((i + 1) % count, i) for i in range(count)])  3.54 us
    pallas_call x1, Pallas kernels, per_device(): call(prelude_kernel, 'prelude', [SCALARS] * 3 + [ANYWHERE] * 2, [flat] *...  2.89 us
  transfers between devices with their start and end apart: 9, of which 3 were waited for; matrix products, arithmetic and copies ran while one was open for 3% of the time, Pallas kernels for 56%

commit v1 on v0

--- a/solution.py
+++ b/solution.py
@@ -182,86 +182,64 @@
     coefficient[...] = -XC_COEF * jnp.exp(jnp.log(values) * (-2.0 / 3.0)) * own[...]
 
 
-def forward_kernel(lines, response, z_table, y_table, waves, flat, response_lines):
+def solve_half(half, signs, lines, values, offset, tables, kernel, waves, turned_waves, total, prior):
+    z_table, z_back, y_table, y_back, x_table, x_back = (table[...] for table in tables)
+    group = 15
+    for x in range(NX, XP):
+        waves[pl.ds(x, YP, stride=XP), :] = jnp.zeros((YP, LANES), F32)
+    for y in range(NY, YP):
+        turned_waves[pl.ds(y, XP, stride=YP), :] = jnp.zeros((XP, LANES), F32)
+
+    def forward(x):
+        spots = [pl.ds((x + u) * NY, YP) for u in range(group)]
+        value = lane_product(jnp.concatenate([lines[spot, :] * values[spot, :] for spot in spots], 0), z_table)
+        value = row_product(y_table, jnp.concatenate([value[u * YP : (u + 1) * YP] for u in range(group)], 1))
+        for u in range(group):
+            waves[pl.ds(x + u, YP, stride=XP), :] = value[:, u * LANES : (u + 1) * LANES]
+
+    def middle(y):
+        spots = [pl.ds(pl.multiple_of((y + u) * XP, XP), XP) for u in range(group)]
+        value = row_product(x_table, jnp.concatenate([waves[spot, :] for spot in spots], 1))
+        value = row_product(x_back, value * jnp.concatenate([kernel[spot, :] for spot in spots], 1))
+        for u in range(group):
+            turned_waves[pl.ds(y + u, XP, stride=YP), :] = value[:, u * LANES : (u + 1) * LANES]
+
+    ids = lane_ids(1)
+    orbital = 2 * half + (ids >= ZP).astype(jnp.int32)
+    sign = jnp.where(ids < ZP, signs[2 * half].astype(F32), signs[2 * half + 1].astype(F32))
+    factor = jnp.where(orbital.astype(F32) >= offset, sign, 0.0)
+
+    def backward(x):
+        spots = [pl.ds(pl.multiple_of((x + u) * YP, YP), YP) for u in range(group)]
+        value = row_product(y_back, jnp.concatenate([turned_waves[spot, :] for spot in spots], 1))
+        value = jnp.concatenate([value[:, u * LANES : (u + 1) * LANES] for u in range(group)], 0)
+        value = lane_product(value, z_back)
+        for u in range(group):
+            spot = pl.ds((x + u) * NY, YP)
+            part = value[u * YP : (u + 1) * YP] * (lines[spot, :] * factor)
+            if prior is not None:
+                part += prior[spot, :]
+                part += pltpu.roll(part, ZP, 1)
+            total[spot, :] = part
+
+    grouped(NX, group, forward)
+    grouped(NY, group, middle)
+    grouped(NX, group, backward)
+
+
+def first_half_kernel(signs, lines, response, *refs):
+    tables, (kernel, values, partial, flat, waves, turned_waves) = refs[:6], refs[6:]
     flat[pl.ds(0, WHOLE + 1), :] = response[pl.ds(0, WHOLE + 1), :]
     flat[pl.ds(WHOLE + 1, FLAT_ROWS - WHOLE - 1), :] = jnp.zeros((FLAT_ROWS - WHOLE - 1, LANES), F32)
-    to_lines(flat, flat, response_lines)
-    for half in range(2):
-        for x in range(NX, XP):
-            waves[half, pl.ds(x, YP, stride=XP), :] = jnp.zeros((YP, LANES), F32)
-    z_weights, y_weights = z_table[...], y_table[...]
-    group = 15
-
-    def body(x):
-        products = []
-        for u in range(group):
-            spot = pl.ds((x + u) * NY, YP)
-            value = response_lines[spot, :]
-            products.append(jnp.concatenate([lines[0, spot, :] * value, lines[1, spot, :] * value], 1))
-        values = lane_product(jnp.concatenate(products, 0), z_weights)
-        values = jnp.concatenate([values[u * YP : (u + 1) * YP] for u in range(group)], 1)
-        values = row_product(y_weights, values)
-        for u in range(group):
-            for half in range(2):
-                start = (2 * u + half) * LANES
-                waves[half, pl.ds(x + u, YP, stride=XP), :] = values[:, start : start + LANES]
-
-    grouped(NX, group, body)
-
-
-def middle_kernel(waves, kernel, forward_table, inverse_table, out):
-    for half in range(2):
-        for y in range(NY, YP):
-            out[half, pl.ds(y, XP, stride=YP), :] = jnp.zeros((XP, LANES), F32)
-    forward, inverse = forward_table[...], inverse_table[...]
-    group = 15
-
-    def body(y):
-        values, factors = [], []
-        for u in range(group):
-            spot = pl.ds(pl.multiple_of((y + u) * XP, XP), XP)
-            factor = kernel[spot, :]
-            values += [waves[0, spot, :], waves[1, spot, :]]
-            factors += [factor, factor]
-        value = row_product(forward, jnp.concatenate(values, 1))
-        value = row_product(inverse, value * jnp.concatenate(factors, 1))
-        for u in range(group):
-            for half in range(2):
-                start = (2 * u + half) * LANES
-                out[half, pl.ds(y + u, XP, stride=YP), :] = value[:, start : start + LANES]
-
-    grouped(NY, group, body)
-
-
-def inverse_kernel(signs, waves, lines, response, y_table, z_table, exchange, total, flat, offset, sem):
-    copy = pltpu.make_async_copy(response.at[pl.ds(SENT_ROWS - 8, 8), :], offset, sem)
-    copy.start()
-    copy.wait()
-    z_weights, y_weights = z_table[...], y_table[...]
-    ids = lane_ids(1)
-    factors = []
-    for half in range(2):
-        orbital = 2 * half + (ids >= ZP).astype(jnp.int32)
-        sign = jnp.where(ids < ZP, signs[2 * half].astype(F32), signs[2 * half + 1].astype(F32))
-        factors.append(jnp.where(orbital.astype(F32) >= offset[7:8, :], sign, 0.0))
-    group = 15
-
-    def body(x):
-        values = []
-        for u in range(group):
-            spot = pl.ds(pl.multiple_of((x + u) * YP, YP), YP)
-            values += [waves[0, spot, :], waves[1, spot, :]]
-        value = row_product(y_weights, jnp.concatenate(values, 1))
-        value = jnp.concatenate([value[:, 2 * u * LANES : 2 * (u + 1) * LANES] for u in range(group)], 0)
-        value = lane_product(value, z_weights)
-        for u in range(group):
-            spot = pl.ds((x + u) * NY, YP)
-            rows = value[u * YP : (u + 1) * YP]
-            summed = rows[:, :LANES] * (lines[0, spot, :] * factors[0])
-            summed += rows[:, LANES:] * (lines[1, spot, :] * factors[1])
-            total[spot, :] = summed + pltpu.roll(summed, ZP, 1)
-
-    grouped(NX, group, body)
+    to_lines(flat, flat, values)
+    offset = response[pl.ds(SENT_ROWS - 1, 1), :]
+    solve_half(0, signs, lines.at[0], values, offset, tables, kernel, waves, turned_waves, partial, None)
+
+
+def second_half_kernel(signs, lines, response, *refs):
+    tables, (kernel, values, partial, exchange, flat, waves, turned_waves, total) = refs[:6], refs[6:]
+    offset = response[pl.ds(SENT_ROWS - 1, 1), :]
+    solve_half(1, signs, lines.at[1], values, offset, tables, kernel, waves, turned_waves, total, partial)
     to_flat(total, flat)
     exchange[...] = flat[pl.ds(0, SENT_ROWS), :]
 
@@ -277,17 +255,27 @@
 ANYWHERE = pl.BlockSpec(memory_space=pl.ANY)
 
 
+def near(shape):
+    return pltpu.VMEM(shape, F32) if shape != (1, POINTS) else jax.ShapeDtypeStruct(shape, F32)
+
+
+def held(values):
+    return pltpu.with_memory_space_constraint(values, pltpu.VMEM)
+
+
 def call(body, name, specs, shapes, scratch, microseconds, outs=None):
     cost = pl.CostEstimate(flops=int(microseconds * 1e9), bytes_accessed=int(microseconds * 1e6), transcendentals=0)
-    return pl.pallas_call(
+    kernel = pl.pallas_call(
         body,
         name=name,
         in_specs=specs,
-        out_shape=[jax.ShapeDtypeStruct(shape, F32) for shape in shapes],
+        out_shape=[near(shape) for shape in shapes],
         out_specs=[VECTORS] * len(shapes),
         scratch_shapes=scratch,
         cost_estimate=cost,
+        compiler_params=pltpu.CompilerParams(vmem_limit_bytes=12 * 2**20),
     )
+    return lambda *values: kernel(*(held(v) if spec is VECTORS else v for spec, v in zip(specs, values)))
 
 
 def swap(values, axis, distance):
@@ -315,30 +303,26 @@
 
 
 def exchange_of(signs, lines, response, tables):
-    waves = call(
-        forward_kernel, "forward", [VECTORS] * 4, [(2, YP * XP, LANES)],
-        [pltpu.VMEM((FLAT_ROWS, LANES), F32), pltpu.VMEM((LINE_ROWS, LANES), F32)], 3,
-    )(lines, response, tables["z"], tables["y"])[0]
-    waves = call(middle_kernel, "middle", [VECTORS] * 4, [(2, XP * YP, LANES)], [], 2)(
-        waves, tables["kernel"], tables["x"], tables["x_back"]
-    )[0]
+    shared = (signs, lines, response, *tables)
+    flat, line = pltpu.VMEM((FLAT_ROWS, LANES), F32), pltpu.VMEM((LINE_ROWS, LANES), F32)
+    waves = pltpu.VMEM((XP * YP, LANES), F32)
+    specs = [SCALARS] + [VECTORS] * (2 + len(tables))
+    values, partial = call(first_half_kernel, "first_half", specs, [(LINE_ROWS, LANES)] * 2, [flat, waves, waves], 3)(*shared)
     return call(
-        inverse_kernel, "inverse", [SCALARS, VECTORS, VECTORS, ANYWHERE, VECTORS, VECTORS], [(SENT_ROWS, LANES)],
-        [pltpu.VMEM((LINE_ROWS, LANES), F32), pltpu.VMEM((FLAT_ROWS, LANES), F32), pltpu.VMEM((8, LANES), F32),
-         pltpu.SemaphoreType.DMA], 3,
-    )(signs, waves, lines, response, tables["y_back"], tables["z_back"])[0]
+        second_half_kernel, "second_half", specs + [VECTORS] * 2, [(SENT_ROWS, LANES)], [flat, waves, waves, line], 3
+    )(*shared, values, partial)[0]
 
 
 def per_device(ground_orbitals, occupation_signs, response_orbitals, window_offsets, ground_density):
     assert ground_orbitals.shape == (4, POINTS) and response_orbitals.shape[0] == 1
     basis_x, basis_y, basis_z = real_basis(NX), real_basis(NY), real_basis(NZ)
-    tables = {
-        "z": lane_table(basis_z.T), "z_back": lane_table(basis_z),
-        "y": row_table(basis_y, YP), "y_back": row_table(basis_y.T, YP),
-        "x": row_table(basis_x, XP), "x_back": row_table(basis_x.T, XP),
-        "kernel": kernel_table(),
-    }
-    tables = {name: jnp.asarray(table) for name, table in tables.items()}
+    tables = (
+        lane_table(basis_z.T), lane_table(basis_z),
+        row_table(basis_y, YP), row_table(basis_y.T, YP),
+        row_table(basis_x, XP), row_table(basis_x.T, XP),
+        kernel_table(),
+    )
+    tables = tuple(jnp.asarray(table) for table in tables)
     flat = (SENT_ROWS, LANES)
     row = pltpu.VMEM((1, POINTS), F32)
     position = lax.axis_index("grid").reshape(1)

time: 64.6 us -> 57.3 us (0.89)
  Pallas kernels: 40.6 us -> 22.6 us
  local copies, waits for them, and re-layouts: 3.38 us -> 8.92 us
  waiting for transfers between devices: 7.47 us -> 11.5 us
  starting transfers between devices: 11.7 us -> 12.6 us
    pallas_call x10 -> x8, Pallas kernels: 40.6 us -> 22.6 us  [call(): kernel(*(held(v) if spec is VECTORS else v for spec, v in zip(specs, valu...]
    unnamed x8 -> x38, local copies, waits for them, and re-layouts: 1.49 us -> 7.68 us
    ppermute x7, waiting for transfers between devices: 1.12 us -> 4.64 us  [swap(): return lax.ppermute(values, axis, [(i, i ^ distance) for i in range(count)])]
    ppermute x7, starting transfers between devices: 7.57 us -> 8.55 us  [swap(): return lax.ppermute(values, axis, [(i, i ^ distance) for i in range(count)])]
    add x2, other arithmetic: 0.03 us -> 0.96 us  [summed_over_devices(): term = kept + swap(sent, axis, distance)]
    squeeze x2, local copies, waits for them, and re-layouts: 0.95 us -> 0.04 us  [summed_over_devices(): sent = lax.dynamic_index_in_dim(pair, 1 - bit, 0, keepdims=False)]
    concatenate x2, other arithmetic: 0.75 us -> 0.04 us  [summed_over_devices(): jnp.concatenate([jnp.where(bit == 0, term, other), jnp.where(bit == 0, ot...]
  transfers between devices with their start and end apart: 9 -> 9, of which waited for: 3 -> 3; matrix products, arithmetic and copies ran while one was open for 3% -> 4% of each run, Pallas kernels for 56% -> 36%
where the time goes in v1:
time: 57.3 us; the launch traced here: 57 us
  Pallas kernels  22.6 us (39%)
  starting transfers between devices  12.6 us (22%)
  waiting for transfers between devices  11.5 us (20%)
  local copies, waits for them, and re-layouts  8.92 us (16%)
  other arithmetic  1.07 us (2%)
    pallas_call x8, Pallas kernels, call(): kernel(*(held(v) if spec is VECTORS else v for spec, v in zip(specs, valu...  22.6 us
    ppermute x7, starting transfers between devices, swap(): return lax.ppermute(values, axis, [(i, i ^ distance) for i in range(count)])  8.55 us
    unnamed x38, local copies, waits for them, and re-layouts  7.68 us
    ppermute x1, waiting for transfers between devices, per_device(): lax.ppermute(away, 'orb', [(i, (i + 1) % count) for i in range(count)])  6.84 us
    ppermute x7, waiting for transfers between devices, swap(): return lax.ppermute(values, axis, [(i, i ^ distance) for i in range(count)])  4.64 us
    ppermute x1, starting transfers between devices, per_device(): lax.ppermute(sent, 'orb', [((i + 1) % count, i) for i in range(count)])  3.54 us
    reshape x1, local copies, waits for them, and re-layouts, per_device(): ground_density.reshape(1, POINTS)  1.2 us
  transfers between devices with their start and end apart: 9, of which 3 were waited for; matrix products, arithmetic and copies ran while one was open for 4% of the time, Pallas kernels for 36%

profile of v1, /device:TPU:0, one launch (start us, length us, event | category | flops | bytes accessed | tf_op | source)
XLA Modules:
  0.0 57.0 jit_solution(239489170492260119)
XLA Ops:
  0.0 1.3 %copy-done = f32[4,81000]{1,0:T(4,128)S(1)} copy-done((f32[4,81000]{1,0:T(4,128)S(1)}, f32[4,81000]{1,0:T(4,128)}, u32[]{:S(2)}) %copy-start) | copy-done | bytes 1296024
  1.3 1.0 %copy-done.2 = f32[1,81000]{1,0:T(1,128)S(1)} copy-done((f32[1,81000]{1,0:T(1,128)S(1)}, f32[1,81000]{1,0:T(1,128)}, u32[]{:S(2)}) %copy-start.2) | copy-done | bytes 324024
  2.3 0.7 %copy-done.3 = s32[1,2]{1,0:T(1,128)S(1)} copy-done((s32[1,2]{1,0:T(1,128)S(1)}, s32[1,2]{1,0:T(1,128)}, u32[]{:S(2)}) %copy-start.3) | copy-done | bytes 32
  2.9 0.7 %copy-done.4 = s32[4]{0:T(128)S(1)} copy-done((s32[4]{0:T(128)S(1)}, s32[4]{0:T(128)}, u32[]{:S(2)}) %copy-start.4) | copy-done | bytes 40
  3.6 1.0 %prelude.1 = (f32[640,128]{1,0:T(8,128)S(1)}, f32[640,128]{1,0:T(8,128)S(1)}, f32[640,128]{1,0:T(8,128)S(1)}, f32[640,128]{1,0:T(8,128)S(1)}) custom-call(s32[1]{0:T(128)} %bitcast.position, s32[4]{0:T(128)S(1)} %copy-done.4, s32[1,2]{1,0:T(1,128)S(1)} %copy-done.3, f32[4,81000]{1,0:T(4,128)S(1)} %copy-done, f32[1,81000]{1,0:T(1,128)S(1)} %copy-done.2), custom_call_target="tpu_custom_call" | custom-call | flops 1000000000 | bytes 1000000 | tf_op jit(solution)/shard_map/prelude/pallas_call | solution.py:278
  4.6 0.0 copy-start.13
  4.6 0.6 collective-permute-start
  5.2 3.5 %collective-permute-start.7 = (f32[640,128]{1,0:T(8,128)S(1)}, f32[640,128]{1,0:T(8,128)S(1)}, u32[]{:S(2)}, u32[]{:S(2)}) collective-permute-start(f32[640,128]{1,0:T(8,128)S(1)} %get-tuple-element.18), channel_id=1, source_target_pairs={{4,0},{8,4},{12,8},{16,12},{20,16},{24,20},{28,24},{0,28},{5,1},{9... | collective-permute-start | bytes 983048 | tf_op jit(solution)/shard_map/ppermute | solution.py:333
  8.7 0.0 collective-permute-done
  8.8 0.0 copy-start.18
  8.8 0.0 copy-done.13
  8.8 0.6 %copy-done.18 = f32[320,128]{1,0:T(8,128)} copy-done((f32[320,128]{1,0:T(8,128)}, f32[320,128]{1,0:T(8,128)S(1)}, u32[]{:S(2)}) %copy-start.18) | copy-done | bytes 163864
  9.4 0.0 copy-start.9
  9.5 0.0 copy-start.10
  9.5 0.0 copy-start.11
  9.5 0.0 copy-start.12
  9.5 0.4 collective-permute-start.1
  9.9 0.0 copy-done.1
  9.9 2.8 %lines.1 = f32[2,1376,128]{2,1,0:T(8,128)S(1)} custom-call(f32[4,81000]{1,0:T(4,128)S(1)} %copy-done.1), custom_call_target="tpu_custom_call" | custom-call | flops 2000000000 | bytes 2000000 | tf_op jit(solution)/shard_map/lines/pallas_call | solution.py:278
  12.7 0.0 copy-start.15
  12.7 1.1 %copy-done.15 = f32[2,1376,128]{2,1,0:T(8,128)} copy-done((f32[2,1376,128]{2,1,0:T(8,128)}, f32[2,1376,128]{2,1,0:T(8,128)S(1)}, u32[]{:S(2)}) %copy-start.15) | copy-done | bytes 1409048
  13.8 1.3 %collective-permute-done.1 = f32[160,128]{1,0:T(8,128)} collective-permute-done((f32[160,128]{1,0:T(8,128)S(1)}, f32[160,128]{1,0:T(8,128)}, u32[]{:S(2)}, u32[]{:S(2)}) %collective-permute-start.1) | collective-permute-done | bytes 81952 | tf_op jit(solution)/shard_map/ppermute | solution.py:283
  15.1 0.9 %bitcast_add_fusion.1 = f32[160,128]{1,0:T(8,128)S(1)} fusion(f32[160,128]{1,0:T(8,128)} %collective-permute-done.1, f32[2,160,128]{2,1,0:T(8,128)} %bitcast.14, s32[]{:T(128)S(6)} %select_n.67), kind=kLoop, calls=%fused_computation.4 | loop fusion | flops 20480 | bytes 245764 | tf_op jit(solution)/shard_map/add | solution.py:295
  16.0 1.7 %collective-permute-start.2 = (f32[160,128]{1,0:T(8,128)S(1)}, f32[160,128]{1,0:T(8,128)S(1)}, u32[]{:S(2)}, u32[]{:S(2)}) collective-permute-start(f32[160,128]{1,0:T(8,128)S(1)} %bitcast_add_fusion.1), channel_id=1, source_target_pairs={{0,16},{4,20},{8,24},{12,28},{16,0},{20,4},{24,8},{28,12},{1,17},{... | collective-permute-start | bytes 245768 | tf_op jit(solution)/shard_map/ppermute | solution.py:283
  17.7 0.0 copy-done.5
  17.7 0.0 copy-done.6
  17.8 0.0 copy-done.7
  17.8 1.0 %copy-done.14 = f32[640,128]{1,0:T(8,128)S(1)} copy-done((f32[640,128]{1,0:T(8,128)S(1)}, f32[640,128]{1,0:T(8,128)}, u32[]{:S(2)}) %copy-start.14) | copy-done | bytes 327704
  18.8 1.3 %copy-done.16 = f32[2,1376,128]{2,1,0:T(8,128)S(1)} copy-done((f32[2,1376,128]{2,1,0:T(8,128)S(1)}, f32[2,1376,128]{2,1,0:T(8,128)}, u32[]{:S(2)}) %copy-start.16) | copy-done | bytes 1409048
  20.1 4.6 %first_half.2 = (f32[1376,128]{1,0:T(8,128)S(1)}, f32[1376,128]{1,0:T(8,128)S(1)}) custom-call(s32[4]{0:T(128)S(1)} %copy-done.5, f32[2,1376,128]{2,1,0:T(8,128)S(1)} %copy-done.16, f32[640,128]{1,0:T(8,128)S(1)} %copy-done.14, bf16[256,256]{1,0:T(8,128)(2,1)S(1)} %copy-done.8, bf16[256,256]{1,0:T(8,128)(2,1)S(1)} %copy-done.7, ...), custom_call_target="tpu_custom_call" | custom-call | flops 3000000000 | bytes 3000000 | tf_op jit(solution)/shard_map/first_half/pallas_call | solution.py:278
  24.7 0.0 collective-permute-done.2
  24.7 1.6 %collective-permute-start.3 = (f32[160,128]{1,0:T(8,128)S(1)}, f32[160,128]{1,0:T(8,128)S(1)}, u32[]{:S(2)}, u32[]{:S(2)}) collective-permute-start(f32[160,128]{1,0:T(8,128)S(1)} %add.50), channel_id=1, source_target_pairs={{0,1},{1,0},{2,3},{3,2},{4,5},{5,4},{6,7},{7,6},{8,9},{9,8},{10,11... | collective-permute-start | bytes 245768 | tf_op jit(solution)/shard_map/ppermute | solution.py:283
  26.4 4.3 %second_half.2.first = f32[640,128]{1,0:T(8,128)S(1)} custom-call(s32[4]{0:T(128)S(1)} %copy-done.5, f32[2,1376,128]{2,1,0:T(8,128)S(1)} %copy-done.16, f32[640,128]{1,0:T(8,128)S(1)} %copy-done.14, bf16[256,256]{1,0:T(8,128)(2,1)S(1)} %copy-done.8, bf16[256,256]{1,0:T(8,128)(2,1)S(1)} %copy-done.7, bf16[48,144]{1,0:T(8,128)(2,1)S(1)} %copy-done.10, ...), custom_call_target="tpu_custom_call" | custom-call | flops 3000000000 | bytes 3000000 | tf_op jit(solution)/shard_map/second_half/pallas_call | solution.py:278
  30.7 1.2 %reshape.12.density = f32[1,81000]{1,0:T(1,128)S(1)} reshape(f32[81000]{0:T(1024)} %param.16) | data formatting | bytes 648000 | tf_op jit(solution)/shard_map/reshape | solution.py:340
  31.9 0.0 collective-permute-done.3
  31.9 2.7 %collective-permute-start.4 = (f32[160,128]{1,0:T(8,128)S(1)}, f32[160,128]{1,0:T(8,128)S(1)}, u32[]{:S(2)}, u32[]{:S(2)}) collective-permute-start(f32[160,128]{1,0:T(8,128)S(1)} %add.51), channel_id=1, source_target_pairs={{0,2},{1,3},{2,0},{3,1},{4,6},{5,7},{6,4},{7,5},{8,10},{9,11},{10,... | collective-permute-start | bytes 245768 | tf_op jit(solution)/shard_map/ppermute | solution.py:283
  34.6 0.2 coefficient.1
  34.8 3.3 %collective-permute-done.4 = f32[160,128]{1,0:T(8,128)S(1)} collective-permute-done((f32[160,128]{1,0:T(8,128)S(1)}, f32[160,128]{1,0:T(8,128)S(1)}, u32[]{:S(2)}, u32[]{:S(2)}) %collective-permute-start.4) | collective-permute-done | bytes 81952 | tf_op jit(solution)/shard_map/ppermute | solution.py:283
  38.1 1.5 %collective-permute-start.5 = (f32[160,128]{1,0:T(8,128)S(1)}, f32[160,128]{1,0:T(8,128)S(1)}, u32[]{:S(2)}, u32[]{:S(2)}) collective-permute-start(f32[160,128]{1,0:T(8,128)S(1)} %add.52), channel_id=1, source_target_pairs={{0,8},{4,12},{8,0},{12,4},{16,24},{20,28},{24,16},{28,20},{1,9},{5... | collective-permute-start | bytes 245768 | tf_op jit(solution)/shard_map/ppermute | solution.py:283
  39.6 0.0 collective-permute-done.7.response
  39.6 4.6 %first_half.3 = (f32[1376,128]{1,0:T(8,128)S(1)}, f32[1376,128]{1,0:T(8,128)S(1)}) custom-call(s32[4]{0:T(128)S(1)} %copy-done.5, f32[2,1376,128]{2,1,0:T(8,128)S(1)} %copy-done.17, f32[640,128]{1,0:T(8,128)S(1)} %collective-permute-done.7.response, bf16[256,256]{1,0:T(8,128)(2,1)S(1)} %copy-done.8, bf16[256,256]{1,0:T(8,128)(2,1)S(1)} %copy-done.7, ...), custom_call_target="tpu_custom_call" | custom-call | flops 3000000000 | bytes 3000000 | tf_op jit(solution)/shard_map/first_half/pallas_call | solution.py:278
  44.2 0.0 collective-permute-done.5
  44.3 0.1 collective-permute-start.6
  44.4 4.3 %second_half.3 = f32[640,128]{1,0:T(8,128)S(1)} custom-call(s32[4]{0:T(128)S(1)} %copy-done.5, f32[2,1376,128]{2,1,0:T(8,128)S(1)} %copy-done.17, f32[640,128]{1,0:T(8,128)S(1)} %collective-permute-done.7.response, bf16[256,256]{1,0:T(8,128)(2,1)S(1)} %copy-done.8, bf16[256,256]{1,0:T(8,128)(2,1)S(1)} %copy-done.7, bf16[48,144]{1,0:T(8,128)(2,1)S(1)} %copy-done.10, ...), custom_call_target="tpu_custom_call" | custom-call | flops 3000000000 | bytes 3000000 | tf_op jit(solution)/shard_map/second_half/pallas_call | solution.py:278
  48.7 0.5 collective-permute-start.8
  49.2 0.0 collective-permute-done.6
  49.3 6.8 %collective-permute-done.8.second = f32[640,128]{1,0:T(8,128)S(1)} collective-permute-done((f32[640,128]{1,0:T(8,128)S(1)}, f32[640,128]{1,0:T(8,128)S(1)}, u32[]{:S(2)}, u32[]{:S(2)}) %collective-permute-start.8) | collective-permute-done | bytes 327712 | tf_op jit(solution)/shard_map/ppermute | solution.py:343
  56.2 0.8 %finish.1 = f32[1,81000]{1,0:T(1,128)} custom-call(f32[640,128]{1,0:T(8,128)S(1)} %coefficient.1, f32[640,128]{1,0:T(8,128)S(1)} %pad_maximum_fusion.density, f32[640,128]{1,0:T(8,128)S(1)} %second_half.2.first, f32[640,128]{1,0:T(8,128)S(1)} %collective-permute-done.8.second), custom_call_target="tpu_custom_call" | custom-call | flops 1000000000 | bytes 1000000 | tf_op jit(solution)/shard_map/finish/pallas_call | solution.py:278
  (28 shorter events, 0.2 us)
Async XLA Ops:
  0.0 1.3 %copy-start = (f32[4,81000]{1,0:T(4,128)S(1)}, f32[4,81000]{1,0:T(4,128)}, u32[]{:S(2)}) copy-start(f32[4,81000]{1,0:T(4,128)} %ground.3) | copy-start | bytes 3888004
  1.3 1.0 %copy-start.2 = (f32[1,81000]{1,0:T(1,128)S(1)}, f32[1,81000]{1,0:T(1,128)}, u32[]{:S(2)}) copy-start(f32[1,81000]{1,0:T(1,128)} %response.1) | copy-start | bytes 972004
  2.3 0.7 %copy-start.3 = (s32[1,2]{1,0:T(1,128)S(1)}, s32[1,2]{1,0:T(1,128)}, u32[]{:S(2)}) copy-start(s32[1,2]{1,0:T(1,128)} %offsets.1) | copy-start | bytes 28
  2.9 0.7 %copy-start.4 = (s32[4]{0:T(128)S(1)}, s32[4]{0:T(128)}, u32[]{:S(2)}) copy-start(s32[4]{0:T(128)} %signs.9) | copy-start | bytes 52
  3.6 6.3 %copy-start.1 = (f32[4,81000]{1,0:T(4,128)S(1)}, f32[4,81000]{1,0:T(4,128)}, u32[]{:S(2)}) copy-start(f32[4,81000]{1,0:T(4,128)} %ground.3) | copy-start | bytes 3888004
  4.6 4.2 %copy-start.13 = (f32[640,128]{1,0:T(8,128)}, f32[640,128]{1,0:T(8,128)S(1)}, u32[]{:S(2)}) copy-start(f32[640,128]{1,0:T(8,128)S(1)} %get-tuple-element.15.response) | copy-start | bytes 983044
  4.6 4.1 %collective-permute-start = (f32[320,128]{1,0:T(8,128)S(1)}, f32[320,128]{1,0:T(8,128)S(1)}, u32[]{:S(2)}, u32[]{:S(2)}) collective-permute-start(f32[320,128]{1,0:T(8,128)S(1)} %dynamic-slice_bitcast_fusion), channel_id=1, source_target_pairs={{0,4},{4,0},{8,12},{12,8},{16,20},{20,16},{24,28},{28,24},{1,5},{5... | collective-permute-start | bytes 491528 | tf_op jit(solution)/shard_map/ppermute | solution.py:283
  5.2 34.5 %collective-permute-start.7 = (f32[640,128]{1,0:T(8,128)S(1)}, f32[640,128]{1,0:T(8,128)S(1)}, u32[]{:S(2)}, u32[]{:S(2)}) collective-permute-start(f32[640,128]{1,0:T(8,128)S(1)} %get-tuple-element.18), channel_id=1, source_target_pairs={{4,0},{8,4},{12,8},{16,12},{20,16},{24,20},{28,24},{0,28},{5,1},{9... | collective-permute-start | bytes 983048 | tf_op jit(solution)/shard_map/ppermute | solution.py:333
  8.8 0.7 %copy-start.18 = (f32[320,128]{1,0:T(8,128)}, f32[320,128]{1,0:T(8,128)S(1)}, u32[]{:S(2)}) copy-start(f32[320,128]{1,0:T(8,128)S(1)} %bitcast_add_fusion) | copy-start | bytes 491524
  9.4 8.3 %copy-start.5 = (s32[4]{0:T(128)S(1)}, s32[4]{0:T(128)}, u32[]{:S(2)}) copy-start(s32[4]{0:T(128)} %signs.9) | copy-start | bytes 52
  9.4 8.3 %copy-start.6 = (f32[1536,128]{1,0:T(8,128)S(1)}, f32[1536,128]{1,0:T(8,128)}, u32[]{:S(2)}) copy-start(f32[1536,128]{1,0:T(8,128)} %constant.90.clone.refs_6_) | copy-start | bytes 2359300
  9.4 8.3 %copy-start.7 = (bf16[256,256]{1,0:T(8,128)(2,1)S(1)}, bf16[256,256]{1,0:T(8,128)(2,1)}, u32[]{:S(2)}) copy-start(bf16[256,256]{1,0:T(8,128)(2,1)} %constant.85.clone.refs_1_) | copy-start | bytes 393220
  9.4 8.3 %copy-start.8 = (bf16[256,256]{1,0:T(8,128)(2,1)S(1)}, bf16[256,256]{1,0:T(8,128)(2,1)}, u32[]{:S(2)}) copy-start(bf16[256,256]{1,0:T(8,128)(2,1)} %constant.84.clone.refs_0_) | copy-start | bytes 393220
  9.4 8.3 %copy-start.9 = (bf16[48,144]{1,0:T(8,128)(2,1)S(1)}, bf16[48,144]{1,0:T(8,128)(2,1)}, u32[]{:S(2)}) copy-start(bf16[48,144]{1,0:T(8,128)(2,1)} %constant.87.clone.refs_3_) | copy-start | bytes 41476
  9.5 8.3 %copy-start.10 = (bf16[48,144]{1,0:T(8,128)(2,1)S(1)}, bf16[48,144]{1,0:T(8,128)(2,1)}, u32[]{:S(2)}) copy-start(bf16[48,144]{1,0:T(8,128)(2,1)} %constant.86.clone.refs_2_) | copy-start | bytes 41476
  9.5 8.3 %copy-start.11 = (bf16[32,96]{1,0:T(8,128)(2,1)S(1)}, bf16[32,96]{1,0:T(8,128)(2,1)}, u32[]{:S(2)}) copy-start(bf16[32,96]{1,0:T(8,128)(2,1)} %constant.89.clone.refs_5_) | copy-start | bytes 18436
  9.5 8.3 %copy-start.12 = (bf16[32,96]{1,0:T(8,128)(2,1)S(1)}, bf16[32,96]{1,0:T(8,128)(2,1)}, u32[]{:S(2)}) copy-start(bf16[32,96]{1,0:T(8,128)(2,1)} %constant.88.clone.refs_4_) | copy-start | bytes 18436
  9.5 5.6 %collective-permute-start.1 = (f32[160,128]{1,0:T(8,128)S(1)}, f32[160,128]{1,0:T(8,128)}, u32[]{:S(2)}, u32[]{:S(2)}) collective-permute-start(f32[160,128]{1,0:T(8,128)S(1)} %dynamic-slice_bitcast_fusion.1), channel_id=1, source_target_pairs={{0,8},{4,12},{8,0},{12,4},{16,24},{20,28},{24,16},{28,20},{1,9},{5... | collective-permute-start | bytes 245768 | tf_op jit(solution)/shard_map/ppermute | solution.py:283
  12.7 1.1 %copy-start.15 = (f32[2,1376,128]{2,1,0:T(8,128)}, f32[2,1376,128]{2,1,0:T(8,128)S(1)}, u32[]{:S(2)}) copy-start(f32[2,1376,128]{2,1,0:T(8,128)S(1)} %lines.1) | copy-start | bytes 4227076
  16.0 8.7 %collective-permute-start.2 = (f32[160,128]{1,0:T(8,128)S(1)}, f32[160,128]{1,0:T(8,128)S(1)}, u32[]{:S(2)}, u32[]{:S(2)}) collective-permute-start(f32[160,128]{1,0:T(8,128)S(1)} %bitcast_add_fusion.1), channel_id=1, source_target_pairs={{0,16},{4,20},{8,24},{12,28},{16,0},{20,4},{24,8},{28,12},{1,17},{... | collective-permute-start | bytes 245768 | tf_op jit(solution)/shard_map/ppermute | solution.py:283
  17.8 1.0 %copy-start.14 = (f32[640,128]{1,0:T(8,128)S(1)}, f32[640,128]{1,0:T(8,128)}, u32[]{:S(2)}) copy-start(f32[640,128]{1,0:T(8,128)} %copy-done.13) | copy-start | bytes 983044
  18.8 1.4 %copy-start.16 = (f32[2,1376,128]{2,1,0:T(8,128)S(1)}, f32[2,1376,128]{2,1,0:T(8,128)}, u32[]{:S(2)}) copy-start(f32[2,1376,128]{2,1,0:T(8,128)} %copy-done.15) | copy-start | bytes 4227076
  24.7 7.2 %collective-permute-start.3 = (f32[160,128]{1,0:T(8,128)S(1)}, f32[160,128]{1,0:T(8,128)S(1)}, u32[]{:S(2)}, u32[]{:S(2)}) collective-permute-start(f32[160,128]{1,0:T(8,128)S(1)} %add.50), channel_id=1, source_target_pairs={{0,1},{1,0},{2,3},{3,2},{4,5},{5,4},{6,7},{7,6},{8,9},{9,8},{10,11... | collective-permute-start | bytes 245768 | tf_op jit(solution)/shard_map/ppermute | solution.py:283
  31.9 6.2 %collective-permute-start.4 = (f32[160,128]{1,0:T(8,128)S(1)}, f32[160,128]{1,0:T(8,128)S(1)}, u32[]{:S(2)}, u32[]{:S(2)}) collective-permute-start(f32[160,128]{1,0:T(8,128)S(1)} %add.51), channel_id=1, source_target_pairs={{0,2},{1,3},{2,0},{3,1},{4,6},{5,7},{6,4},{7,5},{8,10},{9,11},{10,... | collective-permute-start | bytes 245768 | tf_op jit(solution)/shard_map/ppermute | solution.py:283
  34.6 5.1 %copy-start.17 = (f32[2,1376,128]{2,1,0:T(8,128)S(1)}, f32[2,1376,128]{2,1,0:T(8,128)}, u32[]{:S(2)}) copy-start(f32[2,1376,128]{2,1,0:T(8,128)} %copy-done.15) | copy-start | bytes 4227076
  38.1 6.1 %collective-permute-start.5 = (f32[160,128]{1,0:T(8,128)S(1)}, f32[160,128]{1,0:T(8,128)S(1)}, u32[]{:S(2)}, u32[]{:S(2)}) collective-permute-start(f32[160,128]{1,0:T(8,128)S(1)} %add.52), channel_id=1, source_target_pairs={{0,8},{4,12},{8,0},{12,4},{16,24},{20,28},{24,16},{28,20},{1,9},{5... | collective-permute-start | bytes 245768 | tf_op jit(solution)/shard_map/ppermute | solution.py:283
  44.3 5.0 %collective-permute-start.6 = (f32[320,128]{1,0:T(8,128)S(1)}, f32[320,128]{1,0:T(8,128)S(1)}, u32[]{:S(2)}, u32[]{:S(2)}) collective-permute-start(f32[320,128]{1,0:T(8,128)S(1)} %pad_maximum_fusion.1), channel_id=1, source_target_pairs={{0,4},{4,0},{8,12},{12,8},{16,20},{20,16},{24,28},{28,24},{1,5},{5... | collective-permute-start | bytes 491528 | tf_op jit(solution)/shard_map/ppermute | solution.py:283
  48.7 7.5 %collective-permute-start.8 = (f32[640,128]{1,0:T(8,128)S(1)}, f32[640,128]{1,0:T(8,128)S(1)}, u32[]{:S(2)}, u32[]{:S(2)}) collective-permute-start(f32[640,128]{1,0:T(8,128)S(1)} %second_half.3), channel_id=1, source_target_pairs={{0,4},{4,8},{8,12},{12,16},{16,20},{20,24},{24,28},{28,0},{1,5},{5... | collective-permute-start | bytes 983048 | tf_op jit(solution)/shard_map/ppermute | solution.py:343

commit v2 on v1

--- a/solution.py
+++ b/solution.py
@@ -25,6 +25,8 @@
 XP = 32
 YP = 48
 ZP = LANES // 2
+XS = XP + 1
+YS = YP + 1
 LINES = math.lcm(NZ, LANES) // NZ
 CHUNKS = math.lcm(NZ, LANES) // LANES
 PERIODS = -(-NX * NY // LINES)
@@ -114,103 +116,124 @@
     return jnp.where(lane_ids(PERIODS) < place + LANES - start, first, second)
 
 
-def to_lines(left, right, lines):
+def to_lines(left, right, lines, pitched):
     ids = lane_ids(PERIODS)
     for line in range(LINES):
         low, high = line_of(left, line, 0), line_of(right, line, ZP)
         both = jnp.where(ids < NZ, low, jnp.where((ids >= ZP) & (ids < ZP + NZ), high, 0.0))
-        lines[pl.ds(line, PERIODS, stride=LINES), :] = both
-
-
-def to_flat(lines, flat):
+        pitched[pl.ds(line, PERIODS, stride=LINES + 1), :] = both
+    for period in range(PERIODS):
+        lines[pl.ds(period * LINES, LINES), :] = pitched[pl.ds(period * (LINES + 1), LINES), :]
+
+
+def to_flat(lines, flat, pitched):
     ids = lane_ids(PERIODS)
+    for period in range(PERIODS):
+        pitched[pl.ds(period * (LINES + 1), LINES), :] = lines[pl.ds(period * LINES, LINES), :]
     for chunk in range(CHUNKS):
         low = chunk * LANES
         merged = None
         for line in range(low // NZ, -(-(low + LANES) // NZ)):
-            value = turned(lines[pl.ds(line, PERIODS, stride=LINES), :], NZ * line - low)
+            value = turned(pitched[pl.ds(line, PERIODS, stride=LINES + 1), :], NZ * line - low)
             merged = value if merged is None else jnp.where(ids >= NZ * line - low, value, merged)
         flat[pl.ds(chunk, PERIODS, stride=CHUNKS), :] = merged
 
 
-def fill_flat(row, flat):
-    flat[pl.ds(0, WHOLE), :] = row.at[:, pl.ds(0, WHOLE * LANES)].reshape(WHOLE, LANES)[...]
+def body_copy(row, flat, sem):
+    target = flat.at[pl.ds(0, WHOLE), :].reshape(1, WHOLE * LANES)
+    return pltpu.make_async_copy(row.at[:, pl.ds(0, WHOLE * LANES)], target, sem)
+
+
+def fill_tail(tail, flat):
     flat[pl.ds(WHOLE, flat.shape[0] - WHOLE), :] = jnp.zeros((flat.shape[0] - WHOLE, LANES), F32)
-    flat[pl.ds(WHOLE, 1), pl.ds(0, TAIL)] = row[:, pl.ds(WHOLE * LANES, TAIL)]
+    flat[pl.ds(WHOLE, 1), pl.ds(0, TAIL)] = tail
 
 
 def grouped(count, group, body):
     lax.fori_loop(0, count // group, lambda step, carry: (body(step * group), carry)[1], 0)
 
 
-def prelude_kernel(position, signs, offsets, ground, response, term, own, kept, sent, row_g, row_r, sems):
+def prelude_kernel(position, signs, offsets, ground, response, term, own, kept, weights, rows, sign, offset, sems):
     place = position[0]
+    spot = pl.ds(place, 1)
     copies = [
-        pltpu.make_async_copy(ground.at[pl.ds(place, 1), :], row_g, sems.at[0]),
-        pltpu.make_async_copy(response, row_r, sems.at[1]),
+        pltpu.make_async_copy(signs, sign, sems.at[0]),
+        pltpu.make_async_copy(offsets, offset, sems.at[1]),
+        body_copy(response, kept, sems.at[2]),
+        pltpu.make_async_copy(response, rows.at[0], sems.at[3]),
+        body_copy(ground.at[spot, :], own, sems.at[4]),
+        pltpu.make_async_copy(ground.at[spot, :], rows.at[1], sems.at[5]),
     ]
     for copy in copies:
         copy.start()
     for copy in copies:
         copy.wait()
-    fill_flat(row_g, own)
-    fill_flat(row_r, kept)
-    term[...] = signs[place].astype(F32) * own[...] * kept[...]
-    sent[...] = kept[...]
-    last = pl.ds(SENT_ROWS - 1, 1)
-    kept[last, :] = jnp.full((1, LANES), offsets[0, 0].astype(F32))
-    sent[last, :] = jnp.full((1, LANES), offsets[0, 1].astype(F32))
-
-
-def lines_kernel(ground, lines, rows, flats, sems):
-    copies = [
-        pltpu.make_async_copy(ground.at[pl.ds(j, 1), :], rows.at[j], sems.at[j]) for j in range(4)
-    ]
+    last = pl.ds(WHOLE * LANES, TAIL)
+    fill_tail(rows[0, :, last], kept)
+    fill_tail(rows[1, :, last], own)
+    term[...] = sign[place].astype(F32) * own[...] * kept[...]
+    for step in range(2):
+        kept[pl.ds(SENT_ROWS - 2 + step, 1), :] = jnp.full((1, LANES), offset[0, step].astype(F32))
+    ids = lane_ids(1)
+    for half in range(2):
+        pair = jnp.where(ids < ZP, sign[2 * half].astype(F32), sign[2 * half + 1].astype(F32))
+        weights[pl.ds(half, 1), :] = pair
+
+
+def lines_kernel(ground, low_lines, high_lines, flats, pitched, sems):
+    copies = [body_copy(ground.at[pl.ds(j, 1), :], flats.at[j], sems.at[j]) for j in range(4)]
     for copy in copies:
         copy.start()
     for j in range(4):
         copies[j].wait()
-        fill_flat(rows.at[j], flats.at[j])
-    for half in range(2):
-        to_lines(flats.at[2 * half], flats.at[2 * half + 1], lines.at[half])
-
-
-def coefficient_kernel(density, own, coefficient, flat):
-    fill_flat(density, flat)
-    spots = lax.broadcasted_iota(jnp.int32, (SENT_ROWS, LANES), 0) * LANES + lane_ids(SENT_ROWS)
-    values = jnp.where(spots < POINTS, flat[...], 1.0)
-    coefficient[...] = -XC_COEF * jnp.exp(jnp.log(values) * (-2.0 / 3.0)) * own[...]
-
-
-def solve_half(half, signs, lines, values, offset, tables, kernel, waves, turned_waves, total, prior):
+        fill_tail(ground[pl.ds(j, 1), pl.ds(WHOLE * LANES, TAIL)], flats.at[j])
+    to_lines(flats.at[0], flats.at[1], low_lines, pitched)
+    to_lines(flats.at[2], flats.at[3], high_lines, pitched)
+
+
+def coefficient_kernel(density, own, coefficient, values, sem):
+    copy = pltpu.make_async_copy(density, values, sem)
+    copy.start()
+    copy.wait()
+    block = 8 * LANES
+    for start in range(0, POINTS, block):
+        size = min(block, POINTS - start)
+        shape = (8, LANES) if size == block else (1, size)
+        value = values[pl.ds(start, size)].reshape(shape)
+        value = -XC_COEF * jnp.exp(jnp.log(value) * (-2.0 / 3.0))
+        spot = (pl.ds(start // LANES, shape[0]), pl.ds(0, shape[1]))
+        coefficient[spot] = value * own[spot]
+
+
+def solve_half(half, step, weights, lines, values, response, tables, kernel_copy, scratch, total, prior):
+    kernel, waves, turned_waves = scratch
     z_table, z_back, y_table, y_back, x_table, x_back = (table[...] for table in tables)
     group = 15
     for x in range(NX, XP):
-        waves[pl.ds(x, YP, stride=XP), :] = jnp.zeros((YP, LANES), F32)
+        waves[pl.ds(x, YP, stride=XS), :] = jnp.zeros((YP, LANES), F32)
     for y in range(NY, YP):
-        turned_waves[pl.ds(y, XP, stride=YP), :] = jnp.zeros((XP, LANES), F32)
+        turned_waves[pl.ds(y, XP, stride=YS), :] = jnp.zeros((XP, LANES), F32)
 
     def forward(x):
         spots = [pl.ds((x + u) * NY, YP) for u in range(group)]
         value = lane_product(jnp.concatenate([lines[spot, :] * values[spot, :] for spot in spots], 0), z_table)
         value = row_product(y_table, jnp.concatenate([value[u * YP : (u + 1) * YP] for u in range(group)], 1))
         for u in range(group):
-            waves[pl.ds(x + u, YP, stride=XP), :] = value[:, u * LANES : (u + 1) * LANES]
+            waves[pl.ds(x + u, YP, stride=XS), :] = value[:, u * LANES : (u + 1) * LANES]
 
     def middle(y):
         spots = [pl.ds(pl.multiple_of((y + u) * XP, XP), XP) for u in range(group)]
-        value = row_product(x_table, jnp.concatenate([waves[spot, :] for spot in spots], 1))
+        value = row_product(x_table, jnp.concatenate([waves[pl.ds((y + u) * XS, XP), :] for u in range(group)], 1))
         value = row_product(x_back, value * jnp.concatenate([kernel[spot, :] for spot in spots], 1))
         for u in range(group):
-            turned_waves[pl.ds(y + u, XP, stride=YP), :] = value[:, u * LANES : (u + 1) * LANES]
-
-    ids = lane_ids(1)
-    orbital = 2 * half + (ids >= ZP).astype(jnp.int32)
-    sign = jnp.where(ids < ZP, signs[2 * half].astype(F32), signs[2 * half + 1].astype(F32))
-    factor = jnp.where(orbital.astype(F32) >= offset, sign, 0.0)
+            turned_waves[pl.ds(y + u, XP, stride=YS), :] = value[:, u * LANES : (u + 1) * LANES]
+
+    orbital = 2 * half + (lane_ids(1) >= ZP).astype(jnp.int32)
+    offset = response[pl.ds(SENT_ROWS - 2 + step, 1), :]
+    factor = jnp.where(orbital.astype(F32) >= offset, weights[pl.ds(half, 1), :], 0.0)
 
     def backward(x):
-        spots = [pl.ds(pl.multiple_of((x + u) * YP, YP), YP) for u in range(group)]
+        spots = [pl.ds((x + u) * YS, YP) for u in range(group)]
         value = row_product(y_back, jnp.concatenate([turned_waves[spot, :] for spot in spots], 1))
         value = jnp.concatenate([value[:, u * LANES : (u + 1) * LANES] for u in range(group)], 0)
         value = lane_product(value, z_back)
@@ -223,24 +246,27 @@
             total[spot, :] = part
 
     grouped(NX, group, forward)
+    kernel_copy.wait()
     grouped(NY, group, middle)
     grouped(NX, group, backward)
 
 
-def first_half_kernel(signs, lines, response, *refs):
-    tables, (kernel, values, partial, flat, waves, turned_waves) = refs[:6], refs[6:]
+def first_half_kernel(step, weights, lines, response, *refs):
+    tables, (kernel, values, partial, flat, pitched, sem, *scratch) = refs[:6], refs[6:]
+    kernel_copy = pltpu.make_async_copy(kernel, scratch[0], sem)
+    kernel_copy.start()
     flat[pl.ds(0, WHOLE + 1), :] = response[pl.ds(0, WHOLE + 1), :]
     flat[pl.ds(WHOLE + 1, FLAT_ROWS - WHOLE - 1), :] = jnp.zeros((FLAT_ROWS - WHOLE - 1, LANES), F32)
-    to_lines(flat, flat, values)
-    offset = response[pl.ds(SENT_ROWS - 1, 1), :]
-    solve_half(0, signs, lines.at[0], values, offset, tables, kernel, waves, turned_waves, partial, None)
-
-
-def second_half_kernel(signs, lines, response, *refs):
-    tables, (kernel, values, partial, exchange, flat, waves, turned_waves, total) = refs[:6], refs[6:]
-    offset = response[pl.ds(SENT_ROWS - 1, 1), :]
-    solve_half(1, signs, lines.at[1], values, offset, tables, kernel, waves, turned_waves, total, partial)
-    to_flat(total, flat)
+    to_lines(flat, flat, values, pitched)
+    solve_half(0, step, weights, lines, values, response, tables, kernel_copy, scratch, partial, None)
+
+
+def second_half_kernel(step, weights, lines, response, *refs):
+    tables, (kernel, values, partial, exchange, flat, pitched, sem, *scratch, total) = refs[:6], refs[6:]
+    kernel_copy = pltpu.make_async_copy(kernel, scratch[0], sem)
+    kernel_copy.start()
+    solve_half(1, step, weights, lines, values, response, tables, kernel_copy, scratch, total, partial)
+    to_flat(total, flat, pitched)
     exchange[...] = flat[pl.ds(0, SENT_ROWS), :]
 
 
@@ -252,15 +278,16 @@
 
 SCALARS = pl.BlockSpec(memory_space=pltpu.SMEM)
 VECTORS = pl.BlockSpec(memory_space=pltpu.VMEM)
-ANYWHERE = pl.BlockSpec(memory_space=pl.ANY)
+FAR = pl.BlockSpec(memory_space=pltpu.HBM)
 
 
 def near(shape):
     return pltpu.VMEM(shape, F32) if shape != (1, POINTS) else jax.ShapeDtypeStruct(shape, F32)
 
 
-def held(values):
-    return pltpu.with_memory_space_constraint(values, pltpu.VMEM)
+def placed(values, spec):
+    space = {id(FAR): pltpu.HBM, id(VECTORS): pltpu.VMEM}.get(id(spec))
+    return values if space is None else pltpu.with_memory_space_constraint(values, space)
 
 
 def call(body, name, specs, shapes, scratch, microseconds, outs=None):
@@ -275,7 +302,7 @@
         cost_estimate=cost,
         compiler_params=pltpu.CompilerParams(vmem_limit_bytes=12 * 2**20),
     )
-    return lambda *values: kernel(*(held(v) if spec is VECTORS else v for spec, v in zip(specs, values)))
+    return lambda *values: kernel(*(placed(v, spec) for spec, v in zip(specs, values)))
 
 
 def swap(values, axis, distance):
@@ -302,15 +329,21 @@
     return term
 
 
-def exchange_of(signs, lines, response, tables):
-    shared = (signs, lines, response, *tables)
-    flat, line = pltpu.VMEM((FLAT_ROWS, LANES), F32), pltpu.VMEM((LINE_ROWS, LANES), F32)
-    waves = pltpu.VMEM((XP * YP, LANES), F32)
-    specs = [SCALARS] + [VECTORS] * (2 + len(tables))
-    values, partial = call(first_half_kernel, "first_half", specs, [(LINE_ROWS, LANES)] * 2, [flat, waves, waves], 3)(*shared)
-    return call(
-        second_half_kernel, "second_half", specs + [VECTORS] * 2, [(SENT_ROWS, LANES)], [flat, waves, waves, line], 3
-    )(*shared, values, partial)[0]
+def half_call(body, name, step, shapes, extra, values):
+    flat, pitched = pltpu.VMEM((FLAT_ROWS, LANES), F32), pltpu.VMEM((PERIODS * (LINES + 1), LANES), F32)
+    scratch = [flat, pitched, pltpu.SemaphoreType.DMA, pltpu.VMEM((YP * XP, LANES), F32)]
+    scratch += [pltpu.VMEM((YP * XS, LANES), F32), pltpu.VMEM((XP * YS, LANES), F32)] + extra
+    specs = [VECTORS] * 9 + [FAR] + [VECTORS] * (len(values) - 10)
+    return call(functools.partial(body, step), name, specs, shapes, scratch, 3)(*values)
+
+
+def first_half(step, *shared):
+    return half_call(first_half_kernel, "first_half", step, [(LINE_ROWS, LANES)] * 2, [], shared)
+
+
+def second_half(step, *shared):
+    line = pltpu.VMEM((LINE_ROWS, LANES), F32)
+    return half_call(second_half_kernel, "second_half", step, [(SENT_ROWS, LANES)], [line], shared)[0]
 
 
 def per_device(ground_orbitals, occupation_signs, response_orbitals, window_offsets, ground_density):
@@ -324,24 +357,30 @@
     )
     tables = tuple(jnp.asarray(table) for table in tables)
     flat = (SENT_ROWS, LANES)
-    row = pltpu.VMEM((1, POINTS), F32)
     position = lax.axis_index("grid").reshape(1)
-    term, own, kept, sent = call(
-        prelude_kernel, "prelude", [SCALARS] * 3 + [ANYWHERE] * 2, [flat] * 4, [row, row, pltpu.SemaphoreType.DMA((2,))], 1
+    scratch = [pltpu.VMEM((2, 1, POINTS), F32), pltpu.SMEM((4,), jnp.int32), pltpu.SMEM((1, 2), jnp.int32)]
+    term, own, kept, weights = call(
+        prelude_kernel, "prelude", [SCALARS] + [FAR] * 4, [flat] * 3 + [(8, LANES)],
+        scratch + [pltpu.SemaphoreType.DMA((6,))], 1,
     )(position, occupation_signs, window_offsets, ground_orbitals, response_orbitals)
     count = lax.axis_size("orb")
-    visiting = lax.ppermute(sent, "orb", [((i + 1) % count, i) for i in range(count)])
+    visiting = lax.ppermute(kept, "orb", [((i + 1) % count, i) for i in range(count)])
     density = summed_over_devices(term)
-    lines = call(
-        lines_kernel, "lines", [ANYWHERE], [(2, LINE_ROWS, LANES)],
-        [pltpu.VMEM((4, 1, POINTS), F32), pltpu.VMEM((4, FLAT_ROWS, LANES), F32), pltpu.SemaphoreType.DMA((4,))], 2,
-    )(ground_orbitals)[0]
-    coefficient = call(coefficient_kernel, "coefficient", [VECTORS] * 2, [flat], [pltpu.VMEM(flat, F32)], 1)(
-        ground_density.reshape(1, POINTS), own
-    )[0]
-    away = exchange_of(occupation_signs, lines, visiting, tables)
+    low_lines, high_lines = call(
+        lines_kernel, "lines", [VECTORS], [(LINE_ROWS, LANES)] * 2,
+        [pltpu.VMEM((4, FLAT_ROWS, LANES), F32), pltpu.VMEM((PERIODS * (LINES + 1), LANES), F32),
+         pltpu.SemaphoreType.DMA((4,))], 2,
+    )(ground_orbitals)
+    coefficient = call(
+        coefficient_kernel, "coefficient", [FAR, VECTORS], [flat],
+        [pltpu.VMEM((POINTS,), F32), pltpu.SemaphoreType.DMA], 1,
+    )(ground_density, own)[0]
+    values, partial = first_half(0, weights, low_lines, kept, *tables)
+    away_values, away_partial = first_half(1, weights, low_lines, visiting, *tables)
+    away = second_half(1, weights, high_lines, visiting, *tables, away_values, away_partial)
     second = lax.ppermute(away, "orb", [(i, (i + 1) % count) for i in range(count)])
-    first = exchange_of(occupation_signs, lines, kept, tables)
+    values, away = lax.optimization_barrier((values, away))
+    first = second_half(0, weights, high_lines, kept, *tables, values, partial)
     return call(finish_kernel, "finish", [VECTORS] * 4, [(1, POINTS)], [], 1)(coefficient, density, first, second)[0]
 
 

time: 57.3 us -> 45.5 us (0.79)
  local copies, waits for them, and re-layouts: 8.92 us -> 3.54 us
  waiting for transfers between devices: 11.5 us -> 7.9 us
  Pallas kernels: 22.6 us -> 20.1 us
    unnamed x38 -> x24, local copies, waits for them, and re-layouts: 7.68 us -> 2.87 us
    ppermute x1, waiting for transfers between devices: 6.84 us -> 2.7 us  [per_device(): lax.ppermute(away, 'orb', [(i, (i + 1) % count) for i in range(count)])]
    pallas_call x8, Pallas kernels: 22.6 us -> 20.1 us  [call(): kernel(*(placed(v, spec) for spec, v in zip(specs, values)))]
    reshape x1 -> x0, local copies, waits for them, and re-layouts: 1.2 us -> none  [per_device(): ground_density.reshape(1, POINTS)]
    squeeze x2, local copies, waits for them, and re-layouts: 0.04 us -> 0.67 us  [summed_over_devices(): sent = lax.dynamic_index_in_dim(pair, 1 - bit, 0, keepdims=False)]
  transfers between devices with their start and end apart: 9 -> 9, of which waited for: 3 -> 4; matrix products, arithmetic and copies ran while one was open for 4% -> 4% of each run, Pallas kernels for 36% -> 39%
where the time goes in v2:
time: 45.5 us; the launch traced here: 45.1 us
  Pallas kernels  20.1 us (44%)
  starting transfers between devices  12.4 us (27%)
  waiting for transfers between devices  7.9 us (17%)
  local copies, waits for them, and re-layouts  3.54 us (8%)
  other arithmetic  1.03 us (2%)
    pallas_call x8, Pallas kernels, call(): kernel(*(placed(v, spec) for spec, v in zip(specs, values)))  20.1 us
    ppermute x7, starting transfers between devices, swap(): return lax.ppermute(values, axis, [(i, i ^ distance) for i in range(count)])  8.75 us
    ppermute x7, waiting for transfers between devices, swap(): return lax.ppermute(values, axis, [(i, i ^ distance) for i in range(count)])  5.2 us
    ppermute x1, starting transfers between devices, per_device(): lax.ppermute(kept, 'orb', [((i + 1) % count, i) for i in range(count)])  3.54 us
    unnamed x24, local copies, waits for them, and re-layouts  2.87 us
    ppermute x1, waiting for transfers between devices, per_device(): lax.ppermute(away, 'orb', [(i, (i + 1) % count) for i in range(count)])  2.7 us
    add x2, other arithmetic, summed_over_devices(): term = kept + swap(sent, axis, distance)  0.92 us
  transfers between devices with their start and end apart: 9, of which 4 were waited for; matrix products, arithmetic and copies ran while one was open for 4% of the time, Pallas kernels for 39%

profile of v2, /device:TPU:0, one launch (start us, length us, event | category | flops | bytes accessed | tf_op | source)
XLA Modules:
  0.0 45.1 jit_solution(11116259133153239063)
XLA Ops:
  0.0 0.0 copy-start
  0.0 1.5 %prelude.1 = (f32[640,128]{1,0:T(8,128)S(1)}, f32[640,128]{1,0:T(8,128)S(1)}, f32[640,128]{1,0:T(8,128)S(1)}, f32[8,128]{1,0:T(8,128)S(1)}) custom-call(s32[1]{0:T(128)} %bitcast.position, s32[4]{0:T(128)} %signs.1, s32[1,2]{1,0:T(1,128)} %offsets.1, f32[4,81000]{1,0:T(4,128)} %ground.3, f32[1,81000]{1,0:T(1,128)} %response.1), custom_call_target="tpu_custom_call" | custom-call | flops 1000000000 | bytes 1000000 | tf_op jit(solution)/shard_map/prelude/pallas_call | solution.py:305
  1.6 0.6 %collective-permute-start = (f32[320,128]{1,0:T(8,128)S(1)}, f32[320,128]{1,0:T(8,128)S(1)}, u32[]{:S(2)}, u32[]{:S(2)}) collective-permute-start(f32[320,128]{1,0:T(8,128)S(1)} %dynamic-slice_bitcast_fusion), channel_id=1, source_target_pairs={{0,4},{4,0},{8,12},{12,8},{16,20},{20,16},{24,28},{28,24},{1,5},{5... | collective-permute-start | bytes 491528 | tf_op jit(solution)/shard_map/ppermute | solution.py:310
  2.1 3.5 %collective-permute-start.7 = (f32[640,128]{1,0:T(8,128)S(1)}, f32[640,128]{1,0:T(8,128)S(1)}, u32[]{:S(2)}, u32[]{:S(2)}) collective-permute-start(f32[640,128]{1,0:T(8,128)S(1)} %get-tuple-element.20.response), channel_id=1, source_target_pairs={{4,0},{8,4},{12,8},{16,12},{20,16},{24,20},{28,24},{0,28},{5,1},{9... | collective-permute-start | bytes 983048 | tf_op jit(solution)/shard_map/ppermute | solution.py:367
  5.7 0.0 collective-permute-done
  5.7 0.6 %dynamic-slice_bitcast_fusion.1 = f32[160,128]{1,0:T(8,128)} fusion(f32[2,160,128]{2,1,0:T(8,128)S(1)} %bitcast.13, s32[]{:T(128)S(6)} %select_n.68), kind=kLoop, calls=%fused_computation.5 | loop fusion | bytes 163844 | tf_op jit(solution)/shard_map/jit(dynamic_index_in_dim)/squeeze | solution.py:321
  6.3 0.0 copy-start.1
  6.3 0.0 copy-start.2
  6.3 0.0 copy-start.5
  6.4 0.0 copy-start.6
  6.4 0.4 collective-permute-start.1
  6.8 0.0 copy-done
  6.8 2.3 %lines.1 = (f32[1376,128]{1,0:T(8,128)S(1)}, f32[1376,128]{1,0:T(8,128)S(1)}) custom-call(f32[4,81000]{1,0:T(4,128)S(1)} %copy-done), custom_call_target="tpu_custom_call" | custom-call | flops 2000000000 | bytes 2000000 | tf_op jit(solution)/shard_map/lines/pallas_call | solution.py:305
  9.0 0.0 copy-start.7
  9.0 0.8 %copy-done.7 = f32[1376,128]{1,0:T(8,128)} copy-done((f32[1376,128]{1,0:T(8,128)}, f32[1376,128]{1,0:T(8,128)S(1)}, u32[]{:S(2)}) %copy-start.7) | copy-done | bytes 704536
  9.9 2.2 %collective-permute-done.1 = f32[160,128]{1,0:T(8,128)} collective-permute-done((f32[160,128]{1,0:T(8,128)}, f32[160,128]{1,0:T(8,128)}, u32[]{:S(2)}, u32[]{:S(2)}) %collective-permute-start.1) | collective-permute-done | bytes 81952 | tf_op jit(solution)/shard_map/ppermute | solution.py:310
  12.1 0.9 %bitcast_add_fusion.1 = f32[160,128]{1,0:T(8,128)S(1)} fusion(f32[160,128]{1,0:T(8,128)} %collective-permute-done.1, f32[2,160,128]{2,1,0:T(8,128)S(1)} %bitcast.14, s32[]{:T(128)S(6)} %select_n.67), kind=kLoop, calls=%fused_computation.4 | loop fusion | flops 20480 | bytes 245764 | tf_op jit(solution)/shard_map/add | solution.py:322
  13.0 1.6 %collective-permute-start.2 = (f32[160,128]{1,0:T(8,128)S(1)}, f32[160,128]{1,0:T(8,128)S(1)}, u32[]{:S(2)}, u32[]{:S(2)}) collective-permute-start(f32[160,128]{1,0:T(8,128)S(1)} %bitcast_add_fusion.1), channel_id=1, source_target_pairs={{0,16},{4,20},{8,24},{12,28},{16,0},{20,4},{24,8},{28,12},{1,17},{... | collective-permute-start | bytes 245768 | tf_op jit(solution)/shard_map/ppermute | solution.py:310
  14.6 0.0 copy-done.1
  14.6 0.0 copy-done.2
  14.6 0.0 copy-done.3
  14.6 0.0 copy-done.4
  14.6 0.0 copy-done.5
  14.7 0.0 copy-done.6
  14.7 0.0 copy-start.8
  14.7 1.1 %copy-done.8 = f32[1376,128]{1,0:T(8,128)S(1)} copy-done((f32[1376,128]{1,0:T(8,128)S(1)}, f32[1376,128]{1,0:T(8,128)}, u32[]{:S(2)}) %copy-start.8) | copy-done | bytes 704536
  15.8 3.6 %first_half.2 = (f32[1376,128]{1,0:T(8,128)S(1)}, f32[1376,128]{1,0:T(8,128)S(1)}) custom-call(f32[8,128]{1,0:T(8,128)S(1)} %get-tuple-element.18.weights, f32[1376,128]{1,0:T(8,128)S(1)} %copy-done.8, f32[640,128]{1,0:T(8,128)S(1)} %get-tuple-element.20.response, bf16[256,256]{1,0:T(8,128)(2,1)S(1)} %copy-done.2, bf16[256,256]{1,0:T(8,128)(2,1)S(1)} %copy-done.1, ...), custom_call_target="tpu_custom_call" | custom-call | flops 3000000000 | bytes 3000000 | tf_op jit(solution)/shard_map/first_half/pallas_call | solution.py:305
  19.3 0.0 copy-start.10
  19.4 0.9 %copy-done.10 = f32[1376,128]{1,0:T(8,128)} copy-done((f32[1376,128]{1,0:T(8,128)}, f32[1376,128]{1,0:T(8,128)S(1)}, u32[]{:S(2)}) %copy-start.10) | copy-done | bytes 704536
  20.2 0.0 collective-permute-done.2
  20.3 1.6 %collective-permute-start.3 = (f32[160,128]{1,0:T(8,128)S(1)}, f32[160,128]{1,0:T(8,128)S(1)}, u32[]{:S(2)}, u32[]{:S(2)}) collective-permute-start(f32[160,128]{1,0:T(8,128)S(1)} %add.50), channel_id=1, source_target_pairs={{0,1},{1,0},{2,3},{3,2},{4,5},{5,4},{6,7},{7,6},{8,9},{9,8},{10,11... | collective-permute-start | bytes 245768 | tf_op jit(solution)/shard_map/ppermute | solution.py:310
  21.9 1.2 %coefficient.1 = f32[640,128]{1,0:T(8,128)S(1)} custom-call(f32[81000]{0:T(1024)} %density.1, f32[640,128]{1,0:T(8,128)S(1)} %get-tuple-element.16.own), custom_call_target="tpu_custom_call" | custom-call | flops 1000000000 | bytes 1000000 | tf_op jit(solution)/shard_map/coefficient/pallas_call | solution.py:305
  23.0 2.6 %collective-permute-done.3 = f32[160,128]{1,0:T(8,128)S(1)} collective-permute-done((f32[160,128]{1,0:T(8,128)S(1)}, f32[160,128]{1,0:T(8,128)S(1)}, u32[]{:S(2)}, u32[]{:S(2)}) %collective-permute-start.3) | collective-permute-done | bytes 81952 | tf_op jit(solution)/shard_map/ppermute | solution.py:310
  25.7 2.4 %collective-permute-start.4 = (f32[160,128]{1,0:T(8,128)S(1)}, f32[160,128]{1,0:T(8,128)S(1)}, u32[]{:S(2)}, u32[]{:S(2)}) collective-permute-start(f32[160,128]{1,0:T(8,128)S(1)} %add.51), channel_id=1, source_target_pairs={{0,2},{1,3},{2,0},{3,1},{4,6},{5,7},{6,4},{7,5},{8,10},{9,11},{10,... | collective-permute-start | bytes 245768 | tf_op jit(solution)/shard_map/ppermute | solution.py:310
  28.0 0.0 collective-permute-done.7.response
  28.0 0.0 copy-done.9
  28.0 3.6 %first_half.3 = (f32[1376,128]{1,0:T(8,128)S(1)}, f32[1376,128]{1,0:T(8,128)S(1)}) custom-call(f32[8,128]{1,0:T(8,128)S(1)} %get-tuple-element.18.weights, f32[1376,128]{1,0:T(8,128)S(1)} %copy-done.9, f32[640,128]{1,0:T(8,128)S(1)} %collective-permute-done.7.response, bf16[256,256]{1,0:T(8,128)(2,1)S(1)} %copy-done.2, bf16[256,256]{1,0:T(8,128)(2,1)S(1)} %copy-done.1, ...), custom_call_target="tpu_custom_call" | custom-call | flops 3000000000 | bytes 3000000 | tf_op jit(solution)/shard_map/first_half/pallas_call | solution.py:305
  31.6 0.3 collective-permute-done.4
  32.0 1.2 %collective-permute-start.5 = (f32[160,128]{1,0:T(8,128)S(1)}, f32[160,128]{1,0:T(8,128)S(1)}, u32[]{:S(2)}, u32[]{:S(2)}) collective-permute-start(f32[160,128]{1,0:T(8,128)S(1)} %add.52), channel_id=1, source_target_pairs={{0,8},{4,12},{8,0},{12,4},{16,24},{20,28},{24,16},{28,20},{1,9},{5... | collective-permute-start | bytes 245768 | tf_op jit(solution)/shard_map/ppermute | solution.py:310
  33.2 3.6 %second_half.2 = f32[640,128]{1,0:T(8,128)S(1)} custom-call(f32[8,128]{1,0:T(8,128)S(1)} %get-tuple-element.18.weights, f32[1376,128]{1,0:T(8,128)S(1)} %get-tuple-element.19.lines, f32[640,128]{1,0:T(8,128)S(1)} %collective-permute-done.7.response, bf16[256,256]{1,0:T(8,128)(2,1)S(1)} %copy-done.2, bf16[256,256]{1,0:T(8,128)(2,1)S(1)} %copy-done.1, ...), custom_call_target="tpu_custom_call" | custom-call | flops 3000000000 | bytes 3000000 | tf_op jit(solution)/shard_map/second_half/pallas_call | solution.py:305
  36.8 0.1 collective-permute-start.8
  36.9 0.0 collective-permute-done.5
  37.0 1.0 %collective-permute-start.6 = (f32[320,128]{1,0:T(8,128)S(1)}, f32[320,128]{1,0:T(8,128)S(1)}, u32[]{:S(2)}, u32[]{:S(2)}) collective-permute-start(f32[320,128]{1,0:T(8,128)S(1)} %pad_maximum_fusion.1), channel_id=1, source_target_pairs={{0,4},{4,0},{8,12},{12,8},{16,20},{20,16},{24,28},{28,24},{1,5},{5... | collective-permute-start | bytes 491528 | tf_op jit(solution)/shard_map/ppermute | solution.py:310
  37.9 0.0 copy-done.11
  37.9 3.5 %second_half.3.first = f32[640,128]{1,0:T(8,128)S(1)} custom-call(f32[8,128]{1,0:T(8,128)S(1)} %get-tuple-element.18.weights, f32[1376,128]{1,0:T(8,128)S(1)} %get-tuple-element.19.lines, f32[640,128]{1,0:T(8,128)S(1)} %get-tuple-element.20.response, bf16[256,256]{1,0:T(8,128)(2,1)S(1)} %copy-done.2, bf16[256,256]{1,0:T(8,128)(2,1)S(1)} %copy-done.1, ...), custom_call_target="tpu_custom_call" | custom-call | flops 3000000000 | bytes 3000000 | tf_op jit(solution)/shard_map/second_half/pallas_call | solution.py:305
  41.5 0.0 collective-permute-done.6
  41.6 2.7 %collective-permute-done.8.second = f32[640,128]{1,0:T(8,128)S(1)} collective-permute-done((f32[640,128]{1,0:T(8,128)S(1)}, f32[640,128]{1,0:T(8,128)S(1)}, u32[]{:S(2)}, u32[]{:S(2)}) %collective-permute-start.8) | collective-permute-done | bytes 327712 | tf_op jit(solution)/shard_map/ppermute | solution.py:381
  44.3 0.8 %finish.1 = f32[1,81000]{1,0:T(1,128)} custom-call(f32[640,128]{1,0:T(8,128)S(1)} %coefficient.1, f32[640,128]{1,0:T(8,128)S(1)} %pad_maximum_fusion.density, f32[640,128]{1,0:T(8,128)S(1)} %second_half.3.first, f32[640,128]{1,0:T(8,128)S(1)} %collective-permute-done.8.second), custom_call_target="tpu_custom_call" | custom-call | flops 1000000000 | bytes 1000000 | tf_op jit(solution)/shard_map/finish/pallas_call | solution.py:305
  (13 shorter events, 0.2 us)
Async XLA Ops:
  0.0 6.8 %copy-start = (f32[4,81000]{1,0:T(4,128)S(1)}, f32[4,81000]{1,0:T(4,128)}, u32[]{:S(2)}) copy-start(f32[4,81000]{1,0:T(4,128)} %ground.3) | copy-start | bytes 3888004
  1.6 4.1 %collective-permute-start = (f32[320,128]{1,0:T(8,128)S(1)}, f32[320,128]{1,0:T(8,128)S(1)}, u32[]{:S(2)}, u32[]{:S(2)}) collective-permute-start(f32[320,128]{1,0:T(8,128)S(1)} %dynamic-slice_bitcast_fusion), channel_id=1, source_target_pairs={{0,4},{4,0},{8,12},{12,8},{16,20},{20,16},{24,28},{28,24},{1,5},{5... | collective-permute-start | bytes 491528 | tf_op jit(solution)/shard_map/ppermute | solution.py:310
  2.1 25.9 %collective-permute-start.7 = (f32[640,128]{1,0:T(8,128)S(1)}, f32[640,128]{1,0:T(8,128)S(1)}, u32[]{:S(2)}, u32[]{:S(2)}) collective-permute-start(f32[640,128]{1,0:T(8,128)S(1)} %get-tuple-element.20.response), channel_id=1, source_target_pairs={{4,0},{8,4},{12,8},{16,12},{20,16},{24,20},{28,24},{0,28},{5,1},{9... | collective-permute-start | bytes 983048 | tf_op jit(solution)/shard_map/ppermute | solution.py:367
  6.3 8.3 %copy-start.1 = (bf16[256,256]{1,0:T(8,128)(2,1)S(1)}, bf16[256,256]{1,0:T(8,128)(2,1)}, u32[]{:S(2)}) copy-start(bf16[256,256]{1,0:T(8,128)(2,1)} %constant.85.clone.refs_1_) | copy-start | bytes 393220
  6.3 8.3 %copy-start.2 = (bf16[256,256]{1,0:T(8,128)(2,1)S(1)}, bf16[256,256]{1,0:T(8,128)(2,1)}, u32[]{:S(2)}) copy-start(bf16[256,256]{1,0:T(8,128)(2,1)} %constant.84.clone.refs_0_) | copy-start | bytes 393220
  6.3 8.3 %copy-start.3 = (bf16[48,144]{1,0:T(8,128)(2,1)S(1)}, bf16[48,144]{1,0:T(8,128)(2,1)}, u32[]{:S(2)}) copy-start(bf16[48,144]{1,0:T(8,128)(2,1)} %constant.87.clone.refs_3_) | copy-start | bytes 41476
  6.3 8.3 %copy-start.4 = (bf16[48,144]{1,0:T(8,128)(2,1)S(1)}, bf16[48,144]{1,0:T(8,128)(2,1)}, u32[]{:S(2)}) copy-start(bf16[48,144]{1,0:T(8,128)(2,1)} %constant.86.clone.refs_2_) | copy-start | bytes 41476
  6.3 8.3 %copy-start.5 = (bf16[32,96]{1,0:T(8,128)(2,1)S(1)}, bf16[32,96]{1,0:T(8,128)(2,1)}, u32[]{:S(2)}) copy-start(bf16[32,96]{1,0:T(8,128)(2,1)} %constant.89.clone.refs_5_) | copy-start | bytes 18436
  6.4 8.3 %copy-start.6 = (bf16[32,96]{1,0:T(8,128)(2,1)S(1)}, bf16[32,96]{1,0:T(8,128)(2,1)}, u32[]{:S(2)}) copy-start(bf16[32,96]{1,0:T(8,128)(2,1)} %constant.88.clone.refs_4_) | copy-start | bytes 18436
  6.4 5.7 %collective-permute-start.1 = (f32[160,128]{1,0:T(8,128)}, f32[160,128]{1,0:T(8,128)}, u32[]{:S(2)}, u32[]{:S(2)}) collective-permute-start(f32[160,128]{1,0:T(8,128)} %dynamic-slice_bitcast_fusion.1), channel_id=1, source_target_pairs={{0,8},{4,12},{8,0},{12,4},{16,24},{20,28},{24,16},{28,20},{1,9},{5... | collective-permute-start | bytes 245768 | tf_op jit(solution)/shard_map/ppermute | solution.py:310
  9.0 0.9 %copy-start.7 = (f32[1376,128]{1,0:T(8,128)}, f32[1376,128]{1,0:T(8,128)S(1)}, u32[]{:S(2)}) copy-start(f32[1376,128]{1,0:T(8,128)S(1)} %get-tuple-element.21.lines) | copy-start | bytes 2113540
  13.0 7.2 %collective-permute-start.2 = (f32[160,128]{1,0:T(8,128)S(1)}, f32[160,128]{1,0:T(8,128)S(1)}, u32[]{:S(2)}, u32[]{:S(2)}) collective-permute-start(f32[160,128]{1,0:T(8,128)S(1)} %bitcast_add_fusion.1), channel_id=1, source_target_pairs={{0,16},{4,20},{8,24},{12,28},{16,0},{20,4},{24,8},{28,12},{1,17},{... | collective-permute-start | bytes 245768 | tf_op jit(solution)/shard_map/ppermute | solution.py:310
  14.7 1.1 %copy-start.8 = (f32[1376,128]{1,0:T(8,128)S(1)}, f32[1376,128]{1,0:T(8,128)}, u32[]{:S(2)}) copy-start(f32[1376,128]{1,0:T(8,128)} %copy-done.7) | copy-start | bytes 2113540
  19.3 0.9 %copy-start.10 = (f32[1376,128]{1,0:T(8,128)}, f32[1376,128]{1,0:T(8,128)S(1)}, u32[]{:S(2)}) copy-start(f32[1376,128]{1,0:T(8,128)S(1)} %get-tuple-element.26.refs_8_) | copy-start | bytes 2113540
  20.3 5.4 %collective-permute-start.3 = (f32[160,128]{1,0:T(8,128)S(1)}, f32[160,128]{1,0:T(8,128)S(1)}, u32[]{:S(2)}, u32[]{:S(2)}) collective-permute-start(f32[160,128]{1,0:T(8,128)S(1)} %add.50), channel_id=1, source_target_pairs={{0,1},{1,0},{2,3},{3,2},{4,5},{5,4},{6,7},{7,6},{8,9},{9,8},{10,11... | collective-permute-start | bytes 245768 | tf_op jit(solution)/shard_map/ppermute | solution.py:310
  21.9 6.2 %copy-start.9 = (f32[1376,128]{1,0:T(8,128)S(1)}, f32[1376,128]{1,0:T(8,128)}, u32[]{:S(2)}) copy-start(f32[1376,128]{1,0:T(8,128)} %copy-done.7) | copy-start | bytes 2113540
  25.7 6.3 %collective-permute-start.4 = (f32[160,128]{1,0:T(8,128)S(1)}, f32[160,128]{1,0:T(8,128)S(1)}, u32[]{:S(2)}, u32[]{:S(2)}) collective-permute-start(f32[160,128]{1,0:T(8,128)S(1)} %add.51), channel_id=1, source_target_pairs={{0,2},{1,3},{2,0},{3,1},{4,6},{5,7},{6,4},{7,5},{8,10},{9,11},{10,... | collective-permute-start | bytes 245768 | tf_op jit(solution)/shard_map/ppermute | solution.py:310
  32.0 4.9 %collective-permute-start.5 = (f32[160,128]{1,0:T(8,128)S(1)}, f32[160,128]{1,0:T(8,128)S(1)}, u32[]{:S(2)}, u32[]{:S(2)}) collective-permute-start(f32[160,128]{1,0:T(8,128)S(1)} %add.52), channel_id=1, source_target_pairs={{0,8},{4,12},{8,0},{12,4},{16,24},{20,28},{24,16},{28,20},{1,9},{5... | collective-permute-start | bytes 245768 | tf_op jit(solution)/shard_map/ppermute | solution.py:310
  33.2 4.7 %copy-start.11 = (f32[1376,128]{1,0:T(8,128)S(1)}, f32[1376,128]{1,0:T(8,128)}, u32[]{:S(2)}) copy-start(f32[1376,128]{1,0:T(8,128)} %copy-done.10) | copy-start | bytes 2113540
  36.8 7.5 %collective-permute-start.8 = (f32[640,128]{1,0:T(8,128)S(1)}, f32[640,128]{1,0:T(8,128)S(1)}, u32[]{:S(2)}, u32[]{:S(2)}) collective-permute-start(f32[640,128]{1,0:T(8,128)S(1)} %second_half.2), channel_id=1, source_target_pairs={{0,4},{4,8},{8,12},{12,16},{16,20},{20,24},{24,28},{28,0},{1,5},{5... | collective-permute-start | bytes 983048 | tf_op jit(solution)/shard_map/ppermute | solution.py:381
  37.0 4.6 %collective-permute-start.6 = (f32[320,128]{1,0:T(8,128)S(1)}, f32[320,128]{1,0:T(8,128)S(1)}, u32[]{:S(2)}, u32[]{:S(2)}) collective-permute-start(f32[320,128]{1,0:T(8,128)S(1)} %pad_maximum_fusion.1), channel_id=1, source_target_pairs={{0,4},{4,0},{8,12},{12,8},{16,20},{20,16},{24,28},{28,24},{1,5},{5... | collective-permute-start | bytes 491528 | tf_op jit(solution)/shard_map/ppermute | solution.py:310

commit v3 on v2

--- a/solution.py
+++ b/solution.py
@@ -153,8 +153,8 @@
     lax.fori_loop(0, count // group, lambda step, carry: (body(step * group), carry)[1], 0)
 
 
-def prelude_kernel(position, signs, offsets, ground, response, term, own, kept, weights, rows, sign, offset, sems):
-    place = position[0]
+def prelude_kernel(signs, offsets, ground, response, stays, goes, own, kept, weights, rows, sign, offset, term, sems):
+    place = lax.axis_index("grid")
     spot = pl.ds(place, 1)
     copies = [
         pltpu.make_async_copy(signs, sign, sems.at[0]),
@@ -172,6 +172,7 @@
     fill_tail(rows[0, :, last], kept)
     fill_tail(rows[1, :, last], own)
     term[...] = sign[place].astype(F32) * own[...] * kept[...]
+    share(term, 1, stays, goes)
     for step in range(2):
         kept[pl.ds(SENT_ROWS - 2 + step, 1), :] = jnp.full((1, LANES), offset[0, step].astype(F32))
     ids = lane_ids(1)
@@ -270,7 +271,8 @@
     exchange[...] = flat[pl.ds(0, SENT_ROWS), :]
 
 
-def finish_kernel(coefficient, density, first, second, out):
+def finish_kernel(coefficient, mine, other, first, second, out, density):
+    join_kernel(1, mine, other, density)
     value = coefficient[...] * density[...] - HYBRID * (first[...] + second[...])
     out.at[:, pl.ds(0, WHOLE * LANES)].reshape(WHOLE, LANES)[...] = value[:WHOLE]
     out[:, pl.ds(WHOLE * LANES, TAIL)] = value[WHOLE : WHOLE + 1, :TAIL]
@@ -305,28 +307,53 @@
     return lambda *values: kernel(*(placed(v, spec) for spec, v in zip(specs, values)))
 
 
+def orb_bit(distance):
+    return lax.rem(lax.div(lax.axis_index("orb"), distance), 2)
+
+
+def share(term, distance, stays, goes):
+    half, bit = stays.shape[0], orb_bit(distance)
+    stays[...] = term[pl.ds(pl.multiple_of(bit * half, half), half), :]
+    goes[...] = term[pl.ds(pl.multiple_of((1 - bit) * half, half), half), :]
+
+
+def share_kernel(distance, mine, other, stays, goes, term):
+    term[...] = mine[...] + other[...]
+    share(term, distance, stays, goes)
+
+
+def add_kernel(mine, other, out):
+    out[...] = mine[...] + other[...]
+
+
+def join_kernel(distance, mine, other, out):
+    half, bit = mine.shape[0], orb_bit(distance)
+    out[pl.ds(pl.multiple_of(bit * half, half), half), :] = mine[...]
+    out[pl.ds(pl.multiple_of((1 - bit) * half, half), half), :] = other[...]
+
+
 def swap(values, axis, distance):
     count = lax.axis_size(axis)
     return lax.ppermute(values, axis, [(i, i ^ distance) for i in range(count)])
 
 
-def summed_over_devices(term):
+def summed_over_devices(stays, goes):
     orb_bits = [("orb", 1 << bit) for bit in range(lax.axis_size("orb").bit_length() - 1)]
     grid_bits = [("grid", 1 << bit) for bit in range(lax.axis_size("grid").bit_length() - 1)]
-    split_bits, rest = orb_bits[:2], orb_bits[2:] + grid_bits
-    for axis, distance in split_bits:
-        bit = (lax.axis_index(axis) // distance) % 2
-        pair = term.reshape(2, term.shape[0] // 2, LANES)
-        kept = lax.dynamic_index_in_dim(pair, bit, 0, keepdims=False)
-        sent = lax.dynamic_index_in_dim(pair, 1 - bit, 0, keepdims=False)
-        term = kept + swap(sent, axis, distance)
-    for axis, distance in rest:
-        term = term + swap(term, axis, distance)
-    for axis, distance in split_bits[::-1]:
-        bit = (lax.axis_index(axis) // distance) % 2
+    half = (stays.shape[0], LANES)
+    quarter = (stays.shape[0] // 2, LANES)
+    other = swap(goes, "orb", 1)
+    stays, goes = call(
+        functools.partial(share_kernel, 2), "share", [VECTORS] * 2, [quarter] * 2, [pltpu.VMEM(half, F32)], 0.1
+    )(stays, other)
+    term, other = stays, swap(goes, "orb", 2)
+    for axis, distance in orb_bits[2:] + grid_bits:
+        term = call(add_kernel, "add", [VECTORS] * 2, [quarter], [], 0.1)(term, other)[0]
         other = swap(term, axis, distance)
-        term = jnp.concatenate([jnp.where(bit == 0, term, other), jnp.where(bit == 0, other, term)], 0)
-    return term
+    term = call(add_kernel, "add", [VECTORS] * 2, [quarter], [], 0.1)(term, other)[0]
+    other = swap(term, "orb", 2)
+    term = call(functools.partial(join_kernel, 2), "join", [VECTORS] * 2, [half], [], 0.1)(term, other)[0]
+    return term, swap(term, "orb", 1)
 
 
 def half_call(body, name, step, shapes, extra, values):
@@ -357,15 +384,15 @@
     )
     tables = tuple(jnp.asarray(table) for table in tables)
     flat = (SENT_ROWS, LANES)
-    position = lax.axis_index("grid").reshape(1)
+    half = (SENT_ROWS // 2, LANES)
     scratch = [pltpu.VMEM((2, 1, POINTS), F32), pltpu.SMEM((4,), jnp.int32), pltpu.SMEM((1, 2), jnp.int32)]
-    term, own, kept, weights = call(
-        prelude_kernel, "prelude", [SCALARS] + [FAR] * 4, [flat] * 3 + [(8, LANES)],
-        scratch + [pltpu.SemaphoreType.DMA((6,))], 1,
-    )(position, occupation_signs, window_offsets, ground_orbitals, response_orbitals)
+    stays, goes, own, kept, weights = call(
+        prelude_kernel, "prelude", [FAR] * 4, [half] * 2 + [flat] * 2 + [(8, LANES)],
+        scratch + [pltpu.VMEM(flat, F32), pltpu.SemaphoreType.DMA((6,))], 1,
+    )(occupation_signs, window_offsets, ground_orbitals, response_orbitals)
     count = lax.axis_size("orb")
     visiting = lax.ppermute(kept, "orb", [((i + 1) % count, i) for i in range(count)])
-    density = summed_over_devices(term)
+    mine, other = summed_over_devices(stays, goes)
     low_lines, high_lines = call(
         lines_kernel, "lines", [VECTORS], [(LINE_ROWS, LANES)] * 2,
         [pltpu.VMEM((4, FLAT_ROWS, LANES), F32), pltpu.VMEM((PERIODS * (LINES + 1), LANES), F32),
@@ -381,7 +408,9 @@
     second = lax.ppermute(away, "orb", [(i, (i + 1) % count) for i in range(count)])
     values, away = lax.optimization_barrier((values, away))
     first = second_half(0, weights, high_lines, kept, *tables, values, partial)
-    return call(finish_kernel, "finish", [VECTORS] * 4, [(1, POINTS)], [], 1)(coefficient, density, first, second)[0]
+    return call(finish_kernel, "finish", [VECTORS] * 5, [(1, POINTS)], [pltpu.VMEM(flat, F32)], 1)(
+        coefficient, mine, other, first, second
+    )[0]
 
 
 def solution(mesh):

time: 45.5 us -> 42 us (0.923)
  local copies, waits for them, and re-layouts: 3.54 us -> 0.04 us
  starting transfers between devices: 12.4 us -> 15.3 us
  waiting for transfers between devices: 7.9 us -> 6.05 us
  other arithmetic: 1.03 us -> 0 us
    ppermute x7, starting transfers between devices: 8.75 us -> 11.7 us  [swap(): return lax.ppermute(values, axis, [(i, i ^ distance) for i in range(count)])]
    unnamed x24 -> x14, local copies, waits for them, and re-layouts: 2.87 us -> 0.04 us
    ppermute x1, waiting for transfers between devices: 2.7 us -> 0.01 us  [per_device(): lax.ppermute(away, 'orb', [(i, (i + 1) % count) for i in range(count)])]
    add x5 -> x0, other arithmetic: 0.95 us -> none  [the longest x2 0.92 us: summed_over_devices(): term = kept + swap(sent, axis, distance)]
    ppermute x7, waiting for transfers between devices: 5.2 us -> 6.05 us  [swap(): return lax.ppermute(values, axis, [(i, i ^ distance) for i in range(count)])]
    squeeze x2 -> x0, local copies, waits for them, and re-layouts: 0.67 us -> none  [summed_over_devices(): sent = lax.dynamic_index_in_dim(pair, 1 - bit, 0, keepdims=False)]
    pallas_call x8 -> x14, Pallas kernels: 20.1 us -> 20.1 us  [call(): kernel(*(placed(v, spec) for spec, v in zip(specs, values)))]
  transfers between devices with their start and end apart: 9 -> 9, of which waited for: 4 -> 2; matrix products, arithmetic and copies ran while one was open for 4% -> 0% of each run, Pallas kernels for 39% -> 42%
where the time goes in v3:
time: 42 us; the launch traced here: 41.7 us
  Pallas kernels  20.1 us (48%)
  starting transfers between devices  15.3 us (36%)
  waiting for transfers between devices  6.05 us (14%)
    pallas_call x14, Pallas kernels, call(): kernel(*(placed(v, spec) for spec, v in zip(specs, values)))  20.1 us
    ppermute x7, starting transfers between devices, swap(): return lax.ppermute(values, axis, [(i, i ^ distance) for i in range(count)])  11.7 us
    ppermute x7, waiting for transfers between devices, swap(): return lax.ppermute(values, axis, [(i, i ^ distance) for i in range(count)])  6.05 us
    ppermute x1, starting transfers between devices, per_device(): lax.ppermute(kept, 'orb', [((i + 1) % count, i) for i in range(count)])  3.54 us
  transfers between devices with their start and end apart: 9, of which 2 were waited for; matrix products, arithmetic and copies ran while one was open for 0% of the time, Pallas kernels for 42%

profile of v3, /device:TPU:0, one launch (start us, length us, event | category | flops | bytes accessed | tf_op | source)
XLA Modules:
  0.0 41.7 jit_solution(18431958051426562160)
XLA Ops:
  0.0 0.0 copy-start
  0.0 1.5 %prelude.1 = (f32[320,128]{1,0:T(8,128)S(1)}, f32[320,128]{1,0:T(8,128)S(1)}, f32[640,128]{1,0:T(8,128)S(1)}, f32[640,128]{1,0:T(8,128)S(1)}, f32[8,128]{1,0:T(8,128)S(1)}) custom-call(s32[4]{0:T(128)} %signs.1, s32[1,2]{1,0:T(1,128)} %offsets.1, f32[4,81000]{1,0:T(4,128)} %ground.3, f32[1,81000]{1,0:T(1,128)} %response.1), custom_call_target="tpu_custom_call" | custom-call | flops 1000000000 | bytes 1000000 | tf_op jit(solution)/shard_map/prelude/pallas_call | solution.py:307
  1.6 0.6 %collective-permute-start = (f32[320,128]{1,0:T(8,128)S(1)}, f32[320,128]{1,0:T(8,128)S(1)}, u32[]{:S(2)}, u32[]{:S(2)}) collective-permute-start(f32[320,128]{1,0:T(8,128)S(1)} %get-tuple-element.21), channel_id=1, source_target_pairs={{0,4},{4,0},{8,12},{12,8},{16,20},{20,16},{24,28},{28,24},{1,5},{5... | collective-permute-start | bytes 491528 | tf_op jit(solution)/shard_map/ppermute | solution.py:337
  2.1 3.5 %collective-permute-start.7 = (f32[640,128]{1,0:T(8,128)S(1)}, f32[640,128]{1,0:T(8,128)S(1)}, u32[]{:S(2)}, u32[]{:S(2)}) collective-permute-start(f32[640,128]{1,0:T(8,128)S(1)} %get-tuple-element.26.response), channel_id=1, source_target_pairs={{4,0},{8,4},{12,8},{16,12},{20,16},{24,20},{28,24},{0,28},{5,1},{9... | collective-permute-start | bytes 983048 | tf_op jit(solution)/shard_map/ppermute | solution.py:394
  5.7 0.0 collective-permute-done.other
  5.7 0.0 copy-start.1
  5.7 0.0 copy-start.2
  5.7 0.0 copy-start.3
  5.7 0.0 copy-start.4
  5.7 0.0 copy-start.5
  5.8 0.0 copy-start.6
  5.8 0.4 collective-permute-start.1
  6.2 0.0 copy-done
  6.2 2.2 %lines.1 = (f32[1376,128]{1,0:T(8,128)S(1)}, f32[1376,128]{1,0:T(8,128)S(1)}) custom-call(f32[4,81000]{1,0:T(4,128)S(1)} %copy-done), custom_call_target="tpu_custom_call" | custom-call | flops 2000000000 | bytes 2000000 | tf_op jit(solution)/shard_map/lines/pallas_call | solution.py:307
  8.4 3.3 %collective-permute-done.1.other = f32[160,128]{1,0:T(8,128)S(1)} collective-permute-done((f32[160,128]{1,0:T(8,128)S(1)}, f32[160,128]{1,0:T(8,128)S(1)}, u32[]{:S(2)}, u32[]{:S(2)}) %collective-permute-start.1) | collective-permute-done | bytes 81952 | tf_op jit(solution)/shard_map/ppermute | solution.py:337
  11.7 1.9 %collective-permute-start.2 = (f32[160,128]{1,0:T(8,128)S(1)}, f32[160,128]{1,0:T(8,128)S(1)}, u32[]{:S(2)}, u32[]{:S(2)}) collective-permute-start(f32[160,128]{1,0:T(8,128)S(1)} %add.4.mine), channel_id=1, source_target_pairs={{0,16},{4,20},{8,24},{12,28},{16,0},{20,4},{24,8},{28,12},{1,17},{... | collective-permute-start | bytes 245768 | tf_op jit(solution)/shard_map/ppermute | solution.py:337
  13.6 0.0 copy-done.1
  13.6 0.0 copy-done.2
  13.6 0.0 copy-done.3
  13.6 0.0 copy-done.4
  13.7 0.0 copy-done.5
  13.7 0.0 copy-done.6
  13.7 3.6 %first_half.2 = (f32[1376,128]{1,0:T(8,128)S(1)}, f32[1376,128]{1,0:T(8,128)S(1)}) custom-call(f32[8,128]{1,0:T(8,128)S(1)} %get-tuple-element.24.weights, f32[1376,128]{1,0:T(8,128)S(1)} %get-tuple-element.27.lines, f32[640,128]{1,0:T(8,128)S(1)} %get-tuple-element.26.response, bf16[256,256]{1,0:T(8,128)(2,1)S(1)} %copy-done.2, ...), custom_call_target="tpu_custom_call" | custom-call | flops 3000000000 | bytes 3000000 | tf_op jit(solution)/shard_map/first_half/pallas_call | solution.py:307
  17.3 0.0 collective-permute-done.2.other
  17.3 1.6 %collective-permute-start.3 = (f32[160,128]{1,0:T(8,128)S(1)}, f32[160,128]{1,0:T(8,128)S(1)}, u32[]{:S(2)}, u32[]{:S(2)}) collective-permute-start(f32[160,128]{1,0:T(8,128)S(1)} %add.5.mine), channel_id=1, source_target_pairs={{0,1},{1,0},{2,3},{3,2},{4,5},{5,4},{6,7},{7,6},{8,9},{9,8},{10,11... | collective-permute-start | bytes 245768 | tf_op jit(solution)/shard_map/ppermute | solution.py:337
  18.9 0.0 collective-permute-done.7.response
  18.9 3.6 %first_half.3 = (f32[1376,128]{1,0:T(8,128)S(1)}, f32[1376,128]{1,0:T(8,128)S(1)}) custom-call(f32[8,128]{1,0:T(8,128)S(1)} %get-tuple-element.24.weights, f32[1376,128]{1,0:T(8,128)S(1)} %get-tuple-element.27.lines, f32[640,128]{1,0:T(8,128)S(1)} %collective-permute-done.7.response, bf16[256,256]{1,0:T(8,128)(2,1)S(1)} %copy-done.2, ...), custom_call_target="tpu_custom_call" | custom-call | flops 3000000000 | bytes 3000000 | tf_op jit(solution)/shard_map/first_half/pallas_call | solution.py:307
  22.5 0.0 collective-permute-done.3.other
  22.5 2.7 %collective-permute-start.4 = (f32[160,128]{1,0:T(8,128)S(1)}, f32[160,128]{1,0:T(8,128)S(1)}, u32[]{:S(2)}, u32[]{:S(2)}) collective-permute-start(f32[160,128]{1,0:T(8,128)S(1)} %add.6.mine), channel_id=1, source_target_pairs={{0,2},{1,3},{2,0},{3,1},{4,6},{5,7},{6,4},{7,5},{8,10},{9,11},{10,... | collective-permute-start | bytes 245768 | tf_op jit(solution)/shard_map/ppermute | solution.py:337
  25.2 3.5 %second_half.2 = f32[640,128]{1,0:T(8,128)S(1)} custom-call(f32[8,128]{1,0:T(8,128)S(1)} %get-tuple-element.24.weights, f32[1376,128]{1,0:T(8,128)S(1)} %get-tuple-element.25.lines, f32[640,128]{1,0:T(8,128)S(1)} %collective-permute-done.7.response, bf16[256,256]{1,0:T(8,128)(2,1)S(1)} %copy-done.2, bf16[256,256]{1,0:T(8,128)(2,1)S(1)} %copy-done.1, ...), custom_call_target="tpu_custom_call" | custom-call | flops 3000000000 | bytes 3000000 | tf_op jit(solution)/shard_map/second_half/pallas_call | solution.py:307
  28.7 0.1 collective-permute-start.8
  28.8 0.0 collective-permute-done.4.other
  28.8 1.5 %collective-permute-start.5 = (f32[160,128]{1,0:T(8,128)S(1)}, f32[160,128]{1,0:T(8,128)S(1)}, u32[]{:S(2)}, u32[]{:S(2)}) collective-permute-start(f32[160,128]{1,0:T(8,128)S(1)} %add.7.mine), channel_id=1, source_target_pairs={{0,8},{4,12},{8,0},{12,4},{16,24},{20,28},{24,16},{28,20},{1,9},{5... | collective-permute-start | bytes 245768 | tf_op jit(solution)/shard_map/ppermute | solution.py:337
  30.3 1.1 %coefficient.1 = f32[640,128]{1,0:T(8,128)S(1)} custom-call(f32[81000]{0:T(1024)} %density.1, f32[640,128]{1,0:T(8,128)S(1)} %get-tuple-element.19.own), custom_call_target="tpu_custom_call" | custom-call | flops 1000000000 | bytes 1000000 | tf_op jit(solution)/shard_map/coefficient/pallas_call | solution.py:307
  31.4 2.8 %collective-permute-done.5.other = f32[160,128]{1,0:T(8,128)S(1)} collective-permute-done((f32[160,128]{1,0:T(8,128)S(1)}, f32[160,128]{1,0:T(8,128)S(1)}, u32[]{:S(2)}, u32[]{:S(2)}) %collective-permute-start.5) | collective-permute-done | bytes 81952 | tf_op jit(solution)/shard_map/ppermute | solution.py:337
  34.2 3.0 %collective-permute-start.6 = (f32[320,128]{1,0:T(8,128)S(1)}, f32[320,128]{1,0:T(8,128)S(1)}, u32[]{:S(2)}, u32[]{:S(2)}) collective-permute-start(f32[320,128]{1,0:T(8,128)S(1)} %join.1.mine), channel_id=1, source_target_pairs={{0,4},{4,0},{8,12},{12,8},{16,20},{20,16},{24,28},{28,24},{1,5},{5... | collective-permute-start | bytes 491528 | tf_op jit(solution)/shard_map/ppermute | solution.py:337
  37.2 3.6 %second_half.3.first = f32[640,128]{1,0:T(8,128)S(1)} custom-call(f32[8,128]{1,0:T(8,128)S(1)} %get-tuple-element.24.weights, f32[1376,128]{1,0:T(8,128)S(1)} %get-tuple-element.25.lines, f32[640,128]{1,0:T(8,128)S(1)} %get-tuple-element.26.response, bf16[256,256]{1,0:T(8,128)(2,1)S(1)} %copy-done.2, bf16[256,256]{1,0:T(8,128)(2,1)S(1)} %copy-done.1, ...), custom_call_target="tpu_custom_call" | custom-call | flops 3000000000 | bytes 3000000 | tf_op jit(solution)/shard_map/second_half/pallas_call | solution.py:307
  40.8 0.0 collective-permute-done.8.second
  40.8 0.0 collective-permute-done.6.other
  40.8 0.9 %finish.1 = f32[1,81000]{1,0:T(1,128)} custom-call(f32[640,128]{1,0:T(8,128)S(1)} %coefficient.1, f32[320,128]{1,0:T(8,128)S(1)} %join.1.mine, f32[320,128]{1,0:T(8,128)S(1)} %collective-permute-done.6.other, f32[640,128]{1,0:T(8,128)S(1)} %second_half.3.first, f32[640,128]{1,0:T(8,128)S(1)} %collective-permute-done.8.second), custom_call_target="tpu_custom_call" | custom-call | flops 1000000000 | bytes 1000000 | tf_op jit(solution)/shard_map/finish/pallas_call | solution.py:307
  (6 shorter events, 0.1 us)
Async XLA Ops:
  0.0 6.2 %copy-start = (f32[4,81000]{1,0:T(4,128)S(1)}, f32[4,81000]{1,0:T(4,128)}, u32[]{:S(2)}) copy-start(f32[4,81000]{1,0:T(4,128)} %ground.3) | copy-start | bytes 3888004
  1.6 4.1 %collective-permute-start = (f32[320,128]{1,0:T(8,128)S(1)}, f32[320,128]{1,0:T(8,128)S(1)}, u32[]{:S(2)}, u32[]{:S(2)}) collective-permute-start(f32[320,128]{1,0:T(8,128)S(1)} %get-tuple-element.21), channel_id=1, source_target_pairs={{0,4},{4,0},{8,12},{12,8},{16,20},{20,16},{24,28},{28,24},{1,5},{5... | collective-permute-start | bytes 491528 | tf_op jit(solution)/shard_map/ppermute | solution.py:337
  2.1 16.8 %collective-permute-start.7 = (f32[640,128]{1,0:T(8,128)S(1)}, f32[640,128]{1,0:T(8,128)S(1)}, u32[]{:S(2)}, u32[]{:S(2)}) collective-permute-start(f32[640,128]{1,0:T(8,128)S(1)} %get-tuple-element.26.response), channel_id=1, source_target_pairs={{4,0},{8,4},{12,8},{16,12},{20,16},{24,20},{28,24},{0,28},{5,1},{9... | collective-permute-start | bytes 983048 | tf_op jit(solution)/shard_map/ppermute | solution.py:394
  5.7 7.9 %copy-start.1 = (bf16[256,256]{1,0:T(8,128)(2,1)S(1)}, bf16[256,256]{1,0:T(8,128)(2,1)}, u32[]{:S(2)}) copy-start(bf16[256,256]{1,0:T(8,128)(2,1)} %constant.15.clone.refs_1_) | copy-start | bytes 393220
  5.7 7.9 %copy-start.2 = (bf16[256,256]{1,0:T(8,128)(2,1)S(1)}, bf16[256,256]{1,0:T(8,128)(2,1)}, u32[]{:S(2)}) copy-start(bf16[256,256]{1,0:T(8,128)(2,1)} %constant.14.clone.refs_0_) | copy-start | bytes 393220
  5.7 7.9 %copy-start.3 = (bf16[48,144]{1,0:T(8,128)(2,1)S(1)}, bf16[48,144]{1,0:T(8,128)(2,1)}, u32[]{:S(2)}) copy-start(bf16[48,144]{1,0:T(8,128)(2,1)} %constant.17.clone.refs_3_) | copy-start | bytes 41476
  5.7 7.9 %copy-start.4 = (bf16[48,144]{1,0:T(8,128)(2,1)S(1)}, bf16[48,144]{1,0:T(8,128)(2,1)}, u32[]{:S(2)}) copy-start(bf16[48,144]{1,0:T(8,128)(2,1)} %constant.16.clone.refs_2_) | copy-start | bytes 41476
  5.7 7.9 %copy-start.5 = (bf16[32,96]{1,0:T(8,128)(2,1)S(1)}, bf16[32,96]{1,0:T(8,128)(2,1)}, u32[]{:S(2)}) copy-start(bf16[32,96]{1,0:T(8,128)(2,1)} %constant.19.clone.refs_5_) | copy-start | bytes 18436
  5.8 7.9 %copy-start.6 = (bf16[32,96]{1,0:T(8,128)(2,1)S(1)}, bf16[32,96]{1,0:T(8,128)(2,1)}, u32[]{:S(2)}) copy-start(bf16[32,96]{1,0:T(8,128)(2,1)} %constant.18.clone.refs_4_) | copy-start | bytes 18436
  5.8 5.9 %collective-permute-start.1 = (f32[160,128]{1,0:T(8,128)S(1)}, f32[160,128]{1,0:T(8,128)S(1)}, u32[]{:S(2)}, u32[]{:S(2)}) collective-permute-start(f32[160,128]{1,0:T(8,128)S(1)} %get-tuple-element.23), channel_id=1, source_target_pairs={{0,8},{4,12},{8,0},{12,4},{16,24},{20,28},{24,16},{28,20},{1,9},{5... | collective-permute-start | bytes 245768 | tf_op jit(solution)/shard_map/ppermute | solution.py:337
  11.7 5.6 %collective-permute-start.2 = (f32[160,128]{1,0:T(8,128)S(1)}, f32[160,128]{1,0:T(8,128)S(1)}, u32[]{:S(2)}, u32[]{:S(2)}) collective-permute-start(f32[160,128]{1,0:T(8,128)S(1)} %add.4.mine), channel_id=1, source_target_pairs={{0,16},{4,20},{8,24},{12,28},{16,0},{20,4},{24,8},{28,12},{1,17},{... | collective-permute-start | bytes 245768 | tf_op jit(solution)/shard_map/ppermute | solution.py:337
  17.3 5.2 %collective-permute-start.3 = (f32[160,128]{1,0:T(8,128)S(1)}, f32[160,128]{1,0:T(8,128)S(1)}, u32[]{:S(2)}, u32[]{:S(2)}) collective-permute-start(f32[160,128]{1,0:T(8,128)S(1)} %add.5.mine), channel_id=1, source_target_pairs={{0,1},{1,0},{2,3},{3,2},{4,5},{5,4},{6,7},{7,6},{8,9},{9,8},{10,11... | collective-permute-start | bytes 245768 | tf_op jit(solution)/shard_map/ppermute | solution.py:337
  22.5 6.3 %collective-permute-start.4 = (f32[160,128]{1,0:T(8,128)S(1)}, f32[160,128]{1,0:T(8,128)S(1)}, u32[]{:S(2)}, u32[]{:S(2)}) collective-permute-start(f32[160,128]{1,0:T(8,128)S(1)} %add.6.mine), channel_id=1, source_target_pairs={{0,2},{1,3},{2,0},{3,1},{4,6},{5,7},{6,4},{7,5},{8,10},{9,11},{10,... | collective-permute-start | bytes 245768 | tf_op jit(solution)/shard_map/ppermute | solution.py:337
  28.7 12.1 %collective-permute-start.8 = (f32[640,128]{1,0:T(8,128)S(1)}, f32[640,128]{1,0:T(8,128)S(1)}, u32[]{:S(2)}, u32[]{:S(2)}) collective-permute-start(f32[640,128]{1,0:T(8,128)S(1)} %second_half.2), channel_id=1, source_target_pairs={{0,4},{4,8},{8,12},{12,16},{16,20},{20,24},{24,28},{28,0},{1,5},{5... | collective-permute-start | bytes 983048 | tf_op jit(solution)/shard_map/ppermute | solution.py:408
  28.8 5.4 %collective-permute-start.5 = (f32[160,128]{1,0:T(8,128)S(1)}, f32[160,128]{1,0:T(8,128)S(1)}, u32[]{:S(2)}, u32[]{:S(2)}) collective-permute-start(f32[160,128]{1,0:T(8,128)S(1)} %add.7.mine), channel_id=1, source_target_pairs={{0,8},{4,12},{8,0},{12,4},{16,24},{20,28},{24,16},{28,20},{1,9},{5... | collective-permute-start | bytes 245768 | tf_op jit(solution)/shard_map/ppermute | solution.py:337
  34.2 6.6 %collective-permute-start.6 = (f32[320,128]{1,0:T(8,128)S(1)}, f32[320,128]{1,0:T(8,128)S(1)}, u32[]{:S(2)}, u32[]{:S(2)}) collective-permute-start(f32[320,128]{1,0:T(8,128)S(1)} %join.1.mine), channel_id=1, source_target_pairs={{0,4},{4,0},{8,12},{12,8},{16,20},{20,16},{24,28},{28,24},{1,5},{5... | collective-permute-start | bytes 491528 | tf_op jit(solution)/shard_map/ppermute | solution.py:337

commit v4 on v3

--- a/solution.py
+++ b/solution.py
@@ -9,6 +9,7 @@
 from jax.experimental import pallas as pl
 from jax.experimental.pallas import tpu as pltpu
 from jax.sharding import PartitionSpec as P
+
 
 NX = 30
 NY = 45
@@ -292,11 +293,10 @@
     return values if space is None else pltpu.with_memory_space_constraint(values, space)
 
 
-def call(body, name, specs, shapes, scratch, microseconds, outs=None):
+def call(body, specs, shapes, scratch, microseconds):
     cost = pl.CostEstimate(flops=int(microseconds * 1e9), bytes_accessed=int(microseconds * 1e6), transcendentals=0)
     kernel = pl.pallas_call(
         body,
-        name=name,
         in_specs=specs,
         out_shape=[near(shape) for shape in shapes],
         out_specs=[VECTORS] * len(shapes),
@@ -344,33 +344,34 @@
     quarter = (stays.shape[0] // 2, LANES)
     other = swap(goes, "orb", 1)
     stays, goes = call(
-        functools.partial(share_kernel, 2), "share", [VECTORS] * 2, [quarter] * 2, [pltpu.VMEM(half, F32)], 0.1
+        functools.partial(share_kernel, 2), [VECTORS] * 2, [quarter] * 2, [pltpu.VMEM(half, F32)], 0.1
     )(stays, other)
     term, other = stays, swap(goes, "orb", 2)
-    for axis, distance in orb_bits[2:] + grid_bits:
-        term = call(add_kernel, "add", [VECTORS] * 2, [quarter], [], 0.1)(term, other)[0]
+    rest = orb_bits[2:] + grid_bits
+    for axis, distance in rest:
+        term = call(add_kernel, [VECTORS] * 2, [quarter], [], 0.1)(term, other)[0]
         other = swap(term, axis, distance)
-    term = call(add_kernel, "add", [VECTORS] * 2, [quarter], [], 0.1)(term, other)[0]
+    term = call(add_kernel, [VECTORS] * 2, [quarter], [], 0.1)(term, other)[0]
     other = swap(term, "orb", 2)
-    term = call(functools.partial(join_kernel, 2), "join", [VECTORS] * 2, [half], [], 0.1)(term, other)[0]
+    term = call(functools.partial(join_kernel, 2), [VECTORS] * 2, [half], [], 0.1)(term, other)[0]
     return term, swap(term, "orb", 1)
 
 
-def half_call(body, name, step, shapes, extra, values):
+def half_call(body, step, shapes, extra, values):
     flat, pitched = pltpu.VMEM((FLAT_ROWS, LANES), F32), pltpu.VMEM((PERIODS * (LINES + 1), LANES), F32)
     scratch = [flat, pitched, pltpu.SemaphoreType.DMA, pltpu.VMEM((YP * XP, LANES), F32)]
     scratch += [pltpu.VMEM((YP * XS, LANES), F32), pltpu.VMEM((XP * YS, LANES), F32)] + extra
     specs = [VECTORS] * 9 + [FAR] + [VECTORS] * (len(values) - 10)
-    return call(functools.partial(body, step), name, specs, shapes, scratch, 3)(*values)
+    return call(functools.partial(body, step), specs, shapes, scratch, 3)(*values)
 
 
 def first_half(step, *shared):
-    return half_call(first_half_kernel, "first_half", step, [(LINE_ROWS, LANES)] * 2, [], shared)
+    return half_call(first_half_kernel, step, [(LINE_ROWS, LANES)] * 2, [], shared)
 
 
 def second_half(step, *shared):
     line = pltpu.VMEM((LINE_ROWS, LANES), F32)
-    return half_call(second_half_kernel, "second_half", step, [(SENT_ROWS, LANES)], [line], shared)[0]
+    return half_call(second_half_kernel, step, [(SENT_ROWS, LANES)], [line], shared)[0]
 
 
 def per_device(ground_orbitals, occupation_signs, response_orbitals, window_offsets, ground_density):
@@ -387,34 +388,31 @@
     half = (SENT_ROWS // 2, LANES)
     scratch = [pltpu.VMEM((2, 1, POINTS), F32), pltpu.SMEM((4,), jnp.int32), pltpu.SMEM((1, 2), jnp.int32)]
     stays, goes, own, kept, weights = call(
-        prelude_kernel, "prelude", [FAR] * 4, [half] * 2 + [flat] * 2 + [(8, LANES)],
+        prelude_kernel, [FAR] * 4, [half] * 2 + [flat] * 2 + [(8, LANES)],
         scratch + [pltpu.VMEM(flat, F32), pltpu.SemaphoreType.DMA((6,))], 1,
     )(occupation_signs, window_offsets, ground_orbitals, response_orbitals)
     count = lax.axis_size("orb")
     visiting = lax.ppermute(kept, "orb", [((i + 1) % count, i) for i in range(count)])
     mine, other = summed_over_devices(stays, goes)
     low_lines, high_lines = call(
-        lines_kernel, "lines", [VECTORS], [(LINE_ROWS, LANES)] * 2,
+        lines_kernel, [VECTORS], [(LINE_ROWS, LANES)] * 2,
         [pltpu.VMEM((4, FLAT_ROWS, LANES), F32), pltpu.VMEM((PERIODS * (LINES + 1), LANES), F32),
          pltpu.SemaphoreType.DMA((4,))], 2,
     )(ground_orbitals)
     coefficient = call(
-        coefficient_kernel, "coefficient", [FAR, VECTORS], [flat],
+        coefficient_kernel, [FAR, VECTORS], [flat],
         [pltpu.VMEM((POINTS,), F32), pltpu.SemaphoreType.DMA], 1,
     )(ground_density, own)[0]
     values, partial = first_half(0, weights, low_lines, kept, *tables)
     away_values, away_partial = first_half(1, weights, low_lines, visiting, *tables)
     away = second_half(1, weights, high_lines, visiting, *tables, away_values, away_partial)
     second = lax.ppermute(away, "orb", [(i, (i + 1) % count) for i in range(count)])
-    values, away = lax.optimization_barrier((values, away))
     first = second_half(0, weights, high_lines, kept, *tables, values, partial)
-    return call(finish_kernel, "finish", [VECTORS] * 5, [(1, POINTS)], [pltpu.VMEM(flat, F32)], 1)(
+    return call(finish_kernel, [VECTORS] * 5, [(1, POINTS)], [pltpu.VMEM(flat, F32)], 1)(
         coefficient, mine, other, first, second
     )[0]
 
 
 def solution(mesh):
     placed = (P("orb", None), P("orb"), P(("orb", "grid"), None), P(("orb", "grid"), None), P())
-    return jax.shard_map(
-        per_device, mesh=mesh, in_specs=placed, out_specs=P(("orb", "grid"), None), check_vma=False
-    )
+    return jax.shard_map(per_device, mesh=mesh, in_specs=placed, out_specs=P(("orb", "grid"), None), check_vma=False)

time: 42 us -> 41.1 us (0.979)
  starting transfers between devices: 15.3 us -> 14.6 us
    ppermute x7, waiting for transfers between devices: 6.05 us -> 3.27 us  [swap(): return lax.ppermute(values, axis, [(i, i ^ distance) for i in range(count)])]
    ppermute x1, starting transfers between devices: 3.54 us -> 0.96 us  [per_device(): lax.ppermute(kept, 'orb', [((i + 1) % count, i) for i in range(count)])]
    ppermute x1, waiting for transfers between devices: 0.01 us -> 2.5 us  [per_device(): lax.ppermute(away, 'orb', [(i, (i + 1) % count) for i in range(count)])]
    ppermute x7, starting transfers between devices: 11.7 us -> 13.6 us  [swap(): return lax.ppermute(values, axis, [(i, i ^ distance) for i in range(count)])]
  transfers between devices with their start and end apart: 9 -> 9, of which waited for: 2 -> 4; matrix products, arithmetic and copies ran while one was open for 0% -> 0% of each run, Pallas kernels for 42% -> 43%
where the time goes in v4:
time: 41.1 us; the launch traced here: 40.7 us
  Pallas kernels  20.1 us (49%)
  starting transfers between devices  14.6 us (36%)
  waiting for transfers between devices  5.78 us (14%)
    pallas_call x14, Pallas kernels, call(): kernel(*(placed(v, spec) for spec, v in zip(specs, values)))  20.1 us
    ppermute x7, starting transfers between devices, swap(): return lax.ppermute(values, axis, [(i, i ^ distance) for i in range(count)])  13.6 us
    ppermute x7, waiting for transfers between devices, swap(): return lax.ppermute(values, axis, [(i, i ^ distance) for i in range(count)])  3.27 us
    ppermute x1, waiting for transfers between devices, per_device(): lax.ppermute(away, 'orb', [(i, (i + 1) % count) for i in range(count)])  2.5 us
    ppermute x1, starting transfers between devices, per_device(): lax.ppermute(kept, 'orb', [((i + 1) % count, i) for i in range(count)])  0.96 us
  transfers between devices with their start and end apart: 9, of which 4 were waited for; matrix products, arithmetic and copies ran while one was open for 0% of the time, Pallas kernels for 43%

profile of v4, /device:TPU:0, one launch (start us, length us, event | category | flops | bytes accessed | tf_op | source)
XLA Modules:
  0.0 40.7 jit_solution(7932475171491785628)
XLA Ops:
  0.0 0.0 copy-start
  0.0 1.5 %shard_map.118 = (f32[320,128]{1,0:T(8,128)S(1)}, f32[320,128]{1,0:T(8,128)S(1)}, f32[640,128]{1,0:T(8,128)S(1)}, f32[640,128]{1,0:T(8,128)S(1)}, f32[8,128]{1,0:T(8,128)S(1)}) custom-call(s32[4]{0:T(128)} %signs.1, s32[1,2]{1,0:T(1,128)} %offsets.1, f32[4,81000]{1,0:T(4,128)} %ground.3, f32[1,81000]{1,0:T(1,128)} %response.1), custom_call_target="tpu_custom_call" | custom-call | flops 1000000000 | bytes 1000000 | tf_op jit(solution)/shard_map/pallas_call | solution.py:307
  1.6 0.6 %collective-permute-start = (f32[320,128]{1,0:T(8,128)S(1)}, f32[320,128]{1,0:T(8,128)S(1)}, u32[]{:S(2)}, u32[]{:S(2)}) collective-permute-start(f32[320,128]{1,0:T(8,128)S(1)} %get-tuple-element.20), channel_id=1, source_target_pairs={{0,4},{4,0},{8,12},{12,8},{16,20},{20,16},{24,28},{28,24},{1,5},{5... | collective-permute-start | bytes 491528 | tf_op jit(solution)/shard_map/ppermute | solution.py:337
  2.1 1.0 %collective-permute-done.other = f32[320,128]{1,0:T(8,128)S(1)} collective-permute-done((f32[320,128]{1,0:T(8,128)S(1)}, f32[320,128]{1,0:T(8,128)S(1)}, u32[]{:S(2)}, u32[]{:S(2)}) %collective-permute-start) | collective-permute-done | bytes 163872 | tf_op jit(solution)/shard_map/ppermute | solution.py:337
  3.2 2.9 %collective-permute-start.1 = (f32[160,128]{1,0:T(8,128)S(1)}, f32[160,128]{1,0:T(8,128)S(1)}, u32[]{:S(2)}, u32[]{:S(2)}) collective-permute-start(f32[160,128]{1,0:T(8,128)S(1)} %get-tuple-element.22), channel_id=1, source_target_pairs={{0,8},{4,12},{8,0},{12,4},{16,24},{20,28},{24,16},{28,20},{1,9},{5... | collective-permute-start | bytes 245768 | tf_op jit(solution)/shard_map/ppermute | solution.py:337
  6.1 1.0 %collective-permute-start.7 = (f32[640,128]{1,0:T(8,128)S(1)}, f32[640,128]{1,0:T(8,128)S(1)}, u32[]{:S(2)}, u32[]{:S(2)}) collective-permute-start(f32[640,128]{1,0:T(8,128)S(1)} %get-tuple-element.25.response), channel_id=1, source_target_pairs={{4,0},{8,4},{12,8},{16,12},{20,16},{24,20},{28,24},{0,28},{5,1},{9... | collective-permute-start | bytes 983048 | tf_op jit(solution)/shard_map/ppermute | solution.py:395
  7.0 1.8 %collective-permute-done.1.other = f32[160,128]{1,0:T(8,128)S(1)} collective-permute-done((f32[160,128]{1,0:T(8,128)S(1)}, f32[160,128]{1,0:T(8,128)S(1)}, u32[]{:S(2)}, u32[]{:S(2)}) %collective-permute-start.1) | collective-permute-done | bytes 81952 | tf_op jit(solution)/shard_map/ppermute | solution.py:337
  8.8 0.0 copy-start.1
  8.9 0.0 copy-start.2
  8.9 0.0 copy-start.3
  8.9 0.0 copy-start.4
  8.9 0.0 copy-start.5
  8.9 0.0 copy-start.6
  8.9 1.8 %collective-permute-start.2 = (f32[160,128]{1,0:T(8,128)S(1)}, f32[160,128]{1,0:T(8,128)S(1)}, u32[]{:S(2)}, u32[]{:S(2)}) collective-permute-start(f32[160,128]{1,0:T(8,128)S(1)} %shard_map.121.mine), channel_id=1, source_target_pairs={{0,16},{4,20},{8,24},{12,28},{16,0},{20,4},{24,8},{28,12},{1,17},{... | collective-permute-start | bytes 245768 | tf_op jit(solution)/shard_map/ppermute | solution.py:337
  10.8 0.0 copy-done
  10.8 2.2 %shard_map.126 = (f32[1376,128]{1,0:T(8,128)S(1)}, f32[1376,128]{1,0:T(8,128)S(1)}) custom-call(f32[4,81000]{1,0:T(4,128)S(1)} %copy-done), custom_call_target="tpu_custom_call" | custom-call | flops 2000000000 | bytes 2000000 | tf_op jit(solution)/shard_map/pallas_call | solution.py:307
  13.0 0.4 %collective-permute-done.2.other = f32[160,128]{1,0:T(8,128)S(1)} collective-permute-done((f32[160,128]{1,0:T(8,128)S(1)}, f32[160,128]{1,0:T(8,128)S(1)}, u32[]{:S(2)}, u32[]{:S(2)}) %collective-permute-start.2) | collective-permute-done | bytes 81952 | tf_op jit(solution)/shard_map/ppermute | solution.py:337
  13.4 1.8 %collective-permute-start.3 = (f32[160,128]{1,0:T(8,128)S(1)}, f32[160,128]{1,0:T(8,128)S(1)}, u32[]{:S(2)}, u32[]{:S(2)}) collective-permute-start(f32[160,128]{1,0:T(8,128)S(1)} %shard_map.122.mine), channel_id=1, source_target_pairs={{0,1},{1,0},{2,3},{3,2},{4,5},{5,4},{6,7},{7,6},{8,9},{9,8},{10,11... | collective-permute-start | bytes 245768 | tf_op jit(solution)/shard_map/ppermute | solution.py:337
  15.3 0.0 copy-done.1
  15.3 0.0 copy-done.2
  15.3 0.0 copy-done.3
  15.3 0.0 copy-done.4
  15.3 0.0 copy-done.5
  15.3 0.0 copy-done.6
  15.3 3.6 %shard_map.127 = (f32[1376,128]{1,0:T(8,128)S(1)}, f32[1376,128]{1,0:T(8,128)S(1)}) custom-call(f32[8,128]{1,0:T(8,128)S(1)} %get-tuple-element.23.weights, f32[1376,128]{1,0:T(8,128)S(1)} %get-tuple-element.26.lines, f32[640,128]{1,0:T(8,128)S(1)} %get-tuple-element.25.response, bf16[256,256]{1,0:T(8,128)(2,1)S(1)} %copy-done.1, ...), custom_call_target="tpu_custom_call" | custom-call | flops 3000000000 | bytes 3000000 | tf_op jit(solution)/shard_map/pallas_call | solution.py:307
  18.9 0.0 collective-permute-done.3.other
  18.9 2.7 %collective-permute-start.4 = (f32[160,128]{1,0:T(8,128)S(1)}, f32[160,128]{1,0:T(8,128)S(1)}, u32[]{:S(2)}, u32[]{:S(2)}) collective-permute-start(f32[160,128]{1,0:T(8,128)S(1)} %shard_map.123.mine), channel_id=1, source_target_pairs={{0,2},{1,3},{2,0},{3,1},{4,6},{5,7},{6,4},{7,5},{8,10},{9,11},{10,... | collective-permute-start | bytes 245768 | tf_op jit(solution)/shard_map/ppermute | solution.py:337
  21.6 0.0 collective-permute-done.7.response
  21.6 3.6 %shard_map.129 = (f32[1376,128]{1,0:T(8,128)S(1)}, f32[1376,128]{1,0:T(8,128)S(1)}) custom-call(f32[8,128]{1,0:T(8,128)S(1)} %get-tuple-element.23.weights, f32[1376,128]{1,0:T(8,128)S(1)} %get-tuple-element.26.lines, f32[640,128]{1,0:T(8,128)S(1)} %collective-permute-done.7.response, bf16[256,256]{1,0:T(8,128)(2,1)S(1)} %copy-done.1, ...), custom_call_target="tpu_custom_call" | custom-call | flops 3000000000 | bytes 3000000 | tf_op jit(solution)/shard_map/pallas_call | solution.py:307
  25.2 0.0 collective-permute-done.4.other
  25.2 3.6 %collective-permute-start.5 = (f32[160,128]{1,0:T(8,128)S(1)}, f32[160,128]{1,0:T(8,128)S(1)}, u32[]{:S(2)}, u32[]{:S(2)}) collective-permute-start(f32[160,128]{1,0:T(8,128)S(1)} %shard_map.124.mine), channel_id=1, source_target_pairs={{0,8},{4,12},{8,0},{12,4},{16,24},{20,28},{24,16},{28,20},{1,9},{5... | collective-permute-start | bytes 245768 | tf_op jit(solution)/shard_map/ppermute | solution.py:337
  28.9 3.5 %shard_map.130 = f32[640,128]{1,0:T(8,128)S(1)} custom-call(f32[8,128]{1,0:T(8,128)S(1)} %get-tuple-element.23.weights, f32[1376,128]{1,0:T(8,128)S(1)} %get-tuple-element.24.lines, f32[640,128]{1,0:T(8,128)S(1)} %collective-permute-done.7.response, bf16[256,256]{1,0:T(8,128)(2,1)S(1)} %copy-done.1, bf16[256,256]{1,0:T(8,128)(2,1)S(1)} %copy-done.2, ...), custom_call_target="tpu_custom_call" | custom-call | flops 3000000000 | bytes 3000000 | tf_op jit(solution)/shard_map/pallas_call | solution.py:307
  32.4 0.1 collective-permute-start.8
  32.5 0.0 collective-permute-done.5.other
  32.5 0.2 collective-permute-start.6
  32.7 3.5 %shard_map.128.first = f32[640,128]{1,0:T(8,128)S(1)} custom-call(f32[8,128]{1,0:T(8,128)S(1)} %get-tuple-element.23.weights, f32[1376,128]{1,0:T(8,128)S(1)} %get-tuple-element.24.lines, f32[640,128]{1,0:T(8,128)S(1)} %get-tuple-element.25.response, bf16[256,256]{1,0:T(8,128)(2,1)S(1)} %copy-done.1, bf16[256,256]{1,0:T(8,128)(2,1)S(1)} %copy-done.2, ...), custom_call_target="tpu_custom_call" | custom-call | flops 3000000000 | bytes 3000000 | tf_op jit(solution)/shard_map/pallas_call | solution.py:307
  36.3 1.1 %shard_map.119.coefficient = f32[640,128]{1,0:T(8,128)S(1)} custom-call(f32[81000]{0:T(1024)} %density.1, f32[640,128]{1,0:T(8,128)S(1)} %get-tuple-element.18.own), custom_call_target="tpu_custom_call" | custom-call | flops 1000000000 | bytes 1000000 | tf_op jit(solution)/shard_map/pallas_call | solution.py:307
  37.4 2.5 %collective-permute-done.8.second = f32[640,128]{1,0:T(8,128)S(1)} collective-permute-done((f32[640,128]{1,0:T(8,128)S(1)}, f32[640,128]{1,0:T(8,128)S(1)}, u32[]{:S(2)}, u32[]{:S(2)}) %collective-permute-start.8) | collective-permute-done | bytes 327712 | tf_op jit(solution)/shard_map/ppermute | solution.py:409
  39.9 0.0 collective-permute-done.6.other
  39.9 0.9 %shard_map.131 = f32[1,81000]{1,0:T(1,128)} custom-call(f32[640,128]{1,0:T(8,128)S(1)} %shard_map.119.coefficient, f32[320,128]{1,0:T(8,128)S(1)} %shard_map.125.mine, f32[320,128]{1,0:T(8,128)S(1)} %collective-permute-done.6.other, f32[640,128]{1,0:T(8,128)S(1)} %shard_map.128.first, f32[640,128]{1,0:T(8,128)S(1)} %collective-permute-done.8.second), custom_call_target="tpu_custom_call" | custom-call | flops 1000000000 | bytes 1000000 | tf_op jit(solution)/shard_map/pallas_call | solution.py:307
  (6 shorter events, 0.1 us)
Async XLA Ops:
  0.0 10.8 %copy-start = (f32[4,81000]{1,0:T(4,128)S(1)}, f32[4,81000]{1,0:T(4,128)}, u32[]{:S(2)}) copy-start(f32[4,81000]{1,0:T(4,128)} %ground.3) | copy-start | bytes 3888004
  1.6 1.6 %collective-permute-start = (f32[320,128]{1,0:T(8,128)S(1)}, f32[320,128]{1,0:T(8,128)S(1)}, u32[]{:S(2)}, u32[]{:S(2)}) collective-permute-start(f32[320,128]{1,0:T(8,128)S(1)} %get-tuple-element.20), channel_id=1, source_target_pairs={{0,4},{4,0},{8,12},{12,8},{16,20},{20,16},{24,28},{28,24},{1,5},{5... | collective-permute-start | bytes 491528 | tf_op jit(solution)/shard_map/ppermute | solution.py:337
  3.2 5.7 %collective-permute-start.1 = (f32[160,128]{1,0:T(8,128)S(1)}, f32[160,128]{1,0:T(8,128)S(1)}, u32[]{:S(2)}, u32[]{:S(2)}) collective-permute-start(f32[160,128]{1,0:T(8,128)S(1)} %get-tuple-element.22), channel_id=1, source_target_pairs={{0,8},{4,12},{8,0},{12,4},{16,24},{20,28},{24,16},{28,20},{1,9},{5... | collective-permute-start | bytes 245768 | tf_op jit(solution)/shard_map/ppermute | solution.py:337
  6.1 15.5 %collective-permute-start.7 = (f32[640,128]{1,0:T(8,128)S(1)}, f32[640,128]{1,0:T(8,128)S(1)}, u32[]{:S(2)}, u32[]{:S(2)}) collective-permute-start(f32[640,128]{1,0:T(8,128)S(1)} %get-tuple-element.25.response), channel_id=1, source_target_pairs={{4,0},{8,4},{12,8},{16,12},{20,16},{24,20},{28,24},{0,28},{5,1},{9... | collective-permute-start | bytes 983048 | tf_op jit(solution)/shard_map/ppermute | solution.py:395
  8.8 6.4 %copy-start.1 = (bf16[256,256]{1,0:T(8,128)(2,1)S(1)}, bf16[256,256]{1,0:T(8,128)(2,1)}, u32[]{:S(2)}) copy-start(bf16[256,256]{1,0:T(8,128)(2,1)} %constant.14.clone.refs_0_) | copy-start | bytes 393220
  8.9 6.4 %copy-start.2 = (bf16[256,256]{1,0:T(8,128)(2,1)S(1)}, bf16[256,256]{1,0:T(8,128)(2,1)}, u32[]{:S(2)}) copy-start(bf16[256,256]{1,0:T(8,128)(2,1)} %constant.15.clone.refs_1_) | copy-start | bytes 393220
  8.9 6.4 %copy-start.3 = (bf16[48,144]{1,0:T(8,128)(2,1)S(1)}, bf16[48,144]{1,0:T(8,128)(2,1)}, u32[]{:S(2)}) copy-start(bf16[48,144]{1,0:T(8,128)(2,1)} %constant.16.clone.refs_2_) | copy-start | bytes 41476
  8.9 6.4 %copy-start.4 = (bf16[48,144]{1,0:T(8,128)(2,1)S(1)}, bf16[48,144]{1,0:T(8,128)(2,1)}, u32[]{:S(2)}) copy-start(bf16[48,144]{1,0:T(8,128)(2,1)} %constant.17.clone.refs_3_) | copy-start | bytes 41476
  8.9 6.4 %copy-start.5 = (bf16[32,96]{1,0:T(8,128)(2,1)S(1)}, bf16[32,96]{1,0:T(8,128)(2,1)}, u32[]{:S(2)}) copy-start(bf16[32,96]{1,0:T(8,128)(2,1)} %constant.18.clone.refs_4_) | copy-start | bytes 18436
  8.9 6.4 %copy-start.6 = (bf16[32,96]{1,0:T(8,128)(2,1)S(1)}, bf16[32,96]{1,0:T(8,128)(2,1)}, u32[]{:S(2)}) copy-start(bf16[32,96]{1,0:T(8,128)(2,1)} %constant.19.clone.refs_5_) | copy-start | bytes 18436
  8.9 4.5 %collective-permute-start.2 = (f32[160,128]{1,0:T(8,128)S(1)}, f32[160,128]{1,0:T(8,128)S(1)}, u32[]{:S(2)}, u32[]{:S(2)}) collective-permute-start(f32[160,128]{1,0:T(8,128)S(1)} %shard_map.121.mine), channel_id=1, source_target_pairs={{0,16},{4,20},{8,24},{12,28},{16,0},{20,4},{24,8},{28,12},{1,17},{... | collective-permute-start | bytes 245768 | tf_op jit(solution)/shard_map/ppermute | solution.py:337
  13.4 5.5 %collective-permute-start.3 = (f32[160,128]{1,0:T(8,128)S(1)}, f32[160,128]{1,0:T(8,128)S(1)}, u32[]{:S(2)}, u32[]{:S(2)}) collective-permute-start(f32[160,128]{1,0:T(8,128)S(1)} %shard_map.122.mine), channel_id=1, source_target_pairs={{0,1},{1,0},{2,3},{3,2},{4,5},{5,4},{6,7},{7,6},{8,9},{9,8},{10,11... | collective-permute-start | bytes 245768 | tf_op jit(solution)/shard_map/ppermute | solution.py:337
  18.9 6.3 %collective-permute-start.4 = (f32[160,128]{1,0:T(8,128)S(1)}, f32[160,128]{1,0:T(8,128)S(1)}, u32[]{:S(2)}, u32[]{:S(2)}) collective-permute-start(f32[160,128]{1,0:T(8,128)S(1)} %shard_map.123.mine), channel_id=1, source_target_pairs={{0,2},{1,3},{2,0},{3,1},{4,6},{5,7},{6,4},{7,5},{8,10},{9,11},{10,... | collective-permute-start | bytes 245768 | tf_op jit(solution)/shard_map/ppermute | solution.py:337
  25.2 7.3 %collective-permute-start.5 = (f32[160,128]{1,0:T(8,128)S(1)}, f32[160,128]{1,0:T(8,128)S(1)}, u32[]{:S(2)}, u32[]{:S(2)}) collective-permute-start(f32[160,128]{1,0:T(8,128)S(1)} %shard_map.124.mine), channel_id=1, source_target_pairs={{0,8},{4,12},{8,0},{12,4},{16,24},{20,28},{24,16},{28,20},{1,9},{5... | collective-permute-start | bytes 245768 | tf_op jit(solution)/shard_map/ppermute | solution.py:337
  32.4 7.5 %collective-permute-start.8 = (f32[640,128]{1,0:T(8,128)S(1)}, f32[640,128]{1,0:T(8,128)S(1)}, u32[]{:S(2)}, u32[]{:S(2)}) collective-permute-start(f32[640,128]{1,0:T(8,128)S(1)} %shard_map.130), channel_id=1, source_target_pairs={{0,4},{4,8},{8,12},{12,16},{16,20},{20,24},{24,28},{28,0},{1,5},{5... | collective-permute-start | bytes 983048 | tf_op jit(solution)/shard_map/ppermute | solution.py:409
  32.5 7.3 %collective-permute-start.6 = (f32[320,128]{1,0:T(8,128)S(1)}, f32[320,128]{1,0:T(8,128)S(1)}, u32[]{:S(2)}, u32[]{:S(2)}) collective-permute-start(f32[320,128]{1,0:T(8,128)S(1)} %shard_map.125.mine), channel_id=1, source_target_pairs={{0,4},{4,0},{8,12},{12,8},{16,20},{20,16},{24,28},{28,24},{1,5},{5... | collective-permute-start | bytes 491528 | tf_op jit(solution)/shard_map/ppermute | solution.py:337

commit v5 on v4

--- a/solution.py
+++ b/solution.py
@@ -25,7 +25,6 @@
 POINTS = NX * NY * NZ
 XP = 32
 YP = 48
-ZP = LANES // 2
 XS = XP + 1
 YS = YP + 1
 LINES = math.lcm(NZ, LANES) // NZ
@@ -57,7 +56,7 @@
 
 
 def lane_table(matrix):
-    high, low = (np.kron(np.eye(2, dtype=jnp.bfloat16), padded(part, ZP)) for part in split_table(matrix))
+    high, low = (padded(np.kron(np.eye(2, dtype=jnp.bfloat16), part), LANES) for part in split_table(matrix))
     return np.block([[high, low], [high, np.zeros_like(low)]])
 
 
@@ -74,8 +73,8 @@
         return waves * waves
 
     squared = squares(NX)[None, :, None] + squares(NY)[:, None, None] + squares(NZ)[None, None, :]
-    table = np.zeros((YP, XP, 2, ZP), np.float32)
-    table[:NY, :NX, :, :NZ] = (4.0 * math.pi / (squared + SCREEN * SCREEN))[:, :, None, :]
+    table = np.zeros((YP, XP, LANES), np.float32)
+    table[:NY, :NX, : 2 * NZ] = np.tile(4.0 * math.pi / (squared + SCREEN * SCREEN), (1, 1, 2))
     return table.reshape(YP * XP, LANES)
 
 
@@ -108,21 +107,27 @@
     return pltpu.roll(values, shift, 1) if shift else values
 
 
-def line_of(flat, line, place):
+def two_lines(flat, line, places):
     chunk, start = divmod(NZ * line, LANES)
-    first = turned(flat[pl.ds(chunk, PERIODS, stride=CHUNKS), :], place - start)
-    if start + NZ <= LANES:
-        return first
-    second = turned(flat[pl.ds(chunk + 1, PERIODS, stride=CHUNKS), :], place - start)
-    return jnp.where(lane_ids(PERIODS) < place + LANES - start, first, second)
+    value = flat[pl.ds(chunk, PERIODS, stride=CHUNKS), :]
+    if start + 2 * NZ > LANES:
+        after = flat[pl.ds(chunk + 1, PERIODS, stride=CHUNKS), :]
+        value = jnp.where(lane_ids(PERIODS) >= start, value, after)
+    return [turned(value, place - start) for place in places]
 
 
 def to_lines(left, right, lines, pitched):
     ids = lane_ids(PERIODS)
-    for line in range(LINES):
-        low, high = line_of(left, line, 0), line_of(right, line, ZP)
-        both = jnp.where(ids < NZ, low, jnp.where((ids >= ZP) & (ids < ZP + NZ), high, 0.0))
-        pitched[pl.ds(line, PERIODS, stride=LINES + 1), :] = both
+    for line in range(0, LINES, 2):
+        if left is right:
+            middle, late, early = two_lines(left, line, (0, NZ, -NZ))
+            pairs = (jnp.where(ids < NZ, middle, late), jnp.where(ids < NZ, early, middle))
+        else:
+            (low, next_low), (high, next_high) = two_lines(left, line, (0, -NZ)), two_lines(right, line, (NZ, 0))
+            pairs = (jnp.where(ids < NZ, low, high), jnp.where(ids < NZ, next_low, next_high))
+        for place, pair in enumerate(pairs):
+            pair = jnp.where(ids < 2 * NZ, pair, 0.0)
+            pitched[pl.ds(line + place, PERIODS, stride=LINES + 1), :] = pair
     for period in range(PERIODS):
         lines[pl.ds(period * LINES, LINES), :] = pitched[pl.ds(period * (LINES + 1), LINES), :]
 
@@ -178,7 +183,7 @@
         kept[pl.ds(SENT_ROWS - 2 + step, 1), :] = jnp.full((1, LANES), offset[0, step].astype(F32))
     ids = lane_ids(1)
     for half in range(2):
-        pair = jnp.where(ids < ZP, sign[2 * half].astype(F32), sign[2 * half + 1].astype(F32))
+        pair = jnp.where(ids < NZ, sign[2 * half].astype(F32), sign[2 * half + 1].astype(F32))
         weights[pl.ds(half, 1), :] = pair
 
 
@@ -210,13 +215,13 @@
 def solve_half(half, step, weights, lines, values, response, tables, kernel_copy, scratch, total, prior):
     kernel, waves, turned_waves = scratch
     z_table, z_back, y_table, y_back, x_table, x_back = (table[...] for table in tables)
-    group = 15
     for x in range(NX, XP):
         waves[pl.ds(x, YP, stride=XS), :] = jnp.zeros((YP, LANES), F32)
     for y in range(NY, YP):
         turned_waves[pl.ds(y, XP, stride=YS), :] = jnp.zeros((XP, LANES), F32)
 
     def forward(x):
+        group = 15
         spots = [pl.ds((x + u) * NY, YP) for u in range(group)]
         value = lane_product(jnp.concatenate([lines[spot, :] * values[spot, :] for spot in spots], 0), z_table)
         value = row_product(y_table, jnp.concatenate([value[u * YP : (u + 1) * YP] for u in range(group)], 1))
@@ -224,17 +229,19 @@
             waves[pl.ds(x + u, YP, stride=XS), :] = value[:, u * LANES : (u + 1) * LANES]
 
     def middle(y):
+        group = 45
         spots = [pl.ds(pl.multiple_of((y + u) * XP, XP), XP) for u in range(group)]
         value = row_product(x_table, jnp.concatenate([waves[pl.ds((y + u) * XS, XP), :] for u in range(group)], 1))
         value = row_product(x_back, value * jnp.concatenate([kernel[spot, :] for spot in spots], 1))
         for u in range(group):
             turned_waves[pl.ds(y + u, XP, stride=YS), :] = value[:, u * LANES : (u + 1) * LANES]
 
-    orbital = 2 * half + (lane_ids(1) >= ZP).astype(jnp.int32)
+    orbital = 2 * half + (lane_ids(1) >= NZ).astype(jnp.int32)
     offset = response[pl.ds(SENT_ROWS - 2 + step, 1), :]
     factor = jnp.where(orbital.astype(F32) >= offset, weights[pl.ds(half, 1), :], 0.0)
 
     def backward(x):
+        group = 30
         spots = [pl.ds((x + u) * YS, YP) for u in range(group)]
         value = row_product(y_back, jnp.concatenate([turned_waves[spot, :] for spot in spots], 1))
         value = jnp.concatenate([value[:, u * LANES : (u + 1) * LANES] for u in range(group)], 0)
@@ -244,13 +251,13 @@
             part = value[u * YP : (u + 1) * YP] * (lines[spot, :] * factor)
             if prior is not None:
                 part += prior[spot, :]
-                part += pltpu.roll(part, ZP, 1)
+                part += pltpu.roll(part, LANES - NZ, 1)
             total[spot, :] = part
 
-    grouped(NX, group, forward)
+    grouped(NX, 15, forward)
     kernel_copy.wait()
-    grouped(NY, group, middle)
-    grouped(NX, group, backward)
+    grouped(NY, 45, middle)
+    grouped(NX, 30, backward)
 
 
 def first_half_kernel(step, weights, lines, response, *refs):
@@ -372,6 +379,14 @@
 def second_half(step, *shared):
     line = pltpu.VMEM((LINE_ROWS, LANES), F32)
     return half_call(second_half_kernel, step, [(SENT_ROWS, LANES)], [line], shared)[0]
+
+
+def lines_call(ground):
+    return call(
+        lines_kernel, [VECTORS], [(LINE_ROWS, LANES)] * 2,
+        [pltpu.VMEM((4, FLAT_ROWS, LANES), F32), pltpu.VMEM((PERIODS * (LINES + 1), LANES), F32),
+         pltpu.SemaphoreType.DMA((4,))], 2,
+    )(ground)
 
 
 def per_device(ground_orbitals, occupation_signs, response_orbitals, window_offsets, ground_density):
@@ -394,11 +409,7 @@
     count = lax.axis_size("orb")
     visiting = lax.ppermute(kept, "orb", [((i + 1) % count, i) for i in range(count)])
     mine, other = summed_over_devices(stays, goes)
-    low_lines, high_lines = call(
-        lines_kernel, [VECTORS], [(LINE_ROWS, LANES)] * 2,
-        [pltpu.VMEM((4, FLAT_ROWS, LANES), F32), pltpu.VMEM((PERIODS * (LINES + 1), LANES), F32),
-         pltpu.SemaphoreType.DMA((4,))], 2,
-    )(ground_orbitals)
+    low_lines, high_lines = lines_call(ground_orbitals)
     coefficient = call(
         coefficient_kernel, [FAR, VECTORS], [flat],
         [pltpu.VMEM((POINTS,), F32), pltpu.SemaphoreType.DMA], 1,

time: 41.1 us -> 38.3 us (0.932)
  Pallas kernels: 20.1 us -> 15.9 us
  waiting for transfers between devices: 5.78 us -> 7.08 us
    pallas_call x14, Pallas kernels: 20.1 us -> 15.9 us  [call(): kernel(*(placed(v, spec) for spec, v in zip(specs, values)))]
    ppermute x1, waiting for transfers between devices: 2.5 us -> 3.38 us  [per_device(): lax.ppermute(away, 'orb', [(i, (i + 1) % count) for i in range(count)])]
    ppermute x7, waiting for transfers between devices: 3.27 us -> 3.7 us  [swap(): return lax.ppermute(values, axis, [(i, i ^ distance) for i in range(count)])]
  transfers between devices with their start and end apart: 9 -> 9, of which waited for: 4 -> 5; matrix products, arithmetic and copies ran while one was open for 0% -> 0% of each run, Pallas kernels for 43% -> 35%
where the time goes in v5:
time: 38.3 us; the launch traced here: 38 us
  Pallas kernels  15.9 us (42%)
  starting transfers between devices  14.8 us (39%)
  waiting for transfers between devices  7.08 us (18%)
    pallas_call x14, Pallas kernels, call(): kernel(*(placed(v, spec) for spec, v in zip(specs, values)))  15.9 us
    ppermute x7, starting transfers between devices, swap(): return lax.ppermute(values, axis, [(i, i ^ distance) for i in range(count)])  13.8 us
    ppermute x7, waiting for transfers between devices, swap(): return lax.ppermute(values, axis, [(i, i ^ distance) for i in range(count)])  3.7 us
    ppermute x1, waiting for transfers between devices, per_device(): lax.ppermute(away, 'orb', [(i, (i + 1) % count) for i in range(count)])  3.38 us
    ppermute x1, starting transfers between devices, per_device(): lax.ppermute(kept, 'orb', [((i + 1) % count, i) for i in range(count)])  0.96 us
  transfers between devices with their start and end apart: 9, of which 5 were waited for; matrix products, arithmetic and copies ran while one was open for 0% of the time, Pallas kernels for 35%

profile of v5, /device:TPU:0, one launch (start us, length us, event | category | flops | bytes accessed | tf_op | source)
XLA Modules:
  0.0 38.0 jit_solution(11607762571790934626)
XLA Ops:
  0.0 0.0 copy-start
  0.0 1.5 %shard_map.118 = (f32[320,128]{1,0:T(8,128)S(1)}, f32[320,128]{1,0:T(8,128)S(1)}, f32[640,128]{1,0:T(8,128)S(1)}, f32[640,128]{1,0:T(8,128)S(1)}, f32[8,128]{1,0:T(8,128)S(1)}) custom-call(s32[4]{0:T(128)} %signs.1, s32[1,2]{1,0:T(1,128)} %offsets.1, f32[4,81000]{1,0:T(4,128)} %ground.3, f32[1,81000]{1,0:T(1,128)} %response.1), custom_call_target="tpu_custom_call" | custom-call | flops 1000000000 | bytes 1000000 | tf_op jit(solution)/shard_map/pallas_call | solution.py:314
  1.6 0.6 %collective-permute-start = (f32[320,128]{1,0:T(8,128)S(1)}, f32[320,128]{1,0:T(8,128)S(1)}, u32[]{:S(2)}, u32[]{:S(2)}) collective-permute-start(f32[320,128]{1,0:T(8,128)S(1)} %get-tuple-element.20), channel_id=1, source_target_pairs={{0,4},{4,0},{8,12},{12,8},{16,20},{20,16},{24,28},{28,24},{1,5},{5... | collective-permute-start | bytes 491528 | tf_op jit(solution)/shard_map/ppermute | solution.py:344
  2.1 1.0 %collective-permute-done.other = f32[320,128]{1,0:T(8,128)S(1)} collective-permute-done((f32[320,128]{1,0:T(8,128)S(1)}, f32[320,128]{1,0:T(8,128)S(1)}, u32[]{:S(2)}, u32[]{:S(2)}) %collective-permute-start) | collective-permute-done | bytes 163872 | tf_op jit(solution)/shard_map/ppermute | solution.py:344
  3.2 2.9 %collective-permute-start.1 = (f32[160,128]{1,0:T(8,128)S(1)}, f32[160,128]{1,0:T(8,128)S(1)}, u32[]{:S(2)}, u32[]{:S(2)}) collective-permute-start(f32[160,128]{1,0:T(8,128)S(1)} %get-tuple-element.22), channel_id=1, source_target_pairs={{0,8},{4,12},{8,0},{12,4},{16,24},{20,28},{24,16},{28,20},{1,9},{5... | collective-permute-start | bytes 245768 | tf_op jit(solution)/shard_map/ppermute | solution.py:344
  6.1 1.0 %collective-permute-start.7 = (f32[640,128]{1,0:T(8,128)S(1)}, f32[640,128]{1,0:T(8,128)S(1)}, u32[]{:S(2)}, u32[]{:S(2)}) collective-permute-start(f32[640,128]{1,0:T(8,128)S(1)} %get-tuple-element.25.response), channel_id=1, source_target_pairs={{4,0},{8,4},{12,8},{16,12},{20,16},{24,20},{28,24},{0,28},{5,1},{9... | collective-permute-start | bytes 983048 | tf_op jit(solution)/shard_map/ppermute | solution.py:410
  7.0 1.8 %collective-permute-done.1.other = f32[160,128]{1,0:T(8,128)S(1)} collective-permute-done((f32[160,128]{1,0:T(8,128)S(1)}, f32[160,128]{1,0:T(8,128)S(1)}, u32[]{:S(2)}, u32[]{:S(2)}) %collective-permute-start.1) | collective-permute-done | bytes 81952 | tf_op jit(solution)/shard_map/ppermute | solution.py:344
  8.8 0.0 copy-start.1
  8.9 0.0 copy-start.2
  8.9 0.0 copy-start.3
  8.9 0.0 copy-start.4
  8.9 0.0 copy-start.5
  8.9 0.0 copy-start.6
  8.9 1.8 %collective-permute-start.2 = (f32[160,128]{1,0:T(8,128)S(1)}, f32[160,128]{1,0:T(8,128)S(1)}, u32[]{:S(2)}, u32[]{:S(2)}) collective-permute-start(f32[160,128]{1,0:T(8,128)S(1)} %shard_map.121.mine), channel_id=1, source_target_pairs={{0,16},{4,20},{8,24},{12,28},{16,0},{20,4},{24,8},{28,12},{1,17},{... | collective-permute-start | bytes 245768 | tf_op jit(solution)/shard_map/ppermute | solution.py:344
  10.8 0.0 copy-done
  10.8 1.9 %shard_map.126 = (f32[1376,128]{1,0:T(8,128)S(1)}, f32[1376,128]{1,0:T(8,128)S(1)}) custom-call(f32[4,81000]{1,0:T(4,128)S(1)} %copy-done), custom_call_target="tpu_custom_call" | custom-call | flops 2000000000 | bytes 2000000 | tf_op jit(solution)/shard_map/pallas_call | solution.py:314
  12.7 0.8 %collective-permute-done.2.other = f32[160,128]{1,0:T(8,128)S(1)} collective-permute-done((f32[160,128]{1,0:T(8,128)S(1)}, f32[160,128]{1,0:T(8,128)S(1)}, u32[]{:S(2)}, u32[]{:S(2)}) %collective-permute-start.2) | collective-permute-done | bytes 81952 | tf_op jit(solution)/shard_map/ppermute | solution.py:344
  13.4 1.8 %collective-permute-start.3 = (f32[160,128]{1,0:T(8,128)S(1)}, f32[160,128]{1,0:T(8,128)S(1)}, u32[]{:S(2)}, u32[]{:S(2)}) collective-permute-start(f32[160,128]{1,0:T(8,128)S(1)} %shard_map.122.mine), channel_id=1, source_target_pairs={{0,1},{1,0},{2,3},{3,2},{4,5},{5,4},{6,7},{7,6},{8,9},{9,8},{10,11... | collective-permute-start | bytes 245768 | tf_op jit(solution)/shard_map/ppermute | solution.py:344
  15.3 0.0 copy-done.1
  15.3 0.0 copy-done.2
  15.3 0.0 copy-done.3
  15.3 0.0 copy-done.4
  15.3 0.0 copy-done.5
  15.3 0.0 copy-done.6
  15.3 2.5 %shard_map.127 = (f32[1376,128]{1,0:T(8,128)S(1)}, f32[1376,128]{1,0:T(8,128)S(1)}) custom-call(f32[8,128]{1,0:T(8,128)S(1)} %get-tuple-element.23.weights, f32[1376,128]{1,0:T(8,128)S(1)} %get-tuple-element.26.lines, f32[640,128]{1,0:T(8,128)S(1)} %get-tuple-element.25.response, bf16[256,256]{1,0:T(8,128)(2,1)S(1)} %copy-done.1, ...), custom_call_target="tpu_custom_call" | custom-call | flops 3000000000 | bytes 3000000 | tf_op jit(solution)/shard_map/pallas_call | solution.py:314
  17.8 0.1 collective-permute-done.3.other
  18.0 3.3 %collective-permute-start.4 = (f32[160,128]{1,0:T(8,128)S(1)}, f32[160,128]{1,0:T(8,128)S(1)}, u32[]{:S(2)}, u32[]{:S(2)}) collective-permute-start(f32[160,128]{1,0:T(8,128)S(1)} %shard_map.123.mine), channel_id=1, source_target_pairs={{0,2},{1,3},{2,0},{3,1},{4,6},{5,7},{6,4},{7,5},{8,10},{9,11},{10,... | collective-permute-start | bytes 245768 | tf_op jit(solution)/shard_map/ppermute | solution.py:344
  21.3 0.0 collective-permute-done.7.response
  21.3 2.5 %shard_map.129 = (f32[1376,128]{1,0:T(8,128)S(1)}, f32[1376,128]{1,0:T(8,128)S(1)}) custom-call(f32[8,128]{1,0:T(8,128)S(1)} %get-tuple-element.23.weights, f32[1376,128]{1,0:T(8,128)S(1)} %get-tuple-element.26.lines, f32[640,128]{1,0:T(8,128)S(1)} %collective-permute-done.7.response, bf16[256,256]{1,0:T(8,128)(2,1)S(1)} %copy-done.1, ...), custom_call_target="tpu_custom_call" | custom-call | flops 3000000000 | bytes 3000000 | tf_op jit(solution)/shard_map/pallas_call | solution.py:314
  23.8 0.0 collective-permute-done.4.other
  23.8 3.2 %collective-permute-start.5 = (f32[160,128]{1,0:T(8,128)S(1)}, f32[160,128]{1,0:T(8,128)S(1)}, u32[]{:S(2)}, u32[]{:S(2)}) collective-permute-start(f32[160,128]{1,0:T(8,128)S(1)} %shard_map.124.mine), channel_id=1, source_target_pairs={{0,8},{4,12},{8,0},{12,4},{16,24},{20,28},{24,16},{28,20},{1,9},{5... | collective-permute-start | bytes 245768 | tf_op jit(solution)/shard_map/ppermute | solution.py:344
  27.0 2.7 %shard_map.130 = f32[640,128]{1,0:T(8,128)S(1)} custom-call(f32[8,128]{1,0:T(8,128)S(1)} %get-tuple-element.23.weights, f32[1376,128]{1,0:T(8,128)S(1)} %get-tuple-element.24.lines, f32[640,128]{1,0:T(8,128)S(1)} %collective-permute-done.7.response, bf16[256,256]{1,0:T(8,128)(2,1)S(1)} %copy-done.1, bf16[256,256]{1,0:T(8,128)(2,1)S(1)} %copy-done.2, ...), custom_call_target="tpu_custom_call" | custom-call | flops 3000000000 | bytes 3000000 | tf_op jit(solution)/shard_map/pallas_call | solution.py:314
  29.7 0.1 collective-permute-start.8
  29.8 0.0 collective-permute-done.5.other
  29.8 0.2 collective-permute-start.6
  30.0 2.7 %shard_map.128.first = f32[640,128]{1,0:T(8,128)S(1)} custom-call(f32[8,128]{1,0:T(8,128)S(1)} %get-tuple-element.23.weights, f32[1376,128]{1,0:T(8,128)S(1)} %get-tuple-element.24.lines, f32[640,128]{1,0:T(8,128)S(1)} %get-tuple-element.25.response, bf16[256,256]{1,0:T(8,128)(2,1)S(1)} %copy-done.1, bf16[256,256]{1,0:T(8,128)(2,1)S(1)} %copy-done.2, ...), custom_call_target="tpu_custom_call" | custom-call | flops 3000000000 | bytes 3000000 | tf_op jit(solution)/shard_map/pallas_call | solution.py:314
  32.7 1.1 %shard_map.119.coefficient = f32[640,128]{1,0:T(8,128)S(1)} custom-call(f32[81000]{0:T(1024)} %density.1, f32[640,128]{1,0:T(8,128)S(1)} %get-tuple-element.18.own), custom_call_target="tpu_custom_call" | custom-call | flops 1000000000 | bytes 1000000 | tf_op jit(solution)/shard_map/pallas_call | solution.py:314
  33.8 3.4 %collective-permute-done.8.second = f32[640,128]{1,0:T(8,128)S(1)} collective-permute-done((f32[640,128]{1,0:T(8,128)S(1)}, f32[640,128]{1,0:T(8,128)S(1)}, u32[]{:S(2)}, u32[]{:S(2)}) %collective-permute-start.8) | collective-permute-done | bytes 327712 | tf_op jit(solution)/shard_map/ppermute | solution.py:420
  37.1 0.0 collective-permute-done.6.other
  37.1 0.9 %shard_map.131 = f32[1,81000]{1,0:T(1,128)} custom-call(f32[640,128]{1,0:T(8,128)S(1)} %shard_map.119.coefficient, f32[320,128]{1,0:T(8,128)S(1)} %shard_map.125.mine, f32[320,128]{1,0:T(8,128)S(1)} %collective-permute-done.6.other, f32[640,128]{1,0:T(8,128)S(1)} %shard_map.128.first, f32[640,128]{1,0:T(8,128)S(1)} %collective-permute-done.8.second), custom_call_target="tpu_custom_call" | custom-call | flops 1000000000 | bytes 1000000 | tf_op jit(solution)/shard_map/pallas_call | solution.py:314
  (6 shorter events, 0.1 us)
Async XLA Ops:
  0.0 10.8 %copy-start = (f32[4,81000]{1,0:T(4,128)S(1)}, f32[4,81000]{1,0:T(4,128)}, u32[]{:S(2)}) copy-start(f32[4,81000]{1,0:T(4,128)} %ground.3) | copy-start | bytes 3888004
  1.6 1.6 %collective-permute-start = (f32[320,128]{1,0:T(8,128)S(1)}, f32[320,128]{1,0:T(8,128)S(1)}, u32[]{:S(2)}, u32[]{:S(2)}) collective-permute-start(f32[320,128]{1,0:T(8,128)S(1)} %get-tuple-element.20), channel_id=1, source_target_pairs={{0,4},{4,0},{8,12},{12,8},{16,20},{20,16},{24,28},{28,24},{1,5},{5... | collective-permute-start | bytes 491528 | tf_op jit(solution)/shard_map/ppermute | solution.py:344
  3.2 5.7 %collective-permute-start.1 = (f32[160,128]{1,0:T(8,128)S(1)}, f32[160,128]{1,0:T(8,128)S(1)}, u32[]{:S(2)}, u32[]{:S(2)}) collective-permute-start(f32[160,128]{1,0:T(8,128)S(1)} %get-tuple-element.22), channel_id=1, source_target_pairs={{0,8},{4,12},{8,0},{12,4},{16,24},{20,28},{24,16},{28,20},{1,9},{5... | collective-permute-start | bytes 245768 | tf_op jit(solution)/shard_map/ppermute | solution.py:344
  6.1 15.2 %collective-permute-start.7 = (f32[640,128]{1,0:T(8,128)S(1)}, f32[640,128]{1,0:T(8,128)S(1)}, u32[]{:S(2)}, u32[]{:S(2)}) collective-permute-start(f32[640,128]{1,0:T(8,128)S(1)} %get-tuple-element.25.response), channel_id=1, source_target_pairs={{4,0},{8,4},{12,8},{16,12},{20,16},{24,20},{28,24},{0,28},{5,1},{9... | collective-permute-start | bytes 983048 | tf_op jit(solution)/shard_map/ppermute | solution.py:410
  8.8 6.4 %copy-start.1 = (bf16[256,256]{1,0:T(8,128)(2,1)S(1)}, bf16[256,256]{1,0:T(8,128)(2,1)}, u32[]{:S(2)}) copy-start(bf16[256,256]{1,0:T(8,128)(2,1)} %constant.14.clone.refs_0_) | copy-start | bytes 393220
  8.9 6.4 %copy-start.2 = (bf16[256,256]{1,0:T(8,128)(2,1)S(1)}, bf16[256,256]{1,0:T(8,128)(2,1)}, u32[]{:S(2)}) copy-start(bf16[256,256]{1,0:T(8,128)(2,1)} %constant.15.clone.refs_1_) | copy-start | bytes 393220
  8.9 6.4 %copy-start.3 = (bf16[48,144]{1,0:T(8,128)(2,1)S(1)}, bf16[48,144]{1,0:T(8,128)(2,1)}, u32[]{:S(2)}) copy-start(bf16[48,144]{1,0:T(8,128)(2,1)} %constant.16.clone.refs_2_) | copy-start | bytes 41476
  8.9 6.4 %copy-start.4 = (bf16[48,144]{1,0:T(8,128)(2,1)S(1)}, bf16[48,144]{1,0:T(8,128)(2,1)}, u32[]{:S(2)}) copy-start(bf16[48,144]{1,0:T(8,128)(2,1)} %constant.17.clone.refs_3_) | copy-start | bytes 41476
  8.9 6.4 %copy-start.5 = (bf16[32,96]{1,0:T(8,128)(2,1)S(1)}, bf16[32,96]{1,0:T(8,128)(2,1)}, u32[]{:S(2)}) copy-start(bf16[32,96]{1,0:T(8,128)(2,1)} %constant.18.clone.refs_4_) | copy-start | bytes 18436
  8.9 6.4 %copy-start.6 = (bf16[32,96]{1,0:T(8,128)(2,1)S(1)}, bf16[32,96]{1,0:T(8,128)(2,1)}, u32[]{:S(2)}) copy-start(bf16[32,96]{1,0:T(8,128)(2,1)} %constant.19.clone.refs_5_) | copy-start | bytes 18436
  8.9 4.5 %collective-permute-start.2 = (f32[160,128]{1,0:T(8,128)S(1)}, f32[160,128]{1,0:T(8,128)S(1)}, u32[]{:S(2)}, u32[]{:S(2)}) collective-permute-start(f32[160,128]{1,0:T(8,128)S(1)} %shard_map.121.mine), channel_id=1, source_target_pairs={{0,16},{4,20},{8,24},{12,28},{16,0},{20,4},{24,8},{28,12},{1,17},{... | collective-permute-start | bytes 245768 | tf_op jit(solution)/shard_map/ppermute | solution.py:344
  13.4 4.5 %collective-permute-start.3 = (f32[160,128]{1,0:T(8,128)S(1)}, f32[160,128]{1,0:T(8,128)S(1)}, u32[]{:S(2)}, u32[]{:S(2)}) collective-permute-start(f32[160,128]{1,0:T(8,128)S(1)} %shard_map.122.mine), channel_id=1, source_target_pairs={{0,1},{1,0},{2,3},{3,2},{4,5},{5,4},{6,7},{7,6},{8,9},{9,8},{10,11... | collective-permute-start | bytes 245768 | tf_op jit(solution)/shard_map/ppermute | solution.py:344
  18.0 5.8 %collective-permute-start.4 = (f32[160,128]{1,0:T(8,128)S(1)}, f32[160,128]{1,0:T(8,128)S(1)}, u32[]{:S(2)}, u32[]{:S(2)}) collective-permute-start(f32[160,128]{1,0:T(8,128)S(1)} %shard_map.123.mine), channel_id=1, source_target_pairs={{0,2},{1,3},{2,0},{3,1},{4,6},{5,7},{6,4},{7,5},{8,10},{9,11},{10,... | collective-permute-start | bytes 245768 | tf_op jit(solution)/shard_map/ppermute | solution.py:344
  23.8 5.9 %collective-permute-start.5 = (f32[160,128]{1,0:T(8,128)S(1)}, f32[160,128]{1,0:T(8,128)S(1)}, u32[]{:S(2)}, u32[]{:S(2)}) collective-permute-start(f32[160,128]{1,0:T(8,128)S(1)} %shard_map.124.mine), channel_id=1, source_target_pairs={{0,8},{4,12},{8,0},{12,4},{16,24},{20,28},{24,16},{28,20},{1,9},{5... | collective-permute-start | bytes 245768 | tf_op jit(solution)/shard_map/ppermute | solution.py:344
  29.7 7.5 %collective-permute-start.8 = (f32[640,128]{1,0:T(8,128)S(1)}, f32[640,128]{1,0:T(8,128)S(1)}, u32[]{:S(2)}, u32[]{:S(2)}) collective-permute-start(f32[640,128]{1,0:T(8,128)S(1)} %shard_map.130), channel_id=1, source_target_pairs={{0,4},{4,8},{8,12},{12,16},{16,20},{20,24},{24,28},{28,0},{1,5},{5... | collective-permute-start | bytes 983048 | tf_op jit(solution)/shard_map/ppermute | solution.py:420
  29.8 7.3 %collective-permute-start.6 = (f32[320,128]{1,0:T(8,128)S(1)}, f32[320,128]{1,0:T(8,128)S(1)}, u32[]{:S(2)}, u32[]{:S(2)}) collective-permute-start(f32[320,128]{1,0:T(8,128)S(1)} %shard_map.125.mine), channel_id=1, source_target_pairs={{0,4},{4,0},{8,12},{12,8},{16,20},{20,16},{24,28},{28,24},{1,5},{5... | collective-permute-start | bytes 491528 | tf_op jit(solution)/shard_map/ppermute | solution.py:344

commit v6 on v5

--- a/solution.py
+++ b/solution.py
@@ -324,11 +324,6 @@
     goes[...] = term[pl.ds(pl.multiple_of((1 - bit) * half, half), half), :]
 
 
-def share_kernel(distance, mine, other, stays, goes, term):
-    term[...] = mine[...] + other[...]
-    share(term, distance, stays, goes)
-
-
 def add_kernel(mine, other, out):
     out[...] = mine[...] + other[...]
 
@@ -339,29 +334,32 @@
     out[pl.ds(pl.multiple_of((1 - bit) * half, half), half), :] = other[...]
 
 
-def swap(values, axis, distance):
-    count = lax.axis_size(axis)
-    return lax.ppermute(values, axis, [(i, i ^ distance) for i in range(count)])
+def swap(values, partner):
+    orbs, grids = lax.axis_size("orb"), lax.axis_size("grid")
+    pairs = []
+    for orb in range(orbs):
+        for grid in range(grids):
+            axis, distance = partner(orb)
+            to = (orb ^ distance, grid) if axis == "orb" else (orb, grid ^ distance)
+            pairs.append((orb * grids + grid, to[0] * grids + to[1]))
+    return lax.ppermute(values, ("orb", "grid"), pairs)
+
+
+def added(mine, other):
+    return call(add_kernel, [VECTORS] * 2, [mine.shape], [], 0.1)(mine, other)[0]
 
 
 def summed_over_devices(stays, goes):
-    orb_bits = [("orb", 1 << bit) for bit in range(lax.axis_size("orb").bit_length() - 1)]
-    grid_bits = [("grid", 1 << bit) for bit in range(lax.axis_size("grid").bit_length() - 1)]
-    half = (stays.shape[0], LANES)
-    quarter = (stays.shape[0] // 2, LANES)
-    other = swap(goes, "orb", 1)
-    stays, goes = call(
-        functools.partial(share_kernel, 2), [VECTORS] * 2, [quarter] * 2, [pltpu.VMEM(half, F32)], 0.1
-    )(stays, other)
-    term, other = stays, swap(goes, "orb", 2)
-    rest = orb_bits[2:] + grid_bits
-    for axis, distance in rest:
-        term = call(add_kernel, [VECTORS] * 2, [quarter], [], 0.1)(term, other)[0]
-        other = swap(term, axis, distance)
-    term = call(add_kernel, [VECTORS] * 2, [quarter], [], 0.1)(term, other)[0]
-    other = swap(term, "orb", 2)
-    term = call(functools.partial(join_kernel, 2), [VECTORS] * 2, [half], [], 0.1)(term, other)[0]
-    return term, swap(term, "orb", 1)
+    steps = [("orb", 1 << bit) for bit in range(1, lax.axis_size("orb").bit_length() - 1)]
+    steps += [("grid", 1 << bit) for bit in range(lax.axis_size("grid").bit_length() - 1)]
+    turn = len(steps) // 2
+    orders = (steps, steps[turn:] + steps[:turn])
+    other = swap(goes, lambda orb: ("orb", 1))
+    term = added(stays, other)
+    for place in range(len(steps)):
+        other = swap(term, lambda orb: orders[orb % 2][place])
+        term = added(term, other)
+    return term, swap(term, lambda orb: ("orb", 1))
 
 
 def half_call(body, step, shapes, extra, values):

time: 38.3 us -> 36.8 us (0.961)
  starting transfers between devices: 14.8 us -> 10.5 us
  waiting for transfers between devices: 7.08 us -> 9.9 us
    ppermute x7 -> x6, starting transfers between devices: 13.8 us -> 6.89 us  [swap(): return lax.ppermute(values, ('orb', 'grid'), pairs)]
    ppermute x7 -> x6, waiting for transfers between devices: 3.7 us -> 9.06 us  [swap(): return lax.ppermute(values, ('orb', 'grid'), pairs)]
    ppermute x1, starting transfers between devices: 0.96 us -> 3.54 us  [per_device(): lax.ppermute(kept, 'orb', [((i + 1) % count, i) for i in range(count)])]
    ppermute x1, waiting for transfers between devices: 3.38 us -> 0.84 us  [per_device(): lax.ppermute(away, 'orb', [(i, (i + 1) % count) for i in range(count)])]
    pallas_call x14 -> x13, Pallas kernels: 15.9 us -> 15.9 us  [call(): kernel(*(placed(v, spec) for spec, v in zip(specs, values)))]
  transfers between devices with their start and end apart: 9 -> 8, of which waited for: 5 -> 5; matrix products, arithmetic and copies ran while one was open for 0% -> 0% of each run, Pallas kernels for 35% -> 37%
where the time goes in v6:
time: 36.8 us; the launch traced here: 36.5 us
  Pallas kernels  15.9 us (43%)
  starting transfers between devices  10.5 us (29%)
  waiting for transfers between devices  9.9 us (27%)
    pallas_call x13, Pallas kernels, call(): kernel(*(placed(v, spec) for spec, v in zip(specs, values)))  15.9 us
    ppermute x6, waiting for transfers between devices, swap(): return lax.ppermute(values, ('orb', 'grid'), pairs)  9.06 us
    ppermute x6, starting transfers between devices, swap(): return lax.ppermute(values, ('orb', 'grid'), pairs)  6.89 us
    ppermute x1, starting transfers between devices, per_device(): lax.ppermute(kept, 'orb', [((i + 1) % count, i) for i in range(count)])  3.54 us
    ppermute x1, waiting for transfers between devices, per_device(): lax.ppermute(away, 'orb', [(i, (i + 1) % count) for i in range(count)])  0.84 us
  transfers between devices with their start and end apart: 8, of which 5 were waited for; matrix products, arithmetic and copies ran while one was open for 0% of the time, Pallas kernels for 37%

profile of v6, /device:TPU:0, one launch (start us, length us, event | category | flops | bytes accessed | tf_op | source)
XLA Modules:
  0.0 36.5 jit_solution(12336545372206904766)
XLA Ops:
  0.0 0.0 copy-start
  0.0 1.5 %shard_map.118 = (f32[320,128]{1,0:T(8,128)S(1)}, f32[320,128]{1,0:T(8,128)S(1)}, f32[640,128]{1,0:T(8,128)S(1)}, f32[640,128]{1,0:T(8,128)S(1)}, f32[8,128]{1,0:T(8,128)S(1)}) custom-call(s32[4]{0:T(128)} %signs.1, s32[1,2]{1,0:T(1,128)} %offsets.1, f32[4,81000]{1,0:T(4,128)} %ground.3, f32[1,81000]{1,0:T(1,128)} %response.1), custom_call_target="tpu_custom_call" | custom-call | flops 1000000000 | bytes 1000000 | tf_op jit(solution)/shard_map/pallas_call | solution.py:314
  1.6 0.6 %collective-permute-start = (f32[320,128]{1,0:T(8,128)S(1)}, f32[320,128]{1,0:T(8,128)S(1)}, u32[]{:S(2)}, u32[]{:S(2)}) collective-permute-start(f32[320,128]{1,0:T(8,128)S(1)} %get-tuple-element.18), channel_id=1, source_target_pairs={{0,4},{1,5},{2,6},{3,7},{4,0},{5,1},{6,2},{7,3},{8,12},{9,13},{10,... | collective-permute-start | bytes 491528 | tf_op jit(solution)/shard_map/ppermute | solution.py:345
  2.1 3.5 %collective-permute-start.6 = (f32[640,128]{1,0:T(8,128)S(1)}, f32[640,128]{1,0:T(8,128)S(1)}, u32[]{:S(2)}, u32[]{:S(2)}) collective-permute-start(f32[640,128]{1,0:T(8,128)S(1)} %get-tuple-element.21.response), channel_id=1, source_target_pairs={{4,0},{8,4},{12,8},{16,12},{20,16},{24,20},{28,24},{0,28},{5,1},{9... | collective-permute-start | bytes 983048 | tf_op jit(solution)/shard_map/ppermute | solution.py:408
  5.7 0.0 collective-permute-done.other
  5.7 0.0 copy-start.1
  5.7 0.0 copy-start.2
  5.7 0.0 copy-start.3
  5.7 0.0 copy-start.4
  5.7 0.0 copy-start.5
  5.7 0.0 copy-start.6
  5.8 0.4 %collective-permute-start.1 = (f32[320,128]{1,0:T(8,128)S(1)}, f32[320,128]{1,0:T(8,128)S(1)}, u32[]{:S(2)}, u32[]{:S(2)}) collective-permute-start(f32[320,128]{1,0:T(8,128)S(1)} %shard_map.120.mine), channel_id=1, source_target_pairs={{0,8},{1,9},{2,10},{3,11},{4,5},{5,4},{6,7},{7,6},{8,0},{9,1},{10,... | collective-permute-start | bytes 491528 | tf_op jit(solution)/shard_map/ppermute | solution.py:345
  6.1 0.0 copy-done
  6.1 1.9 %shard_map.125 = (f32[1376,128]{1,0:T(8,128)S(1)}, f32[1376,128]{1,0:T(8,128)S(1)}) custom-call(f32[4,81000]{1,0:T(4,128)S(1)} %copy-done), custom_call_target="tpu_custom_call" | custom-call | flops 2000000000 | bytes 2000000 | tf_op jit(solution)/shard_map/pallas_call | solution.py:314
  8.1 3.9 %collective-permute-done.1.other = f32[320,128]{1,0:T(8,128)S(1)} collective-permute-done((f32[320,128]{1,0:T(8,128)S(1)}, f32[320,128]{1,0:T(8,128)S(1)}, u32[]{:S(2)}, u32[]{:S(2)}) %collective-permute-start.1) | collective-permute-done | bytes 163872 | tf_op jit(solution)/shard_map/ppermute | solution.py:345
  12.0 1.6 %collective-permute-start.2 = (f32[320,128]{1,0:T(8,128)S(1)}, f32[320,128]{1,0:T(8,128)S(1)}, u32[]{:S(2)}, u32[]{:S(2)}) collective-permute-start(f32[320,128]{1,0:T(8,128)S(1)} %shard_map.121.mine), channel_id=1, source_target_pairs={{0,16},{1,17},{2,18},{3,19},{4,6},{5,7},{6,4},{7,5},{8,24},{9,25},... | collective-permute-start | bytes 491528 | tf_op jit(solution)/shard_map/ppermute | solution.py:345
  13.6 0.0 copy-done.1
  13.6 0.0 copy-done.2
  13.7 0.0 copy-done.3
  13.7 0.0 copy-done.4
  13.7 0.0 copy-done.5
  13.7 0.0 copy-done.6
  13.7 2.5 %shard_map.126 = (f32[1376,128]{1,0:T(8,128)S(1)}, f32[1376,128]{1,0:T(8,128)S(1)}) custom-call(f32[8,128]{1,0:T(8,128)S(1)} %get-tuple-element.19.weights, f32[1376,128]{1,0:T(8,128)S(1)} %get-tuple-element.22.lines, f32[640,128]{1,0:T(8,128)S(1)} %get-tuple-element.21.response, bf16[256,256]{1,0:T(8,128)(2,1)S(1)} %copy-done.1, ...), custom_call_target="tpu_custom_call" | custom-call | flops 3000000000 | bytes 3000000 | tf_op jit(solution)/shard_map/pallas_call | solution.py:314
  16.2 1.2 %collective-permute-done.2.other = f32[320,128]{1,0:T(8,128)S(1)} collective-permute-done((f32[320,128]{1,0:T(8,128)S(1)}, f32[320,128]{1,0:T(8,128)S(1)}, u32[]{:S(2)}, u32[]{:S(2)}) %collective-permute-start.2) | collective-permute-done | bytes 163872 | tf_op jit(solution)/shard_map/ppermute | solution.py:345
  17.4 1.6 %collective-permute-start.3 = (f32[320,128]{1,0:T(8,128)S(1)}, f32[320,128]{1,0:T(8,128)S(1)}, u32[]{:S(2)}, u32[]{:S(2)}) collective-permute-start(f32[320,128]{1,0:T(8,128)S(1)} %shard_map.122.mine), channel_id=1, source_target_pairs={{0,1},{1,0},{2,3},{3,2},{4,12},{5,13},{6,14},{7,15},{8,9},{9,8},{1... | collective-permute-start | bytes 491528 | tf_op jit(solution)/shard_map/ppermute | solution.py:345
  19.1 0.0 collective-permute-done.6.response
  19.1 2.5 %shard_map.128 = (f32[1376,128]{1,0:T(8,128)S(1)}, f32[1376,128]{1,0:T(8,128)S(1)}) custom-call(f32[8,128]{1,0:T(8,128)S(1)} %get-tuple-element.19.weights, f32[1376,128]{1,0:T(8,128)S(1)} %get-tuple-element.22.lines, f32[640,128]{1,0:T(8,128)S(1)} %collective-permute-done.6.response, bf16[256,256]{1,0:T(8,128)(2,1)S(1)} %copy-done.1, ...), custom_call_target="tpu_custom_call" | custom-call | flops 3000000000 | bytes 3000000 | tf_op jit(solution)/shard_map/pallas_call | solution.py:314
  21.6 1.2 %collective-permute-done.3.other = f32[320,128]{1,0:T(8,128)S(1)} collective-permute-done((f32[320,128]{1,0:T(8,128)S(1)}, f32[320,128]{1,0:T(8,128)S(1)}, u32[]{:S(2)}, u32[]{:S(2)}) %collective-permute-start.3) | collective-permute-done | bytes 163872 | tf_op jit(solution)/shard_map/ppermute | solution.py:345
  22.8 2.6 %collective-permute-start.4 = (f32[320,128]{1,0:T(8,128)S(1)}, f32[320,128]{1,0:T(8,128)S(1)}, u32[]{:S(2)}, u32[]{:S(2)}) collective-permute-start(f32[320,128]{1,0:T(8,128)S(1)} %shard_map.123.mine), channel_id=1, source_target_pairs={{0,2},{1,3},{2,0},{3,1},{4,20},{5,21},{6,22},{7,23},{8,10},{9,11},... | collective-permute-start | bytes 491528 | tf_op jit(solution)/shard_map/ppermute | solution.py:345
  25.5 2.7 %shard_map.129 = f32[640,128]{1,0:T(8,128)S(1)} custom-call(f32[8,128]{1,0:T(8,128)S(1)} %get-tuple-element.19.weights, f32[1376,128]{1,0:T(8,128)S(1)} %get-tuple-element.20.lines, f32[640,128]{1,0:T(8,128)S(1)} %collective-permute-done.6.response, bf16[256,256]{1,0:T(8,128)(2,1)S(1)} %copy-done.1, bf16[256,256]{1,0:T(8,128)(2,1)S(1)} %copy-done.2, ...), custom_call_target="tpu_custom_call" | custom-call | flops 3000000000 | bytes 3000000 | tf_op jit(solution)/shard_map/pallas_call | solution.py:314
  28.2 0.1 collective-permute-start.7
  28.2 2.7 %collective-permute-done.4.other = f32[320,128]{1,0:T(8,128)S(1)} collective-permute-done((f32[320,128]{1,0:T(8,128)S(1)}, f32[320,128]{1,0:T(8,128)S(1)}, u32[]{:S(2)}, u32[]{:S(2)}) %collective-permute-start.4) | collective-permute-done | bytes 163872 | tf_op jit(solution)/shard_map/ppermute | solution.py:345
  30.9 0.1 collective-permute-start.5
  31.0 2.7 %shard_map.127.first = f32[640,128]{1,0:T(8,128)S(1)} custom-call(f32[8,128]{1,0:T(8,128)S(1)} %get-tuple-element.19.weights, f32[1376,128]{1,0:T(8,128)S(1)} %get-tuple-element.20.lines, f32[640,128]{1,0:T(8,128)S(1)} %get-tuple-element.21.response, bf16[256,256]{1,0:T(8,128)(2,1)S(1)} %copy-done.1, bf16[256,256]{1,0:T(8,128)(2,1)S(1)} %copy-done.2, ...), custom_call_target="tpu_custom_call" | custom-call | flops 3000000000 | bytes 3000000 | tf_op jit(solution)/shard_map/pallas_call | solution.py:314
  33.7 1.1 %shard_map.119.coefficient = f32[640,128]{1,0:T(8,128)S(1)} custom-call(f32[81000]{0:T(1024)} %density.1, f32[640,128]{1,0:T(8,128)S(1)} %get-tuple-element.16.own), custom_call_target="tpu_custom_call" | custom-call | flops 1000000000 | bytes 1000000 | tf_op jit(solution)/shard_map/pallas_call | solution.py:314
  34.8 0.8 %collective-permute-done.7.second = f32[640,128]{1,0:T(8,128)S(1)} collective-permute-done((f32[640,128]{1,0:T(8,128)S(1)}, f32[640,128]{1,0:T(8,128)S(1)}, u32[]{:S(2)}, u32[]{:S(2)}) %collective-permute-start.7) | collective-permute-done | bytes 327712 | tf_op jit(solution)/shard_map/ppermute | solution.py:418
  35.6 0.0 collective-permute-done.5.other
  35.6 0.9 %shard_map.130 = f32[1,81000]{1,0:T(1,128)} custom-call(f32[640,128]{1,0:T(8,128)S(1)} %shard_map.119.coefficient, f32[320,128]{1,0:T(8,128)S(1)} %shard_map.124.mine, f32[320,128]{1,0:T(8,128)S(1)} %collective-permute-done.5.other, f32[640,128]{1,0:T(8,128)S(1)} %shard_map.127.first, f32[640,128]{1,0:T(8,128)S(1)} %collective-permute-done.7.second), custom_call_target="tpu_custom_call" | custom-call | flops 1000000000 | bytes 1000000 | tf_op jit(solution)/shard_map/pallas_call | solution.py:314
  (5 shorter events, 0.1 us)
Async XLA Ops:
  0.0 6.1 %copy-start = (f32[4,81000]{1,0:T(4,128)S(1)}, f32[4,81000]{1,0:T(4,128)}, u32[]{:S(2)}) copy-start(f32[4,81000]{1,0:T(4,128)} %ground.3) | copy-start | bytes 3888004
  1.6 4.1 %collective-permute-start = (f32[320,128]{1,0:T(8,128)S(1)}, f32[320,128]{1,0:T(8,128)S(1)}, u32[]{:S(2)}, u32[]{:S(2)}) collective-permute-start(f32[320,128]{1,0:T(8,128)S(1)} %get-tuple-element.18), channel_id=1, source_target_pairs={{0,4},{1,5},{2,6},{3,7},{4,0},{5,1},{6,2},{7,3},{8,12},{9,13},{10,... | collective-permute-start | bytes 491528 | tf_op jit(solution)/shard_map/ppermute | solution.py:345
  2.1 16.9 %collective-permute-start.6 = (f32[640,128]{1,0:T(8,128)S(1)}, f32[640,128]{1,0:T(8,128)S(1)}, u32[]{:S(2)}, u32[]{:S(2)}) collective-permute-start(f32[640,128]{1,0:T(8,128)S(1)} %get-tuple-element.21.response), channel_id=1, source_target_pairs={{4,0},{8,4},{12,8},{16,12},{20,16},{24,20},{28,24},{0,28},{5,1},{9... | collective-permute-start | bytes 983048 | tf_op jit(solution)/shard_map/ppermute | solution.py:408
  5.7 8.0 %copy-start.1 = (bf16[256,256]{1,0:T(8,128)(2,1)S(1)}, bf16[256,256]{1,0:T(8,128)(2,1)}, u32[]{:S(2)}) copy-start(bf16[256,256]{1,0:T(8,128)(2,1)} %constant.14.clone.refs_0_) | copy-start | bytes 393220
  5.7 8.0 %copy-start.2 = (bf16[256,256]{1,0:T(8,128)(2,1)S(1)}, bf16[256,256]{1,0:T(8,128)(2,1)}, u32[]{:S(2)}) copy-start(bf16[256,256]{1,0:T(8,128)(2,1)} %constant.15.clone.refs_1_) | copy-start | bytes 393220
  5.7 7.9 %copy-start.3 = (bf16[48,144]{1,0:T(8,128)(2,1)S(1)}, bf16[48,144]{1,0:T(8,128)(2,1)}, u32[]{:S(2)}) copy-start(bf16[48,144]{1,0:T(8,128)(2,1)} %constant.16.clone.refs_2_) | copy-start | bytes 41476
  5.7 7.9 %copy-start.4 = (bf16[48,144]{1,0:T(8,128)(2,1)S(1)}, bf16[48,144]{1,0:T(8,128)(2,1)}, u32[]{:S(2)}) copy-start(bf16[48,144]{1,0:T(8,128)(2,1)} %constant.17.clone.refs_3_) | copy-start | bytes 41476
  5.7 7.9 %copy-start.5 = (bf16[32,96]{1,0:T(8,128)(2,1)S(1)}, bf16[32,96]{1,0:T(8,128)(2,1)}, u32[]{:S(2)}) copy-start(bf16[32,96]{1,0:T(8,128)(2,1)} %constant.18.clone.refs_4_) | copy-start | bytes 18436
  5.7 7.9 %copy-start.6 = (bf16[32,96]{1,0:T(8,128)(2,1)S(1)}, bf16[32,96]{1,0:T(8,128)(2,1)}, u32[]{:S(2)}) copy-start(bf16[32,96]{1,0:T(8,128)(2,1)} %constant.19.clone.refs_5_) | copy-start | bytes 18436
  5.8 6.2 %collective-permute-start.1 = (f32[320,128]{1,0:T(8,128)S(1)}, f32[320,128]{1,0:T(8,128)S(1)}, u32[]{:S(2)}, u32[]{:S(2)}) collective-permute-start(f32[320,128]{1,0:T(8,128)S(1)} %shard_map.120.mine), channel_id=1, source_target_pairs={{0,8},{1,9},{2,10},{3,11},{4,5},{5,4},{6,7},{7,6},{8,0},{9,1},{10,... | collective-permute-start | bytes 491528 | tf_op jit(solution)/shard_map/ppermute | solution.py:345
  12.0 5.4 %collective-permute-start.2 = (f32[320,128]{1,0:T(8,128)S(1)}, f32[320,128]{1,0:T(8,128)S(1)}, u32[]{:S(2)}, u32[]{:S(2)}) collective-permute-start(f32[320,128]{1,0:T(8,128)S(1)} %shard_map.121.mine), channel_id=1, source_target_pairs={{0,16},{1,17},{2,18},{3,19},{4,6},{5,7},{6,4},{7,5},{8,24},{9,25},... | collective-permute-start | bytes 491528 | tf_op jit(solution)/shard_map/ppermute | solution.py:345
  17.4 5.4 %collective-permute-start.3 = (f32[320,128]{1,0:T(8,128)S(1)}, f32[320,128]{1,0:T(8,128)S(1)}, u32[]{:S(2)}, u32[]{:S(2)}) collective-permute-start(f32[320,128]{1,0:T(8,128)S(1)} %shard_map.122.mine), channel_id=1, source_target_pairs={{0,1},{1,0},{2,3},{3,2},{4,12},{5,13},{6,14},{7,15},{8,9},{9,8},{1... | collective-permute-start | bytes 491528 | tf_op jit(solution)/shard_map/ppermute | solution.py:345
  22.8 8.0 %collective-permute-start.4 = (f32[320,128]{1,0:T(8,128)S(1)}, f32[320,128]{1,0:T(8,128)S(1)}, u32[]{:S(2)}, u32[]{:S(2)}) collective-permute-start(f32[320,128]{1,0:T(8,128)S(1)} %shard_map.123.mine), channel_id=1, source_target_pairs={{0,2},{1,3},{2,0},{3,1},{4,20},{5,21},{6,22},{7,23},{8,10},{9,11},... | collective-permute-start | bytes 491528 | tf_op jit(solution)/shard_map/ppermute | solution.py:345
  28.2 7.5 %collective-permute-start.7 = (f32[640,128]{1,0:T(8,128)S(1)}, f32[640,128]{1,0:T(8,128)S(1)}, u32[]{:S(2)}, u32[]{:S(2)}) collective-permute-start(f32[640,128]{1,0:T(8,128)S(1)} %shard_map.129), channel_id=1, source_target_pairs={{0,4},{4,8},{8,12},{12,16},{16,20},{20,24},{24,28},{28,0},{1,5},{5... | collective-permute-start | bytes 983048 | tf_op jit(solution)/shard_map/ppermute | solution.py:418
  30.9 4.7 %collective-permute-start.5 = (f32[320,128]{1,0:T(8,128)S(1)}, f32[320,128]{1,0:T(8,128)S(1)}, u32[]{:S(2)}, u32[]{:S(2)}) collective-permute-start(f32[320,128]{1,0:T(8,128)S(1)} %shard_map.124.mine), channel_id=1, source_target_pairs={{0,4},{1,5},{2,6},{3,7},{4,0},{5,1},{6,2},{7,3},{8,12},{9,13},{10,... | collective-permute-start | bytes 491528 | tf_op jit(solution)/shard_map/ppermute | solution.py:345

commit v7 on v6

--- a/solution.py
+++ b/solution.py
@@ -31,7 +31,9 @@
 CHUNKS = math.lcm(NZ, LANES) // LANES
 PERIODS = -(-NX * NY // LINES)
 LINE_ROWS = PERIODS * LINES
-FLAT_ROWS = PERIODS * CHUNKS
+GROUPED = -(-PERIODS // 8) * 8
+FLAT_ROWS = GROUPED * CHUNKS
+PITCHED_ROWS = GROUPED * (LINES + 1)
 WHOLE = POINTS // LANES
 TAIL = POINTS - WHOLE * LANES
 SENT_ROWS = 640
@@ -363,7 +365,7 @@
 
 
 def half_call(body, step, shapes, extra, values):
-    flat, pitched = pltpu.VMEM((FLAT_ROWS, LANES), F32), pltpu.VMEM((PERIODS * (LINES + 1), LANES), F32)
+    flat, pitched = pltpu.VMEM((FLAT_ROWS, LANES), F32), pltpu.VMEM((PITCHED_ROWS, LANES), F32)
     scratch = [flat, pitched, pltpu.SemaphoreType.DMA, pltpu.VMEM((YP * XP, LANES), F32)]
     scratch += [pltpu.VMEM((YP * XS, LANES), F32), pltpu.VMEM((XP * YS, LANES), F32)] + extra
     specs = [VECTORS] * 9 + [FAR] + [VECTORS] * (len(values) - 10)
@@ -382,7 +384,7 @@
 def lines_call(ground):
     return call(
         lines_kernel, [VECTORS], [(LINE_ROWS, LANES)] * 2,
-        [pltpu.VMEM((4, FLAT_ROWS, LANES), F32), pltpu.VMEM((PERIODS * (LINES + 1), LANES), F32),
+        [pltpu.VMEM((4, FLAT_ROWS, LANES), F32), pltpu.VMEM((PITCHED_ROWS, LANES), F32),
          pltpu.SemaphoreType.DMA((4,))], 2,
     )(ground)
 

time: 36.8 us -> 36.8 us (level)
  no operation moved by 1% of the time
where the time goes in v7:
time: 36.8 us; the launch traced here: 36.5 us
  Pallas kernels  15.9 us (43%)
  starting transfers between devices  10.5 us (29%)
  waiting for transfers between devices  9.91 us (27%)
    pallas_call x13, Pallas kernels, call(): kernel(*(placed(v, spec) for spec, v in zip(specs, values)))  15.9 us
    ppermute x6, waiting for transfers between devices, swap(): return lax.ppermute(values, ('orb', 'grid'), pairs)  9.06 us
    ppermute x6, starting transfers between devices, swap(): return lax.ppermute(values, ('orb', 'grid'), pairs)  6.89 us
    ppermute x1, starting transfers between devices, per_device(): lax.ppermute(kept, 'orb', [((i + 1) % count, i) for i in range(count)])  3.54 us
    ppermute x1, waiting for transfers between devices, per_device(): lax.ppermute(away, 'orb', [(i, (i + 1) % count) for i in range(count)])  0.85 us
  transfers between devices with their start and end apart: 8, of which 5 were waited for; matrix products, arithmetic and copies ran while one was open for 0% of the time, Pallas kernels for 37%

profile of v7, /device:TPU:0, one launch (start us, length us, event | category | flops | bytes accessed | tf_op | source)
XLA Modules:
  0.0 36.5 jit_solution(7161568422352140491)
XLA Ops:
  0.0 0.0 copy-start
  0.0 1.5 %shard_map.118 = (f32[320,128]{1,0:T(8,128)S(1)}, f32[320,128]{1,0:T(8,128)S(1)}, f32[640,128]{1,0:T(8,128)S(1)}, f32[640,128]{1,0:T(8,128)S(1)}, f32[8,128]{1,0:T(8,128)S(1)}) custom-call(s32[4]{0:T(128)} %signs.1, s32[1,2]{1,0:T(1,128)} %offsets.1, f32[4,81000]{1,0:T(4,128)} %ground.3, f32[1,81000]{1,0:T(1,128)} %response.1), custom_call_target="tpu_custom_call" | custom-call | flops 1000000000 | bytes 1000000 | tf_op jit(solution)/shard_map/pallas_call | solution.py:316
  1.6 0.6 %collective-permute-start = (f32[320,128]{1,0:T(8,128)S(1)}, f32[320,128]{1,0:T(8,128)S(1)}, u32[]{:S(2)}, u32[]{:S(2)}) collective-permute-start(f32[320,128]{1,0:T(8,128)S(1)} %get-tuple-element.18), channel_id=1, source_target_pairs={{0,4},{1,5},{2,6},{3,7},{4,0},{5,1},{6,2},{7,3},{8,12},{9,13},{10,... | collective-permute-start | bytes 491528 | tf_op jit(solution)/shard_map/ppermute | solution.py:347
  2.1 3.5 %collective-permute-start.6 = (f32[640,128]{1,0:T(8,128)S(1)}, f32[640,128]{1,0:T(8,128)S(1)}, u32[]{:S(2)}, u32[]{:S(2)}) collective-permute-start(f32[640,128]{1,0:T(8,128)S(1)} %get-tuple-element.21.response), channel_id=1, source_target_pairs={{4,0},{8,4},{12,8},{16,12},{20,16},{24,20},{28,24},{0,28},{5,1},{9... | collective-permute-start | bytes 983048 | tf_op jit(solution)/shard_map/ppermute | solution.py:410
  5.7 0.0 collective-permute-done.other
  5.7 0.0 copy-start.1
  5.7 0.0 copy-start.2
  5.7 0.0 copy-start.3
  5.7 0.0 copy-start.4
  5.7 0.0 copy-start.5
  5.7 0.0 copy-start.6
  5.8 0.4 %collective-permute-start.1 = (f32[320,128]{1,0:T(8,128)S(1)}, f32[320,128]{1,0:T(8,128)S(1)}, u32[]{:S(2)}, u32[]{:S(2)}) collective-permute-start(f32[320,128]{1,0:T(8,128)S(1)} %shard_map.120.mine), channel_id=1, source_target_pairs={{0,8},{1,9},{2,10},{3,11},{4,5},{5,4},{6,7},{7,6},{8,0},{9,1},{10,... | collective-permute-start | bytes 491528 | tf_op jit(solution)/shard_map/ppermute | solution.py:347
  6.1 0.0 copy-done
  6.1 1.9 %shard_map.125 = (f32[1376,128]{1,0:T(8,128)S(1)}, f32[1376,128]{1,0:T(8,128)S(1)}) custom-call(f32[4,81000]{1,0:T(4,128)S(1)} %copy-done), custom_call_target="tpu_custom_call" | custom-call | flops 2000000000 | bytes 2000000 | tf_op jit(solution)/shard_map/pallas_call | solution.py:316
  8.1 4.0 %collective-permute-done.1.other = f32[320,128]{1,0:T(8,128)S(1)} collective-permute-done((f32[320,128]{1,0:T(8,128)S(1)}, f32[320,128]{1,0:T(8,128)S(1)}, u32[]{:S(2)}, u32[]{:S(2)}) %collective-permute-start.1) | collective-permute-done | bytes 163872 | tf_op jit(solution)/shard_map/ppermute | solution.py:347
  12.0 1.6 %collective-permute-start.2 = (f32[320,128]{1,0:T(8,128)S(1)}, f32[320,128]{1,0:T(8,128)S(1)}, u32[]{:S(2)}, u32[]{:S(2)}) collective-permute-start(f32[320,128]{1,0:T(8,128)S(1)} %shard_map.121.mine), channel_id=1, source_target_pairs={{0,16},{1,17},{2,18},{3,19},{4,6},{5,7},{6,4},{7,5},{8,24},{9,25},... | collective-permute-start | bytes 491528 | tf_op jit(solution)/shard_map/ppermute | solution.py:347
  13.6 0.0 copy-done.1
  13.6 0.0 copy-done.2
  13.7 0.0 copy-done.3
  13.7 0.0 copy-done.4
  13.7 0.0 copy-done.5
  13.7 0.0 copy-done.6
  13.7 2.5 %shard_map.126 = (f32[1376,128]{1,0:T(8,128)S(1)}, f32[1376,128]{1,0:T(8,128)S(1)}) custom-call(f32[8,128]{1,0:T(8,128)S(1)} %get-tuple-element.19.weights, f32[1376,128]{1,0:T(8,128)S(1)} %get-tuple-element.22.lines, f32[640,128]{1,0:T(8,128)S(1)} %get-tuple-element.21.response, bf16[256,256]{1,0:T(8,128)(2,1)S(1)} %copy-done.1, ...), custom_call_target="tpu_custom_call" | custom-call | flops 3000000000 | bytes 3000000 | tf_op jit(solution)/shard_map/pallas_call | solution.py:316
  16.2 1.2 %collective-permute-done.2.other = f32[320,128]{1,0:T(8,128)S(1)} collective-permute-done((f32[320,128]{1,0:T(8,128)S(1)}, f32[320,128]{1,0:T(8,128)S(1)}, u32[]{:S(2)}, u32[]{:S(2)}) %collective-permute-start.2) | collective-permute-done | bytes 163872 | tf_op jit(solution)/shard_map/ppermute | solution.py:347
  17.4 1.6 %collective-permute-start.3 = (f32[320,128]{1,0:T(8,128)S(1)}, f32[320,128]{1,0:T(8,128)S(1)}, u32[]{:S(2)}, u32[]{:S(2)}) collective-permute-start(f32[320,128]{1,0:T(8,128)S(1)} %shard_map.122.mine), channel_id=1, source_target_pairs={{0,1},{1,0},{2,3},{3,2},{4,12},{5,13},{6,14},{7,15},{8,9},{9,8},{1... | collective-permute-start | bytes 491528 | tf_op jit(solution)/shard_map/ppermute | solution.py:347
  19.1 0.0 collective-permute-done.6.response
  19.1 2.5 %shard_map.128 = (f32[1376,128]{1,0:T(8,128)S(1)}, f32[1376,128]{1,0:T(8,128)S(1)}) custom-call(f32[8,128]{1,0:T(8,128)S(1)} %get-tuple-element.19.weights, f32[1376,128]{1,0:T(8,128)S(1)} %get-tuple-element.22.lines, f32[640,128]{1,0:T(8,128)S(1)} %collective-permute-done.6.response, bf16[256,256]{1,0:T(8,128)(2,1)S(1)} %copy-done.1, ...), custom_call_target="tpu_custom_call" | custom-call | flops 3000000000 | bytes 3000000 | tf_op jit(solution)/shard_map/pallas_call | solution.py:316
  21.6 1.2 %collective-permute-done.3.other = f32[320,128]{1,0:T(8,128)S(1)} collective-permute-done((f32[320,128]{1,0:T(8,128)S(1)}, f32[320,128]{1,0:T(8,128)S(1)}, u32[]{:S(2)}, u32[]{:S(2)}) %collective-permute-start.3) | collective-permute-done | bytes 163872 | tf_op jit(solution)/shard_map/ppermute | solution.py:347
  22.8 2.6 %collective-permute-start.4 = (f32[320,128]{1,0:T(8,128)S(1)}, f32[320,128]{1,0:T(8,128)S(1)}, u32[]{:S(2)}, u32[]{:S(2)}) collective-permute-start(f32[320,128]{1,0:T(8,128)S(1)} %shard_map.123.mine), channel_id=1, source_target_pairs={{0,2},{1,3},{2,0},{3,1},{4,20},{5,21},{6,22},{7,23},{8,10},{9,11},... | collective-permute-start | bytes 491528 | tf_op jit(solution)/shard_map/ppermute | solution.py:347
  25.5 2.7 %shard_map.129 = f32[640,128]{1,0:T(8,128)S(1)} custom-call(f32[8,128]{1,0:T(8,128)S(1)} %get-tuple-element.19.weights, f32[1376,128]{1,0:T(8,128)S(1)} %get-tuple-element.20.lines, f32[640,128]{1,0:T(8,128)S(1)} %collective-permute-done.6.response, bf16[256,256]{1,0:T(8,128)(2,1)S(1)} %copy-done.1, bf16[256,256]{1,0:T(8,128)(2,1)S(1)} %copy-done.2, ...), custom_call_target="tpu_custom_call" | custom-call | flops 3000000000 | bytes 3000000 | tf_op jit(solution)/shard_map/pallas_call | solution.py:316
  28.2 0.1 collective-permute-start.7
  28.2 2.7 %collective-permute-done.4.other = f32[320,128]{1,0:T(8,128)S(1)} collective-permute-done((f32[320,128]{1,0:T(8,128)S(1)}, f32[320,128]{1,0:T(8,128)S(1)}, u32[]{:S(2)}, u32[]{:S(2)}) %collective-permute-start.4) | collective-permute-done | bytes 163872 | tf_op jit(solution)/shard_map/ppermute | solution.py:347
  30.9 0.1 collective-permute-start.5
  31.0 2.7 %shard_map.127.first = f32[640,128]{1,0:T(8,128)S(1)} custom-call(f32[8,128]{1,0:T(8,128)S(1)} %get-tuple-element.19.weights, f32[1376,128]{1,0:T(8,128)S(1)} %get-tuple-element.20.lines, f32[640,128]{1,0:T(8,128)S(1)} %get-tuple-element.21.response, bf16[256,256]{1,0:T(8,128)(2,1)S(1)} %copy-done.1, bf16[256,256]{1,0:T(8,128)(2,1)S(1)} %copy-done.2, ...), custom_call_target="tpu_custom_call" | custom-call | flops 3000000000 | bytes 3000000 | tf_op jit(solution)/shard_map/pallas_call | solution.py:316
  33.7 1.1 %shard_map.119.coefficient = f32[640,128]{1,0:T(8,128)S(1)} custom-call(f32[81000]{0:T(1024)} %density.1, f32[640,128]{1,0:T(8,128)S(1)} %get-tuple-element.16.own), custom_call_target="tpu_custom_call" | custom-call | flops 1000000000 | bytes 1000000 | tf_op jit(solution)/shard_map/pallas_call | solution.py:316
  34.8 0.8 %collective-permute-done.7.second = f32[640,128]{1,0:T(8,128)S(1)} collective-permute-done((f32[640,128]{1,0:T(8,128)S(1)}, f32[640,128]{1,0:T(8,128)S(1)}, u32[]{:S(2)}, u32[]{:S(2)}) %collective-permute-start.7) | collective-permute-done | bytes 327712 | tf_op jit(solution)/shard_map/ppermute | solution.py:420
  35.6 0.0 collective-permute-done.5.other
  35.6 0.9 %shard_map.130 = f32[1,81000]{1,0:T(1,128)} custom-call(f32[640,128]{1,0:T(8,128)S(1)} %shard_map.119.coefficient, f32[320,128]{1,0:T(8,128)S(1)} %shard_map.124.mine, f32[320,128]{1,0:T(8,128)S(1)} %collective-permute-done.5.other, f32[640,128]{1,0:T(8,128)S(1)} %shard_map.127.first, f32[640,128]{1,0:T(8,128)S(1)} %collective-permute-done.7.second), custom_call_target="tpu_custom_call" | custom-call | flops 1000000000 | bytes 1000000 | tf_op jit(solution)/shard_map/pallas_call | solution.py:316
  (5 shorter events, 0.1 us)
Async XLA Ops:
  0.0 6.1 %copy-start = (f32[4,81000]{1,0:T(4,128)S(1)}, f32[4,81000]{1,0:T(4,128)}, u32[]{:S(2)}) copy-start(f32[4,81000]{1,0:T(4,128)} %ground.3) | copy-start | bytes 3888004
  1.6 4.1 %collective-permute-start = (f32[320,128]{1,0:T(8,128)S(1)}, f32[320,128]{1,0:T(8,128)S(1)}, u32[]{:S(2)}, u32[]{:S(2)}) collective-permute-start(f32[320,128]{1,0:T(8,128)S(1)} %get-tuple-element.18), channel_id=1, source_target_pairs={{0,4},{1,5},{2,6},{3,7},{4,0},{5,1},{6,2},{7,3},{8,12},{9,13},{10,... | collective-permute-start | bytes 491528 | tf_op jit(solution)/shard_map/ppermute | solution.py:347
  2.1 16.9 %collective-permute-start.6 = (f32[640,128]{1,0:T(8,128)S(1)}, f32[640,128]{1,0:T(8,128)S(1)}, u32[]{:S(2)}, u32[]{:S(2)}) collective-permute-start(f32[640,128]{1,0:T(8,128)S(1)} %get-tuple-element.21.response), channel_id=1, source_target_pairs={{4,0},{8,4},{12,8},{16,12},{20,16},{24,20},{28,24},{0,28},{5,1},{9... | collective-permute-start | bytes 983048 | tf_op jit(solution)/shard_map/ppermute | solution.py:410
  5.7 8.0 %copy-start.1 = (bf16[256,256]{1,0:T(8,128)(2,1)S(1)}, bf16[256,256]{1,0:T(8,128)(2,1)}, u32[]{:S(2)}) copy-start(bf16[256,256]{1,0:T(8,128)(2,1)} %constant.14.clone.refs_0_) | copy-start | bytes 393220
  5.7 8.0 %copy-start.2 = (bf16[256,256]{1,0:T(8,128)(2,1)S(1)}, bf16[256,256]{1,0:T(8,128)(2,1)}, u32[]{:S(2)}) copy-start(bf16[256,256]{1,0:T(8,128)(2,1)} %constant.15.clone.refs_1_) | copy-start | bytes 393220
  5.7 7.9 %copy-start.3 = (bf16[48,144]{1,0:T(8,128)(2,1)S(1)}, bf16[48,144]{1,0:T(8,128)(2,1)}, u32[]{:S(2)}) copy-start(bf16[48,144]{1,0:T(8,128)(2,1)} %constant.16.clone.refs_2_) | copy-start | bytes 41476
  5.7 7.9 %copy-start.4 = (bf16[48,144]{1,0:T(8,128)(2,1)S(1)}, bf16[48,144]{1,0:T(8,128)(2,1)}, u32[]{:S(2)}) copy-start(bf16[48,144]{1,0:T(8,128)(2,1)} %constant.17.clone.refs_3_) | copy-start | bytes 41476
  5.7 7.9 %copy-start.5 = (bf16[32,96]{1,0:T(8,128)(2,1)S(1)}, bf16[32,96]{1,0:T(8,128)(2,1)}, u32[]{:S(2)}) copy-start(bf16[32,96]{1,0:T(8,128)(2,1)} %constant.18.clone.refs_4_) | copy-start | bytes 18436
  5.7 7.9 %copy-start.6 = (bf16[32,96]{1,0:T(8,128)(2,1)S(1)}, bf16[32,96]{1,0:T(8,128)(2,1)}, u32[]{:S(2)}) copy-start(bf16[32,96]{1,0:T(8,128)(2,1)} %constant.19.clone.refs_5_) | copy-start | bytes 18436
  5.8 6.2 %collective-permute-start.1 = (f32[320,128]{1,0:T(8,128)S(1)}, f32[320,128]{1,0:T(8,128)S(1)}, u32[]{:S(2)}, u32[]{:S(2)}) collective-permute-start(f32[320,128]{1,0:T(8,128)S(1)} %shard_map.120.mine), channel_id=1, source_target_pairs={{0,8},{1,9},{2,10},{3,11},{4,5},{5,4},{6,7},{7,6},{8,0},{9,1},{10,... | collective-permute-start | bytes 491528 | tf_op jit(solution)/shard_map/ppermute | solution.py:347
  12.0 5.4 %collective-permute-start.2 = (f32[320,128]{1,0:T(8,128)S(1)}, f32[320,128]{1,0:T(8,128)S(1)}, u32[]{:S(2)}, u32[]{:S(2)}) collective-permute-start(f32[320,128]{1,0:T(8,128)S(1)} %shard_map.121.mine), channel_id=1, source_target_pairs={{0,16},{1,17},{2,18},{3,19},{4,6},{5,7},{6,4},{7,5},{8,24},{9,25},... | collective-permute-start | bytes 491528 | tf_op jit(solution)/shard_map/ppermute | solution.py:347
  17.4 5.4 %collective-permute-start.3 = (f32[320,128]{1,0:T(8,128)S(1)}, f32[320,128]{1,0:T(8,128)S(1)}, u32[]{:S(2)}, u32[]{:S(2)}) collective-permute-start(f32[320,128]{1,0:T(8,128)S(1)} %shard_map.122.mine), channel_id=1, source_target_pairs={{0,1},{1,0},{2,3},{3,2},{4,12},{5,13},{6,14},{7,15},{8,9},{9,8},{1... | collective-permute-start | bytes 491528 | tf_op jit(solution)/shard_map/ppermute | solution.py:347
  22.8 8.0 %collective-permute-start.4 = (f32[320,128]{1,0:T(8,128)S(1)}, f32[320,128]{1,0:T(8,128)S(1)}, u32[]{:S(2)}, u32[]{:S(2)}) collective-permute-start(f32[320,128]{1,0:T(8,128)S(1)} %shard_map.123.mine), channel_id=1, source_target_pairs={{0,2},{1,3},{2,0},{3,1},{4,20},{5,21},{6,22},{7,23},{8,10},{9,11},... | collective-permute-start | bytes 491528 | tf_op jit(solution)/shard_map/ppermute | solution.py:347
  28.2 7.5 %collective-permute-start.7 = (f32[640,128]{1,0:T(8,128)S(1)}, f32[640,128]{1,0:T(8,128)S(1)}, u32[]{:S(2)}, u32[]{:S(2)}) collective-permute-start(f32[640,128]{1,0:T(8,128)S(1)} %shard_map.129), channel_id=1, source_target_pairs={{0,4},{4,8},{8,12},{12,16},{16,20},{20,24},{24,28},{28,0},{1,5},{5... | collective-permute-start | bytes 983048 | tf_op jit(solution)/shard_map/ppermute | solution.py:420
  30.9 4.7 %collective-permute-start.5 = (f32[320,128]{1,0:T(8,128)S(1)}, f32[320,128]{1,0:T(8,128)S(1)}, u32[]{:S(2)}, u32[]{:S(2)}) collective-permute-start(f32[320,128]{1,0:T(8,128)S(1)} %shard_map.124.mine), channel_id=1, source_target_pairs={{0,4},{1,5},{2,6},{3,7},{4,0},{5,1},{6,2},{7,3},{8,12},{9,13},{10,... | collective-permute-start | bytes 491528 | tf_op jit(solution)/shard_map/ppermute | solution.py:347
